TPU v7x, 32 devices: a whole 2x2x4 slice. The times are simulated.
32 devices in a mesh: tile: 16 (over z, y, x), dp: 2 (over core).
Axes of the slice: x: 2, y: 2, z: 4, core: 2. Of those that a mesh axis runs over, the one named last changes fastest.
Arguments:
- observations: bfloat16 [32768, 256], P(('dp', 'tile')), parts along dimension 0, may hold values from -6 to 6
- instrument: int32 [32768], P(('dp', 'tile')), parts along dimension 0, may hold values from 0 to 31
- route: int32 [32768, 1], P(('dp', 'tile')), parts along dimension 0, may hold values from 0 to 15; in each aligned block of 1024 rows (0 to 1023, 1024 to 2047, ...) at most 128 rows name the same one
- cell_index: int32 [32768], P(('dp', 'tile')), parts along dimension 0, may hold values from 0 to 255
- latent: bfloat16 [8192, 512], P(('dp', 'tile')), parts along dimension 0, may hold values from -6 to 6
- inst_table: bfloat16 [32, 256], replicated, may hold values from -4 to 4
- w_obs_kv: bfloat16 [256, 1024], replicated, may hold values from -0.375 to 0.375
- w_cross_q: bfloat16 [512, 512], replicated, may hold values from -0.25 to 0.25
- w_cross_out: bfloat16 [512, 512], replicated, may hold values from -0.25 to 0.25
- w_win_qkv: bfloat16 [512, 1536], replicated, may hold values from -0.25 to 0.25
- w_win_out: bfloat16 [512, 512], replicated, may hold values from -0.25 to 0.25
- w_up: bfloat16 [512, 2048], replicated, may hold values from -0.25 to 0.25
- w_down: bfloat16 [2048, 512], replicated, may hold values from -0.125 to 0.125
- cotangent: bfloat16 [8192, 512], P(('dp', 'tile')), parts along dimension 0, may hold values from -6 to 6
Outputs:
- latent_out: bfloat16 [8192, 512], P(('dp', 'tile')), parts along dimension 0
- grad_down: float32 [4096, 512], P('dp'), parts along dimension 0
There are 2 independent parts, one for each index of `dp`. A program takes and returns all parts, laid end to end along the dimension named above; an argument that names none is the same for every part. Nothing has to cross between parts.
Inputs may be any that keep to these rules, and one draw needn't show every extreme that they name: `route`: among the 1024 observations of one index of tile, at most 128 name the same tile, and this bound is met; every tile is named by some observation.
All inputs are finite; a program needn't handle non-finite values.
Results may differ from a plain program's by a relative error of at most 0.0072.
Values may be sent and summed in bfloat16 or wider, within the bound.
No kernel may reach another device: no remote copies, remote signals or barrier semaphores. Data moves between devices by JAX's collectives and lax.ppermute only.
A program may use at most 128 MiB of HBM per device.

v0:
```python
import jax
import jax.numpy as jnp
from jax import lax
from jax.sharding import PartitionSpec as P

H = 8


def with_halo(block, sides, width):
    for axis, dim in sides:
        count = lax.axis_size(axis)
        forward = [(i, i + 1) for i in range(count - 1)]
        forward.append((count - 1, 0))
        backward = [(target, source) for source, target in forward]
        low = lax.ppermute(
            lax.slice_in_dim(block, block.shape[dim] - width, None, axis=dim), axis, forward
        )
        high = lax.ppermute(lax.slice_in_dim(block, 0, width, axis=dim), axis, backward)
        block = jnp.concatenate([low, block, high], axis=dim)
    return block


def rms_norm(values):
    return values * lax.rsqrt(jnp.mean(values * values, axis=-1, keepdims=True) + 1e-06)


def attend(query, keys, values, bias, allowed):
    head_size = query.shape[1] // H
    query_heads = query.reshape(query.shape[0], H, head_size)
    key_heads = keys.reshape(keys.shape[0], H, head_size)
    value_heads = values.reshape(values.shape[0], H, head_size)
    scores = (
        jnp.einsum("lhd,rhd->hlr", query_heads, key_heads, preferred_element_type=jnp.float32)
        * head_size ** (-0.5)
        + bias[None]
    )
    scores = jnp.where(allowed[None], scores, -1e30)
    row_peak = jnp.max(scores, axis=2, keepdims=True)
    expo = jnp.exp(scores - row_peak)
    row_total = jnp.sum(expo, axis=2, keepdims=True)
    weights = (expo / row_total).astype(jnp.bfloat16)
    mixed = jnp.einsum("hlr,rhd->lhd", weights, value_heads, preferred_element_type=jnp.float32)
    return mixed.astype(jnp.bfloat16).reshape(query.shape[0], query.shape[1])


def hidden_product(hidden_part, cotangent):
    return lax.dot_general(
        hidden_part, cotangent, (((0,), (0,)), ((), ())), preferred_element_type=jnp.float32
    )


def on_device(
    observations,
    instrument,
    route,
    cell_index,
    latent,
    inst_table,
    w_obs_kv,
    w_cross_q,
    w_cross_out,
    w_win_qkv,
    w_win_out,
    w_up,
    w_down,
    cotangent,
):
    devices = lax.axis_size("tile")
    obs_count = observations.shape[0]
    capacity = 2 * obs_count // devices
    width = latent.shape[1]
    cells = latent.shape[0]
    kinds = (instrument[:, None] == jnp.arange(inst_table.shape[0])[None, :]).astype(jnp.bfloat16)
    embedded = (
        observations.astype(jnp.float32)
        + jnp.dot(kinds, inst_table, preferred_element_type=jnp.float32)
    ).astype(jnp.bfloat16)
    target = route[:, 0]
    chosen = (target[:, None] == jnp.arange(devices)[None, :]).astype(jnp.int32)
    rank = jnp.sum(jnp.cumsum(chosen, axis=0) * chosen, axis=1) - 1
    slot = target * capacity + rank
    outgoing = (
        jnp.zeros((devices * capacity, observations.shape[1]), jnp.bfloat16).at[slot].set(embedded)
    )
    marker = (
        jnp.zeros((devices * capacity,), jnp.bfloat16)
        .at[slot]
        .set((cell_index + 1).astype(jnp.float32).astype(jnp.bfloat16))
    )
    arrived, arrived_mark = (
        lax.all_to_all(outgoing, "tile", split_axis=0, concat_axis=0, tiled=True),
        lax.all_to_all(marker, "tile", split_axis=0, concat_axis=0, tiled=True),
    )
    mark_value = arrived_mark.astype(jnp.float32)
    present = mark_value > 0.5
    obs_cell = mark_value - 1.0
    obs_kv = jnp.dot(arrived, w_obs_kv, preferred_element_type=jnp.float32).astype(jnp.bfloat16)
    latent_f = latent.astype(jnp.float32)
    query = jnp.dot(
        rms_norm(latent_f).astype(jnp.bfloat16), w_cross_q, preferred_element_type=jnp.float32
    ).astype(jnp.bfloat16)
    positions = jnp.arange(cells).astype(jnp.float32)
    distance_bias = -4.0 * jnp.abs(positions[:, None] - obs_cell[None, :]) / cells
    allowed = jnp.broadcast_to(present[None, :], (cells, present.shape[0]))
    cross = attend(query, obs_kv[:, :width], obs_kv[:, width:], distance_bias, allowed)
    stream = latent_f + jnp.dot(cross, w_cross_out, preferred_element_type=jnp.float32)
    projected = jnp.dot(
        rms_norm(stream).astype(jnp.bfloat16), w_win_qkv, preferred_element_type=jnp.float32
    ).astype(jnp.bfloat16)
    reach = cells // 2
    rimmed = with_halo(projected[:, width:], (("tile", 0),), reach)
    offsets = jnp.arange(cells + 2 * reach)[None, :] - jnp.arange(cells)[:, None]
    window_mask = (offsets >= 0) & (offsets <= 2 * reach)
    zero_bias = jnp.zeros((cells, cells + 2 * reach), jnp.float32)
    windowed = attend(
        projected[:, :width], rimmed[:, :width], rimmed[:, width:], zero_bias, window_mask
    )
    stream = stream + jnp.dot(windowed, w_win_out, preferred_element_type=jnp.float32)
    hidden = jax.nn.gelu(
        jnp.dot(rms_norm(stream).astype(jnp.bfloat16), w_up, preferred_element_type=jnp.float32)
    ).astype(jnp.bfloat16)
    latent_out = (stream + jnp.dot(hidden, w_down, preferred_element_type=jnp.float32)).astype(
        jnp.bfloat16
    )
    summed = lax.psum(hidden_product(hidden, cotangent), "tile")
    factor = jnp.minimum(1.0, 0.5 / jnp.sqrt(jnp.mean(summed * summed) + 1e-06))
    clipped = summed * factor
    return (latent_out, clipped)


def solution(mesh):
    return jax.shard_map(
        on_device,
        mesh=mesh,
        in_specs=(
            P(("dp", "tile"), None),
            P(("dp", "tile")),
            P(("dp", "tile"), None),
            P(("dp", "tile")),
            P(("dp", "tile"), None),
            P(),
            P(),
            P(),
            P(),
            P(),
            P(),
            P(),
            P(),
            P(("dp", "tile"), None),
        ),
        out_specs=(P(("dp", "tile"), None), P("dp", None)),
        check_vma=False,
    )
```

profile of v0, /device:TPU:0, one launch (start us, length us, event | category | flops | bytes accessed | tf_op | source)
XLA Modules:
  0.0 312.5 jit_solution(5338943887115091403)
XLA Ops:
  8.0 4.5 %reduce-window.6 = s32[16,8,128]{2,1,0:T(8,128)S(1)} reduce-window(s32[16,8,128]{2,1,0:T(8,128)S(1)} %fusion.42, s32[]{:T(128)} %constant.22.clone.1), window={size=1x1x128 pad=0_0x0_0x127_0}, to_apply=%region_0.0 | reduce-window | flops 2080768 | bytes 131076 | tf_op jit(solution)/shard_map/reduce-window
  15.1 7.6 %scatter_custom_fusion.1 = bf16[2048]{0:T(1024)(128)(2,1)S(1)} fusion(s32[1024]{0:T(1024)S(1)} %bitcast.77, bf16[1024]{0:T(1024)(128)(2,1)S(1)} %convert_convert_fusion, bf16[]{:T(256)} %constant.20.clone.1), kind=kCustom, calls=%fused_computation.79 | custom fusion | bytes 4098 | tf_op jit(solution)/shard_map/scatter | solution.py:88
  23.3 8.3 %all-to-all-start.1 = ((bf16[16,128,1]{1,2,0:T(2,128)(2,1)}), bf16[16,128,1]{1,2,0:T(2,128)(2,1)S(1)}, u32[]{:S(2)}, u32[]{:S(2)}) async-start(bf16[16,128,1]{1,2,0:T(2,128)(2,1)} %copy.30), calls=%async_computation.1 | async-start | bytes 16384 | tf_op jit(solution)/shard_map/all_to_all | solution.py:92
  33.1 6.0 %scatter_custom_fusion = bf16[2048,256]{1,0:T(8,128)(2,1)} fusion(s32[1024]{0:T(1024)S(1)} %bitcast.78, bf16[1024,256]{1,0:T(8,128)(2,1)S(1)} %fusion.21, bf16[]{:T(256)} %constant.20.clone.1), kind=kCustom, calls=%fused_computation.57 | custom fusion | bytes 1048578 | tf_op jit(solution)/shard_map/scatter | solution.py:83
  39.1 6.9 %all-to-all-start = ((bf16[16,128,256]{2,1,0:T(8,128)(2,1)}), bf16[16,128,256]{2,1,0:T(8,128)(2,1)S(1)}, u32[]{:S(2)}, u32[]{:S(2)}) async-start(bf16[16,128,256]{2,1,0:T(8,128)(2,1)} %bitcast.62), calls=%async_computation | async-start | bytes 2097152 | tf_op jit(solution)/shard_map/all_to_all | solution.py:91
  46.4 2.1 convolution_convert_fusion.2
  48.5 1.8 copy.32
  50.3 1.6 abs_multiply_fusion
  51.8 18.0 %all-to-all-done = bf16[16,128,256]{2,1,0:T(8,128)(2,1)S(1)} async-done(((bf16[16,128,256]{2,1,0:T(8,128)(2,1)}), bf16[16,128,256]{2,1,0:T(8,128)(2,1)S(1)}, u32[]{:S(2)}, u32[]{:S(2)}) %all-to-all-start) | async-done | bytes 1048608 | tf_op jit(solution)/shard_map/all_to_all | solution.py:91
  69.9 2.3 convolution_convert_fusion
  72.2 2.6 fusion.53
  74.8 10.6 %fusion.56 = (f32[8,256]{1,0:T(8,128)S(1)}, f32[8,256,2048]{2,1,0:T(8,128)}) fusion(f32[256,2048]{1,0:T(8,128)} %abs_multiply_fusion, pred[2048]{0:T(1024)(128)(4,1)S(1)} %fusion.44, bf16[256,8,64]{0,2,1:T(8,128)(2,1)S(1)} %bitcast.69, bf16[2048,8,64]{0,2,1:T(8,128)(2,1)} %bitcast.64), kind=kOutput, calls=%fused_computation.94 | convolution fusion | flops 557844480 | bytes 21243904 | tf_op jit(solution)/shard_map/sub | solution.py:39
  85.4 9.2 %fusion.24 = bf16[8,64,256]{2,1,0:T(8,128)(2,1)S(1)} fusion(bf16[2048,8,64]{0,2,1:T(8,128)(2,1)} %bitcast.63, f32[8,256,2048]{2,1,0:T(8,128)} %get-tuple-element.9, f32[8,256]{1,0:T(8,128)S(1)} %get-tuple-element.8), kind=kOutput, calls=%fused_computation.43 | convolution fusion | flops 545390592 | bytes 19144704 | tf_op jit(solution)/shard_map/hlr,rhd->lhd/dot_general | solution.py:42
  97.5 4.5 %collective-permute-start.1 = (bf16[128,1024]{1,0:T(8,128)(2,1)}, bf16[128,1024]{1,0:T(8,128)(2,1)}, u32[]{:S(2)}, u32[]{:S(2)}) collective-permute-start(bf16[128,1024]{1,0:T(8,128)(2,1)} %get-tuple-element.7), channel_id=1, source_target_pairs={{2,0},{4,2},{6,4},{8,6},{10,8},{12,10},{14,12},{16,14},{18,16},{20... | collective-permute-start | bytes 786440 | tf_op jit(solution)/shard_map/ppermute | solution.py:18
  102.9 3.4 %collective-permute-done.1 = bf16[128,1024]{1,0:T(8,128)(2,1)} collective-permute-done((bf16[128,1024]{1,0:T(8,128)(2,1)}, bf16[128,1024]{1,0:T(8,128)(2,1)}, u32[]{:S(2)}, u32[]{:S(2)}) %collective-permute-start.1) | collective-permute-done | bytes 262176 | tf_op jit(solution)/shard_map/ppermute | solution.py:18
  106.3 5.9 %collective-permute-done = bf16[128,1024]{1,0:T(8,128)(2,1)} collective-permute-done((bf16[128,1024]{1,0:T(8,128)(2,1)}, bf16[128,1024]{1,0:T(8,128)(2,1)}, u32[]{:S(2)}, u32[]{:S(2)}) %collective-permute-start) | collective-permute-done | bytes 262176 | tf_op jit(solution)/shard_map/ppermute | solution.py:15
  114.2 2.0 copy.33
  117.2 4.7 %fusion.57 = (f32[8,256]{1,0:T(8,128)S(1)}, f32[8,256,512]{2,1,0:T(8,128)}) fusion(pred[256,512]{1,0:T(8,128)(4,1)S(1)} %fusion.31, bf16[256,8,64]{0,2,1:T(8,128)(2,1)S(1)} %bitcast.68, bf16[512,8,64]{0,2,1:T(8,128)(2,1)} %bitcast.66), kind=kOutput, calls=%fused_computation.95 | convolution fusion | flops 138412544 | bytes 5120000 | tf_op jit(solution)/shard_map/sub | solution.py:39
  121.9 3.1 fusion.23
  126.6 2.8 fusion.58
  129.4 3.1 fusion.22
  132.5 163.9 %all-reduce.2.cloned.1.call-done = f32[2048,512]{1,0:T(8,128)} async-done(((f32[2048,512]{1,0:T(8,128)}), f32[2048,512]{1,0:T(8,128)}) %all-reduce.2.cloned.1.call-update) | async-done | bytes 4194320 | tf_op jit(solution)/shard_map/psum | solution.py:125
  296.4 3.9 %multiply_reduce_fusion = f32[]{:T(128)} fusion(f32[2048,512]{1,0:T(8,128)} %all-reduce.2.cloned.1.call-done), kind=kLoop, calls=%fused_computation.13 | loop fusion | flops 2097151 | bytes 4194308 | tf_op jit(solution)/shard_map/reduce_sum | solution.py:126
  301.0 4.7 %broadcast_multiply_fusion = f32[2048,512]{1,0:T(8,128)} fusion(f32[2048,512]{1,0:T(8,128)} %all-reduce.2.cloned.1.call-done, f32[]{:T(128)S(6)} %min.3), kind=kLoop, calls=%fused_computation.29 | loop fusion | flops 1048576 | bytes 8388612 | tf_op jit(solution)/shard_map/mul | solution.py:127
  (56 shorter events, 14.2 us)
Async XLA Ops:
  7.2 118.3 %copy-start = (bf16[512,2048]{1,0:T(8,128)(2,1)S(1)}, bf16[512,2048]{1,0:T(8,128)(2,1)}, u32[]{:S(2)}) copy-start(bf16[512,2048]{1,0:T(8,128)(2,1)} %param.25) | copy-start | bytes 6291460
  23.3 15.8 %all-to-all-start.1 = ((bf16[16,128,1]{1,2,0:T(2,128)(2,1)}), bf16[16,128,1]{1,2,0:T(2,128)(2,1)S(1)}, u32[]{:S(2)}, u32[]{:S(2)}) async-start(bf16[16,128,1]{1,2,0:T(2,128)(2,1)} %copy.30), calls=%async_computation.1 | async-start | bytes 16384 | tf_op jit(solution)/shard_map/all_to_all | solution.py:92
  31.6 14.7 %copy-start.1 = (bf16[256,512]{1,0:T(8,128)(2,1)S(1)}, bf16[256,512]{1,0:T(8,128)(2,1)}, u32[]{:S(2)}) copy-start(bf16[256,512]{1,0:T(8,128)(2,1)} %param.18) | copy-start | bytes 786436
  39.1 30.8 %all-to-all-start = ((bf16[16,128,256]{2,1,0:T(8,128)(2,1)}), bf16[16,128,256]{2,1,0:T(8,128)(2,1)S(1)}, u32[]{:S(2)}, u32[]{:S(2)}) async-start(bf16[16,128,256]{2,1,0:T(8,128)(2,1)} %bitcast.62), calls=%async_computation | async-start | bytes 2097152 | tf_op jit(solution)/shard_map/all_to_all | solution.py:91
  46.0 250.4 %all-reduce.2.cloned.1.call-start = ((), (), s32[]{:S(2)}) async-start(), calls=%async_computation.2 | async-start | bytes 8388608 | tf_op jit(solution)/shard_map/psum | solution.py:125
  72.2 2.6 copy-start.9
  85.4 9.2 %copy-start.6 = (bf16[512,512]{1,0:T(8,128)(2,1)S(1)}, bf16[512,512]{1,0:T(8,128)(2,1)}, u32[]{:S(2)}) copy-start(bf16[512,512]{1,0:T(8,128)(2,1)} %param.22) | copy-start | bytes 1572868
  94.6 1.4 copy-start.2
  97.5 8.9 %collective-permute-start.1 = (bf16[128,1024]{1,0:T(8,128)(2,1)}, bf16[128,1024]{1,0:T(8,128)(2,1)}, u32[]{:S(2)}, u32[]{:S(2)}) collective-permute-start(bf16[128,1024]{1,0:T(8,128)(2,1)} %get-tuple-element.7), channel_id=1, source_target_pairs={{2,0},{4,2},{6,4},{8,6},{10,8},{12,10},{14,12},{16,14},{18,16},{20... | collective-permute-start | bytes 786440 | tf_op jit(solution)/shard_map/ppermute | solution.py:18
  101.9 10.3 %collective-permute-start = (bf16[128,1024]{1,0:T(8,128)(2,1)}, bf16[128,1024]{1,0:T(8,128)(2,1)}, u32[]{:S(2)}, u32[]{:S(2)}) collective-permute-start(bf16[128,1024]{1,0:T(8,128)(2,1)} %get-tuple-element.6), channel_id=1, source_target_pairs={{0,2},{2,4},{4,6},{6,8},{8,10},{10,12},{12,14},{14,16},{16,18},{18... | collective-permute-start | bytes 786440 | tf_op jit(solution)/shard_map/ppermute | solution.py:15
  113.3 3.9 %copy-start.8 = (bf16[256,512]{0,1:T(8,128)(2,1)S(1)}, bf16[256,512]{0,1:T(8,128)(2,1)}, u32[]{:S(2)}) copy-start(bf16[256,512]{0,1:T(8,128)(2,1)} %copy.34) | copy-start | bytes 786436
  117.2 4.7 %copy-start.5 = (bf16[512,512]{0,1:T(8,128)(2,1)S(1)}, bf16[512,512]{0,1:T(8,128)(2,1)}, u32[]{:S(2)}) copy-start(bf16[512,512]{0,1:T(8,128)(2,1)} %copy.33) | copy-start | bytes 1572868
  121.9 3.1 copy-start.3
  125.4 1.1 copy-start.4
  125.5 1.1 copy-start.7
Sparse Core Ops, SparseCore 0:
  129.5 166.8 all-reduce.1
where the time goes:
time: 313 us; the launch traced here: 312 us
  waiting for transfers between devices  191 us (61%)
  matrix products  41.8 us (13%)
  local copies, waits for them, and re-layouts  25.6 us (8%)
  starting transfers between devices  19.9 us (6%)
  other arithmetic  19 us (6%)
  between operations  15 us (5%)
    psum x1, waiting for transfers between devices, on_device(): summed = lax.psum(hidden_product(hidden, cotangent), 'tile')  164 us
    all_to_all x1, waiting for transfers between devices, on_device(): lax.all_to_all(outgoing, 'tile', split_axis=0, concat_axis=0, tiled=True)  18 us
    sub x2, matrix products, attend(): expo = jnp.exp(scores - row_peak)  15.3 us
    dot_general x2, matrix products, attend(): jnp.einsum('hlr,rhd->lhd', weights, value_heads, preferred_element_type=j...  12.3 us
    all_to_all x1, starting transfers between devices, on_device(): lax.all_to_all(marker, 'tile', split_axis=0, concat_axis=0, tiled=True)  8.31 us
    scatter x1, local copies, waits for them, and re-layouts, on_device(): marker = jnp.zeros((devices * capacity,), jnp.bfloat16).at[slot].set((cel...  7.58 us
    all_to_all x1, starting transfers between devices, on_device(): lax.all_to_all(outgoing, 'tile', split_axis=0, concat_axis=0, tiled=True)  6.91 us
  transfers between devices with their start and end apart: 5, of which 4 were waited for; matrix products, arithmetic and copies ran while one was open for 5% of the time, Pallas kernels for 0%

commit v1 on v0

v1 whole, which is shorter than its diff:
```python
import functools
import jax
import jax.numpy as jnp
from jax import lax
from jax.experimental import pallas as pl
from jax.experimental.pallas import tpu as pltpu
from jax.sharding import PartitionSpec as P

H = 8
LANES = 128
BF = jnp.bfloat16
F32 = jnp.float32
VMEM_LIMIT = 48 * 1024 * 1024


def dot(a, b, dims=((1,), (0,))):
    return lax.dot_general(a, b, (dims, ((), ())), preferred_element_type=F32)


def rms_norm(values):
    return values * lax.rsqrt(jnp.mean(values * values, axis=-1, keepdims=True) + 1e-06)


def iota(shape, dim):
    return lax.broadcasted_iota(jnp.int32, shape, dim)


def call(kernel, out_shape, flops, moved, scratch=(), in_specs=None, transcendentals=0):
    kwargs = {} if in_specs is None else {"in_specs": in_specs}
    return pl.pallas_call(
        kernel,
        out_shape=out_shape,
        scratch_shapes=scratch,
        compiler_params=pltpu.CompilerParams(vmem_limit_bytes=VMEM_LIMIT),
        cost_estimate=pl.CostEstimate(
            flops=flops, bytes_accessed=moved, transcendentals=transcendentals
        ),
        **kwargs,
    )


def pack_kernel(obs, inst, route, cell, table, out, *, tiles, cap):
    rows, channels = obs.shape
    kinds = (iota((table.shape[0], rows), 0) == inst[...]).astype(F32).astype(BF)
    embedded = (obs[...].astype(F32) + dot(kinds, table[...], ((0,), (0,)))).astype(BF)
    chosen = (iota((tiles, rows), 0) == route[...]).astype(F32)
    pieces = rows // LANES
    stacked = jnp.concatenate(
        [chosen[:, i * LANES : (i + 1) * LANES] for i in range(pieces)], axis=0
    )
    upto = (iota((LANES, LANES), 0) <= iota((LANES, LANES), 1)).astype(F32).astype(BF)
    counted = dot(stacked.astype(BF), upto)
    base = jnp.zeros((tiles, 1), F32)
    parts = []
    for i in range(pieces):
        part = counted[i * tiles : (i + 1) * tiles]
        parts.append(part + base)
        base = base + part[:, LANES - 1 :]
    place = jnp.concatenate(parts, axis=1)
    rank = (jnp.sum(chosen * place, axis=0, keepdims=True) - 1.0).astype(jnp.int32)
    mark = chosen * (cell[...] + 1).astype(F32)
    at_rank = (iota((cap, rows), 0) == rank).astype(F32).astype(BF)
    marks = dot(mark.astype(BF), at_rank, ((1,), (1,))).astype(BF)
    slot = route[...] * cap + rank
    step = min(256, tiles * cap)
    for first in range(0, tiles * cap, step):
        pick = (iota((step, rows), 0) + first == slot).astype(F32).astype(BF)
        moved = dot(pick, embedded).astype(BF)
        for i in range(step // cap):
            t = first // cap + i
            for c in range(channels // LANES):
                out[t, c * cap : (c + 1) * cap, :] = moved[
                    i * cap : (i + 1) * cap, c * LANES : (c + 1) * LANES
                ]
    tail = out.shape[1] - (channels // LANES) * cap
    if cap < LANES:
        marks = jnp.concatenate([marks, jnp.zeros((tiles, LANES - cap), BF)], axis=1)
    for t in range(tiles):
        out[t, (channels // LANES) * cap :, :] = jnp.broadcast_to(
            marks[t : t + 1, :].astype(F32), (tail, LANES)
        ).astype(BF)


def heads_pair(query, keys, values, add):
    low = iota(query.shape, 1) < query.shape[1] // 2
    zero = jnp.zeros_like(query)
    with_ones = jnp.concatenate([values, jnp.ones_like(values)], axis=1)
    results = []
    for q in (jnp.where(low, query, zero), jnp.where(low, zero, query)):
        scores = dot(q, keys, ((1,), (1,))) + add
        expo = jnp.exp(scores - jnp.max(scores, axis=1, keepdims=True)).astype(BF)
        mixed = dot(expo, with_ones)
        results.append(mixed[:, : query.shape[1]] / mixed[:, query.shape[1] :])
    return jnp.where(low, results[0], results[1]).astype(BF)


def cross_kernel(
    arrived, marks, latent, w_kv, w_q, w_out, stream_out, top, bottom, x, kv, q, add, cross, *, cap
):
    tiles = arrived.shape[0]
    cells, width = latent.shape
    for s in range(tiles):
        for c in range(x.shape[1] // LANES):
            x[s * cap : (s + 1) * cap, c * LANES : (c + 1) * LANES] = arrived[
                s, c * cap : (c + 1) * cap, :
            ]
    kv[...] = dot(x[...], w_kv[...]).astype(BF)
    latent_f = latent[...].astype(F32)
    scale = (width // H) ** -0.5
    q[...] = (dot(rms_norm(latent_f).astype(BF), w_q[...]).astype(BF).astype(F32) * scale).astype(
        BF
    )
    mark = marks[...]
    positions = iota((cells, 1), 0).astype(F32)
    add[...] = jnp.where(mark > 0.5, -4.0 * jnp.abs(positions - (mark - 1.0)) / cells, -1e30)

    def pair(p, carry):
        at = pl.multiple_of(p * LANES, LANES)
        cross[:, pl.ds(at, LANES)] = heads_pair(
            q[:, pl.ds(at, LANES)],
            kv[:, pl.ds(at, LANES)],
            kv[:, pl.ds(pl.multiple_of(width + p * LANES, LANES), LANES)],
            add[...],
        )
        return carry

    lax.fori_loop(0, width // LANES, pair, 0)
    stream = latent_f + dot(cross[...], w_out[...])
    stream_out[...] = stream
    normed = rms_norm(stream).astype(BF)
    top[...] = normed[: cells // 2]
    bottom[...] = normed[cells // 2 :]


def window_kernel(
    stream_in,
    before,
    top,
    bottom,
    after,
    w_qkv,
    w_out,
    w_up,
    stream_out,
    hidden,
    sliced,
    around,
    kv,
    q,
    add,
    mixed,
):
    cells, width = stream_in.shape
    reach = cells // 2
    for i, part in enumerate((before, top, bottom, after)):
        around[i * reach : (i + 1) * reach, :] = part[...]
    kv[...] = dot(around[...], w_qkv[:, width:]).astype(BF)
    scale = (width // H) ** -0.5
    own = around[reach : reach + cells, :]
    q[...] = (dot(own, w_qkv[:, :width]).astype(BF).astype(F32) * scale).astype(BF)
    offsets = iota(add.shape, 1) - iota(add.shape, 0)
    add[...] = jnp.where((offsets >= 0) & (offsets <= 2 * reach), 0.0, -1e30)

    def pair(p, carry):
        at = pl.multiple_of(p * LANES, LANES)
        mixed[:, pl.ds(at, LANES)] = heads_pair(
            q[:, pl.ds(at, LANES)],
            kv[:, pl.ds(at, LANES)],
            kv[:, pl.ds(pl.multiple_of(width + p * LANES, LANES), LANES)],
            add[...],
        )
        return carry

    lax.fori_loop(0, width // LANES, pair, 0)
    stream = stream_in[...] + dot(mixed[...], w_out[...])
    stream_out[...] = stream
    normed = rms_norm(stream).astype(BF)
    tiles, _, part = sliced.shape
    step = 512
    for first in range(0, hidden.shape[1], step):
        block = jax.nn.gelu(dot(normed, w_up[:, first : first + step])).astype(BF)
        hidden[:, first : first + step] = block
        if part == LANES:
            for i in range(step // LANES):
                sliced[first // LANES + i] = block[:, i * LANES : (i + 1) * LANES]


def down_kernel(stream, hidden, w_down, out):
    out[...] = (stream[...] + dot(hidden[...], w_down[...])).astype(BF)


def gradient_kernel(hidden, cotangent, out):
    out[...] = dot(hidden[...], cotangent[...], ((0,), (0,))).astype(BF)


def clip_kernel(me, *refs, order):
    pieces, out = refs[:-1], refs[-1]
    total = jnp.zeros((1, 1), F32)
    for piece in pieces:
        for i in range(piece.shape[0]):
            v = piece[i].astype(F32)
            total = total + jnp.sum(jnp.sum(v * v, axis=0, keepdims=True), axis=1, keepdims=True)
    factor = jnp.minimum(1.0, 0.5 / jnp.sqrt(total / (out.shape[0] * out.shape[1]) + 1e-06))
    for piece, steps in zip(pieces, order, strict=True):
        rows = piece.shape[1]
        for i, (flip, base, stride) in enumerate(steps):
            at = pl.multiple_of((me[0] ^ flip) * stride + base, rows)
            out[pl.ds(at, rows), :] = piece[i].astype(F32) * factor


def gathered(part, axis):
    count = lax.axis_size(axis)
    rows = part.shape[0]
    if count != 16 or rows % 32:
        whole = lax.all_gather(part, axis, axis=0)
        return [whole.reshape(1, count * rows, -1)], [[(0, 0, 0)]]

    def flipped(value, k):
        return lax.ppermute(value, axis, [(i, i ^ k) for i in range(count)])

    half = rows // 2
    column = (0, 4, 8, 12)
    stack = jnp.stack([part] + [flipped(part, k) for k in column[1:]], axis=0)
    first, second = stack[:, :half], stack[:, half:]
    first_1, second_1 = flipped(first, 1), flipped(second, 2)
    first = jnp.concatenate([first, first_1], axis=0)
    second = jnp.concatenate([second, second_1], axis=0)
    first_2, second_2 = flipped(first, 2), flipped(second, 1)
    order_a = [(k, 0, rows) for k in column] + [(k ^ 1, 0, rows) for k in column]
    order_b = [(k, half, rows) for k in column] + [(k ^ 2, half, rows) for k in column]
    return [first, first_2, second, second_2], [
        order_a,
        [(k ^ 2, b, s) for k, b, s in order_a],
        order_b,
        [(k ^ 1, b, s) for k, b, s in order_b],
    ]


def on_device(
    observations,
    instrument,
    route,
    cell_index,
    latent,
    inst_table,
    w_obs_kv,
    w_cross_q,
    w_cross_out,
    w_win_qkv,
    w_win_out,
    w_up,
    w_down,
    cotangent,
):
    tiles = lax.axis_size("tile")
    count, channels = observations.shape
    cells, width = latent.shape
    hidden_width = w_up.shape[1]
    cap = 2 * count // tiles
    keys = tiles * cap
    split = channels // LANES
    block_rows = split * cap + 8
    shape = jax.ShapeDtypeStruct

    payload = call(
        functools.partial(pack_kernel, tiles=tiles, cap=cap),
        shape((tiles, block_rows, LANES), BF),
        2 * keys * count * channels,
        2 * keys * channels + 2 * count * channels,
    )(
        observations,
        instrument.reshape(1, count),
        route.reshape(1, count),
        cell_index.reshape(1, count),
        inst_table,
    )
    arrived = lax.all_to_all(payload, "tile", split_axis=0, concat_axis=0, tiled=True)
    cot_all = lax.all_gather(cotangent, "tile", axis=0, tiled=True)
    marks = arrived[:, split * cap, :cap].reshape(1, keys).astype(F32)

    stream1, top, bottom = call(
        functools.partial(cross_kernel, cap=cap),
        (
            shape((cells, width), F32),
            shape((cells // 2, width), BF),
            shape((cells // 2, width), BF),
        ),
        4 * keys * channels * width + 4 * cells * keys * width,
        2 * keys * channels + 6 * width * width,
        scratch=[
            pltpu.VMEM((keys, channels), BF),
            pltpu.VMEM((keys, 2 * width), BF),
            pltpu.VMEM((cells, width), BF),
            pltpu.VMEM((cells, keys), F32),
            pltpu.VMEM((cells, width), BF),
        ],
        transcendentals=H * cells * keys,
    )(arrived, marks, latent, w_obs_kv, w_cross_q, w_cross_out)

    forward = [(i, (i + 1) % tiles) for i in range(tiles)]
    backward = [(b, a) for a, b in forward]
    before = lax.ppermute(bottom, "tile", forward)
    after = lax.ppermute(top, "tile", backward)

    part = hidden_width // tiles
    direct = part == LANES
    stream2, hidden, sliced = call(
        window_kernel,
        (
            shape((cells, width), F32),
            shape((cells, hidden_width), BF),
            shape((tiles, cells, part) if direct else (1, 16, LANES + 1), BF),
        ),
        2 * cells * width * (5 * width + hidden_width) + 8 * cells * cells * width,
        2 * width * (4 * width + hidden_width) + 4 * cells * hidden_width,
        scratch=[
            pltpu.VMEM((2 * cells, width), BF),
            pltpu.VMEM((2 * cells, 2 * width), BF),
            pltpu.VMEM((cells, width), BF),
            pltpu.VMEM((cells, 2 * cells), F32),
            pltpu.VMEM((cells, width), BF),
        ],
        transcendentals=2 * H * cells * cells + cells * hidden_width,
    )(stream1, before, top, bottom, after, w_win_qkv, w_win_out, w_up)
    if not direct:
        sliced = hidden.reshape(cells, tiles, part).transpose(1, 0, 2)
    swapped = lax.all_to_all(sliced, "tile", split_axis=0, concat_axis=0, tiled=True)
    latent_out = call(
        down_kernel,
        shape((cells, width), BF),
        2 * cells * width * hidden_width,
        2 * width * hidden_width + 2 * cells * hidden_width,
    )(stream2, hidden, w_down)
    gradient = call(
        gradient_kernel,
        shape((part, width), BF),
        2 * tiles * cells * part * width,
        2 * tiles * cells * (part + width),
    )(swapped.reshape(tiles * cells, part), cot_all)
    pieces, order = gathered(gradient, "tile")
    clipped = call(
        functools.partial(clip_kernel, order=order),
        shape((hidden_width, width), F32),
        4 * hidden_width * width,
        6 * hidden_width * width,
        in_specs=[pl.BlockSpec(memory_space=pltpu.SMEM)]
        + [pl.BlockSpec(memory_space=pltpu.VMEM)] * len(pieces),
    )(lax.axis_index("tile").reshape(1), *pieces)
    return (latent_out, clipped)


def solution(mesh):
    split = P(("dp", "tile"))
    rows = P(("dp", "tile"), None)
    return jax.shard_map(
        on_device,
        mesh=mesh,
        in_specs=(rows, split, rows, split, rows, P(), P(), P(), P(), P(), P(), P(), P(), rows),
        out_specs=(rows, P("dp", None)),
        check_vma=False,
    )
```

time: 313 us -> 175 us (0.56)
  waiting for transfers between devices: 191 us -> 29.8 us
  blocking collectives: 0 us -> 80.5 us
  matrix products: 41.8 us -> 0 us
  Pallas kernels: 0 us -> 25.4 us
  other arithmetic: 19 us -> 0.17 us
  local copies, waits for them, and re-layouts: 25.6 us -> 10.1 us
  starting transfers between devices: 19.9 us -> 14.2 us
    psum x1 -> x0, waiting for transfers between devices: 164 us -> none  [on_device(): summed = lax.psum(hidden_product(hidden, cotangent), 'tile')]
    all_to_all x0 -> x2, blocking collectives: none -> 80.5 us  [the longest x1 53 us: on_device(): lax.all_to_all(payload, 'tile', split_axis=0, concat_axis=0, tiled=True)]
    dot_general x11 -> x0, matrix products: 26.5 us -> none  [the longest x2 12.3 us: attend(): jnp.einsum('hlr,rhd->lhd', weights, value_heads, preferred_element_type=j...]
    pallas_call x0 -> x6, Pallas kernels: none -> 25.4 us  [the longest x1 11.1 us: on_device(): call(functools.partial(cross_kernel, cap=cap), (shape((cells, width), F32...]
    ppermute x2 -> x9, waiting for transfers between devices: 9.26 us -> 29.2 us  [the longest x7 21.2 us: flipped(): return lax.ppermute(value, axis, [(i, i ^ k) for i in range(count)])]
    all_to_all x2 -> x0, waiting for transfers between devices: 18 us -> none  [the longest x1 18 us: on_device(): lax.all_to_all(outgoing, 'tile', split_axis=0, concat_axis=0, tiled=True)]
    sub x2 -> x0, matrix products: 15.3 us -> none  [attend(): expo = jnp.exp(scores - row_peak)]
    all_to_all x2 -> x0, starting transfers between devices: 15.2 us -> none  [the longest x1 8.31 us: on_device(): lax.all_to_all(marker, 'tile', split_axis=0, concat_axis=0, tiled=True)]
  transfers between devices with their start and end apart: 5 -> 10, of which waited for: 4 -> 7; matrix products, arithmetic and copies ran while one was open for 5% -> 0% of each run, Pallas kernels for 0% -> 12%
where the time goes in v1:
time: 175 us; the launch traced here: 174 us
  blocking collectives  80.5 us (46%)
  waiting for transfers between devices  29.8 us (17%)
  Pallas kernels  25.4 us (15%)
  starting transfers between devices  14.2 us (8%)
  between operations  14.2 us (8%)
  local copies, waits for them, and re-layouts  10.1 us (6%)
    all_to_all x1, blocking collectives, on_device(): lax.all_to_all(payload, 'tile', split_axis=0, concat_axis=0, tiled=True)  53 us
    all_to_all x1, blocking collectives, on_device(): lax.all_to_all(sliced, 'tile', split_axis=0, concat_axis=0, tiled=True)  27.5 us
    ppermute x7, waiting for transfers between devices, flipped(): return lax.ppermute(value, axis, [(i, i ^ k) for i in range(count)])  21.2 us
    pallas_call x1, Pallas kernels, on_device(): call(functools.partial(cross_kernel, cap=cap), (shape((cells, width), F32...  11.1 us
    unnamed x34, local copies, waits for them, and re-layouts  10.1 us
    ppermute x7, starting transfers between devices, flipped(): return lax.ppermute(value, axis, [(i, i ^ k) for i in range(count)])  8.46 us
    pallas_call x1, Pallas kernels, on_device(): call(window_kernel, (shape((cells, width), F32), shape((cells, hidden_wid...  6.66 us
    ppermute x1, waiting for transfers between devices, on_device(): before = lax.ppermute(bottom, 'tile', forward)  5.73 us
  transfers between devices with their start and end apart: 10, of which 7 were waited for; matrix products, arithmetic and copies ran while one was open for 0% of the time, Pallas kernels for 12%

profile of v1, /device:TPU:0, one launch (start us, length us, event | category | flops | bytes accessed | tf_op | source)
XLA Modules:
  0.0 174.4 jit_solution(9973156168241202762)
XLA Ops:
  7.9 1.0 copy-done.7
  11.7 1.7 shard_map.149
  13.4 53.0 %all_to_all.10.arrived = bf16[16,264,128]{2,1,0:T(8,128)(2,1)S(1)} all-to-all(bf16[16,264,128]{2,1,0:T(8,128)(2,1)S(1)} %shard_map.149), channel_id=1, replica_groups=mesh['tile'=16,'dp'=2] {'tile'}, dimensions={0} | all-to-all | bytes 2162688 | tf_op jit(solution)/shard_map/all_to_all | solution.py:277
  66.5 11.1 %shard_map.150 = (f32[256,512]{1,0:T(8,128)S(1)}, bf16[128,512]{1,0:T(8,128)(2,1)S(1)}, bf16[128,512]{1,0:T(8,128)(2,1)S(1)}) custom-call(bf16[16,264,128]{2,1,0:T(8,128)(2,1)S(1)} %all_to_all.10.arrived, f32[1,2048]{1,0:T(1,128)S(1)} %fusion.marks, bf16[256,512]{1,0:T(8,128)(2,1)S(1)} %copy-done.12, bf16[256,1024]{1,0:T(8,128)(2,1)S(1)} %copy-done.8, ...), custom_call_target="tpu_custom_call" | custom-call | flops 2147483648 | bytes 2621440 | tf_op jit(solution)/shard_map/pallas_call | solution.py:281
  78.2 5.1 %collective-permute-start.1 = (bf16[128,512]{1,0:T(8,128)(2,1)S(1)}, bf16[128,512]{1,0:T(8,128)(2,1)S(1)}, u32[]{:S(2)}, u32[]{:S(2)}) collective-permute-start(bf16[128,512]{1,0:T(8,128)(2,1)S(1)} %get-tuple-element.10.top), channel_id=1, source_target_pairs={{2,0},{4,2},{6,4},{8,6},{10,8},{12,10},{14,12},{16,14},{18,16},{20... | collective-permute-start | bytes 393224 | tf_op jit(solution)/shard_map/ppermute | solution.py:303
  83.3 5.7 %collective-permute-done.before = bf16[128,512]{1,0:T(8,128)(2,1)S(1)} collective-permute-done((bf16[128,512]{1,0:T(8,128)(2,1)S(1)}, bf16[128,512]{1,0:T(8,128)(2,1)S(1)}, u32[]{:S(2)}, u32[]{:S(2)}) %collective-permute-start) | collective-permute-done | bytes 131104 | tf_op jit(solution)/shard_map/ppermute | solution.py:302
  89.0 2.2 %collective-permute-done.1.after = bf16[128,512]{1,0:T(8,128)(2,1)S(1)} collective-permute-done((bf16[128,512]{1,0:T(8,128)(2,1)S(1)}, bf16[128,512]{1,0:T(8,128)(2,1)S(1)}, u32[]{:S(2)}, u32[]{:S(2)}) %collective-permute-start.1) | collective-permute-done | bytes 131104 | tf_op jit(solution)/shard_map/ppermute | solution.py:303
  91.2 6.7 %shard_map.151 = (f32[256,512]{1,0:T(8,128)S(1)}, bf16[256,2048]{1,0:T(8,128)(2,1)S(1)}, bf16[16,256,128]{2,1,0:T(8,128)(2,1)S(1)}) custom-call(f32[256,512]{1,0:T(8,128)S(1)} %get-tuple-element.8.stream_in, bf16[128,512]{1,0:T(8,128)(2,1)S(1)} %collective-permute-done.before, bf16[128,512]{1,0:T(8,128)(2,1)S(1)} %get-tuple-element.10.top, ...), custom_call_target="tpu_custom_call" | custom-call | flops 1476395008 | bytes 6291456 | tf_op jit(solution)/shard_map/pallas_call | solution.py:307
  97.9 1.0 copy-done.2
  99.6 27.5 %all_to_all.11 = bf16[16,256,128]{2,1,0:T(8,128)(2,1)S(1)} all-to-all(bf16[16,256,128]{2,1,0:T(8,128)(2,1)S(1)} %get-tuple-element.13), channel_id=1, replica_groups=mesh['tile'=16,'dp'=2] {'tile'}, dimensions={0} | all-to-all | bytes 2097152 | tf_op jit(solution)/shard_map/all_to_all | solution.py:327
  127.2 2.2 %copy-done = bf16[4096,512]{1,0:T(8,128)(2,1)S(1)} copy-done((bf16[4096,512]{1,0:T(8,128)(2,1)S(1)}, bf16[4096,512]{1,0:T(8,128)(2,1)}, u32[]{:S(2)}) %copy-start) | copy-done | bytes 4194328
  130.1 1.9 %collective-permute-start.4 = (bf16[128,512]{1,0:T(8,128)(2,1)S(1)}, bf16[128,512]{1,0:T(8,128)(2,1)S(1)}, u32[]{:S(2)}, u32[]{:S(2)}) collective-permute-start(bf16[128,512]{1,0:T(8,128)(2,1)S(1)} %shard_map.153), channel_id=1, source_target_pairs={{0,24},{2,26},{4,28},{6,30},{8,16},{10,18},{12,20},{14,22},{16,8},... | collective-permute-start | bytes 393224 | tf_op jit(solution)/shard_map/ppermute | solution.py:219
  132.0 0.9 collective-permute-start.3
  132.9 1.6 collective-permute-start.2
  134.6 2.8 %collective-permute-done.4 = bf16[128,512]{1,0:T(8,128)(2,1)S(1)} collective-permute-done((bf16[128,512]{1,0:T(8,128)(2,1)S(1)}, bf16[128,512]{1,0:T(8,128)(2,1)S(1)}, u32[]{:S(2)}, u32[]{:S(2)}) %collective-permute-start.4) | collective-permute-done | bytes 131104 | tf_op jit(solution)/shard_map/ppermute | solution.py:219
  137.4 5.0 %collective-permute-done.3 = bf16[128,512]{1,0:T(8,128)(2,1)S(1)} collective-permute-done((bf16[128,512]{1,0:T(8,128)(2,1)S(1)}, bf16[128,512]{1,0:T(8,128)(2,1)S(1)}, u32[]{:S(2)}, u32[]{:S(2)}) %collective-permute-start.3) | collective-permute-done | bytes 131104 | tf_op jit(solution)/shard_map/ppermute | solution.py:219
  143.2 1.2 collective-permute-start.7
  144.4 5.8 %collective-permute-done.5 = bf16[4,64,512]{2,1,0:T(8,128)(2,1)S(1)} collective-permute-done((bf16[4,64,512]{2,1,0:T(8,128)(2,1)S(1)}, bf16[4,64,512]{2,1,0:T(8,128)(2,1)S(1)}, u32[]{:S(2)}, u32[]{:S(2)}) %collective-permute-start.5) | collective-permute-done | bytes 262176 | tf_op jit(solution)/shard_map/ppermute | solution.py:219
  150.3 1.2 collective-permute-start.6
  152.4 1.2 copy-done.3
  153.7 1.0 copy-done.5
  154.7 1.4 shard_map.152
  156.1 6.8 %collective-permute-done.6.refs_1_ = bf16[8,64,512]{2,1,0:T(8,128)(2,1)} collective-permute-done((bf16[8,64,512]{2,1,0:T(8,128)(2,1)S(1)}, bf16[8,64,512]{2,1,0:T(8,128)(2,1)}, u32[]{:S(2)}, u32[]{:S(2)}) %collective-permute-start.6) | collective-permute-done | bytes 524320 | tf_op jit(solution)/shard_map/ppermute | solution.py:219
  163.7 3.8 %shard_map.154 = f32[2048,512]{1,0:T(8,128)} custom-call(s32[1]{0:T(128)} %bitcast.4.me, bf16[8,64,512]{2,1,0:T(8,128)(2,1)S(1)} %pad_maximum_fusion.1.refs_0_, bf16[8,64,512]{2,1,0:T(8,128)(2,1)} %collective-permute-done.6.refs_1_, bf16[8,64,512]{2,1,0:T(8,128)(2,1)S(1)} %pad_maximum_fusion.2.refs_2_, bf16[8,64,512]{2,1,0:T(8,128)(2,1)} %collective-permute-done.8.refs_3_), custom_call_target="tpu_custom_call" | custom-call | flops 4194304 | bytes 6291456 | tf_op jit(solution)/shard_map/pallas_call | solution.py:341
  (44 shorter events, 8.3 us)
Async XLA Ops:
  7.2 120.0 %all-gather.2.cloned.1.call-start = ((), (), s32[]{:S(2)}) async-start(), calls=%async_computation.2 | async-start | bytes 4456448 | tf_op jit(solution)/shard_map/all_gather | solution.py:278
  7.9 1.0 copy-start.7
  8.9 0.7 copy-start.13
  11.7 54.7 %copy-start.8 = (bf16[256,1024]{1,0:T(8,128)(2,1)S(1)}, bf16[256,1024]{1,0:T(8,128)(2,1)}, u32[]{:S(2)}) copy-start(bf16[256,1024]{1,0:T(8,128)(2,1)} %w_kv.1) | copy-start | bytes 1572868
  11.7 54.7 %copy-start.9 = (bf16[512,512]{1,0:T(8,128)(2,1)S(1)}, bf16[512,512]{1,0:T(8,128)(2,1)}, u32[]{:S(2)}) copy-start(bf16[512,512]{1,0:T(8,128)(2,1)} %w_q.1) | copy-start | bytes 1572868
  11.7 54.7 %copy-start.10 = (bf16[512,512]{1,0:T(8,128)(2,1)S(1)}, bf16[512,512]{1,0:T(8,128)(2,1)}, u32[]{:S(2)}) copy-start(bf16[512,512]{1,0:T(8,128)(2,1)} %w_out.2) | copy-start | bytes 1572868
  11.7 54.7 %copy-start.12 = (bf16[256,512]{1,0:T(8,128)(2,1)S(1)}, bf16[256,512]{1,0:T(8,128)(2,1)}, u32[]{:S(2)}) copy-start(bf16[256,512]{1,0:T(8,128)(2,1)} %latent.1) | copy-start | bytes 786436
  66.4 24.7 %copy-start.6 = (bf16[512,1536]{1,0:T(8,128)(2,1)S(1)}, bf16[512,1536]{1,0:T(8,128)(2,1)}, u32[]{:S(2)}) copy-start(bf16[512,1536]{1,0:T(8,128)(2,1)} %w_qkv.1) | copy-start | bytes 4718596
  66.5 24.7 %copy-start.11 = (bf16[512,512]{1,0:T(8,128)(2,1)S(1)}, bf16[512,512]{1,0:T(8,128)(2,1)}, u32[]{:S(2)}) copy-start(bf16[512,512]{1,0:T(8,128)(2,1)} %w_out.3) | copy-start | bytes 1572868
  77.6 11.4 %collective-permute-start = (bf16[128,512]{1,0:T(8,128)(2,1)S(1)}, bf16[128,512]{1,0:T(8,128)(2,1)S(1)}, u32[]{:S(2)}, u32[]{:S(2)}) collective-permute-start(bf16[128,512]{1,0:T(8,128)(2,1)S(1)} %get-tuple-element.9.bottom), channel_id=1, source_target_pairs={{0,2},{2,4},{4,6},{6,8},{8,10},{10,12},{12,14},{14,16},{16,18},{18... | collective-permute-start | bytes 393224 | tf_op jit(solution)/shard_map/ppermute | solution.py:302
  78.2 13.0 %collective-permute-start.1 = (bf16[128,512]{1,0:T(8,128)(2,1)S(1)}, bf16[128,512]{1,0:T(8,128)(2,1)S(1)}, u32[]{:S(2)}, u32[]{:S(2)}) collective-permute-start(bf16[128,512]{1,0:T(8,128)(2,1)S(1)} %get-tuple-element.10.top), channel_id=1, source_target_pairs={{2,0},{4,2},{6,4},{8,6},{10,8},{12,10},{14,12},{16,14},{18,16},{20... | collective-permute-start | bytes 393224 | tf_op jit(solution)/shard_map/ppermute | solution.py:303
  97.8 1.0 copy-start.2
  98.8 0.8 copy-start.4
  127.2 2.2 %copy-start = (bf16[4096,512]{1,0:T(8,128)(2,1)S(1)}, bf16[4096,512]{1,0:T(8,128)(2,1)}, u32[]{:S(2)}) copy-start(bf16[4096,512]{1,0:T(8,128)(2,1)} %all-gather.2.cloned.1.call-done.cotangent) | copy-start | bytes 12582916
  130.1 7.3 %collective-permute-start.4 = (bf16[128,512]{1,0:T(8,128)(2,1)S(1)}, bf16[128,512]{1,0:T(8,128)(2,1)S(1)}, u32[]{:S(2)}, u32[]{:S(2)}) collective-permute-start(bf16[128,512]{1,0:T(8,128)(2,1)S(1)} %shard_map.153), channel_id=1, source_target_pairs={{0,24},{2,26},{4,28},{6,30},{8,16},{10,18},{12,20},{14,22},{16,8},... | collective-permute-start | bytes 393224 | tf_op jit(solution)/shard_map/ppermute | solution.py:219
  132.0 10.4 %collective-permute-start.3 = (bf16[128,512]{1,0:T(8,128)(2,1)S(1)}, bf16[128,512]{1,0:T(8,128)(2,1)S(1)}, u32[]{:S(2)}, u32[]{:S(2)}) collective-permute-start(bf16[128,512]{1,0:T(8,128)(2,1)S(1)} %shard_map.153), channel_id=1, source_target_pairs={{0,16},{2,18},{4,20},{6,22},{8,24},{10,26},{12,28},{14,30},{16,0},... | collective-permute-start | bytes 393224 | tf_op jit(solution)/shard_map/ppermute | solution.py:219
  132.9 9.4 %collective-permute-start.2 = (bf16[128,512]{1,0:T(8,128)(2,1)S(1)}, bf16[128,512]{1,0:T(8,128)(2,1)S(1)}, u32[]{:S(2)}, u32[]{:S(2)}) collective-permute-start(bf16[128,512]{1,0:T(8,128)(2,1)S(1)} %shard_map.153), channel_id=1, source_target_pairs={{0,8},{2,10},{4,12},{6,14},{8,0},{10,2},{12,4},{14,6},{16,24},{18,... | collective-permute-start | bytes 393224 | tf_op jit(solution)/shard_map/ppermute | solution.py:219
  142.4 10.1 %copy-start.1 = (bf16[2048,512]{1,0:T(8,128)(2,1)S(1)}, bf16[2048,512]{1,0:T(8,128)(2,1)}, u32[]{:S(2)}) copy-start(bf16[2048,512]{1,0:T(8,128)(2,1)} %w_down.1) | copy-start | bytes 6291460
  142.5 7.8 %collective-permute-start.5 = (bf16[4,64,512]{2,1,0:T(8,128)(2,1)S(1)}, bf16[4,64,512]{2,1,0:T(8,128)(2,1)S(1)}, u32[]{:S(2)}, u32[]{:S(2)}) collective-permute-start(bf16[4,64,512]{2,1,0:T(8,128)(2,1)S(1)} %get-tuple-element.15), channel_id=1, source_target_pairs={{0,2},{2,0},{4,6},{6,4},{8,10},{10,8},{12,14},{14,12},{16,18},{18,... | collective-permute-start | bytes 786440 | tf_op jit(solution)/shard_map/ppermute | solution.py:219
  143.2 8.3 %collective-permute-start.7 = (bf16[4,64,512]{2,1,0:T(8,128)(2,1)S(1)}, bf16[4,64,512]{2,1,0:T(8,128)(2,1)S(1)}, u32[]{:S(2)}, u32[]{:S(2)}) collective-permute-start(bf16[4,64,512]{2,1,0:T(8,128)(2,1)S(1)} %get-tuple-element.14), channel_id=1, source_target_pairs={{0,4},{2,6},{4,0},{6,2},{8,12},{10,14},{12,8},{14,10},{16,20},{18,... | collective-permute-start | bytes 786440 | tf_op jit(solution)/shard_map/ppermute | solution.py:219
  150.3 12.6 %collective-permute-start.6 = (bf16[8,64,512]{2,1,0:T(8,128)(2,1)S(1)}, bf16[8,64,512]{2,1,0:T(8,128)(2,1)}, u32[]{:S(2)}, u32[]{:S(2)}) collective-permute-start(bf16[8,64,512]{2,1,0:T(8,128)(2,1)S(1)} %pad_maximum_fusion.1.refs_0_), channel_id=1, source_target_pairs={{0,4},{2,6},{4,0},{6,2},{8,12},{10,14},{12,8},{14,10},{16,20},{18,... | collective-permute-start | bytes 1572872 | tf_op jit(solution)/shard_map/ppermute | solution.py:219
  151.6 12.1 %collective-permute-start.8 = (bf16[8,64,512]{2,1,0:T(8,128)(2,1)S(1)}, bf16[8,64,512]{2,1,0:T(8,128)(2,1)}, u32[]{:S(2)}, u32[]{:S(2)}) collective-permute-start(bf16[8,64,512]{2,1,0:T(8,128)(2,1)S(1)} %pad_maximum_fusion.2.refs_2_), channel_id=1, source_target_pairs={{0,2},{2,0},{4,6},{6,4},{8,10},{10,8},{12,14},{14,12},{16,18},{18,... | collective-permute-start | bytes 1572872 | tf_op jit(solution)/shard_map/ppermute | solution.py:219
  152.4 1.2 copy-start.3
  153.7 1.0 copy-start.5
  (3 other events, 2.1 us)
Sparse Core Ops, SparseCore 0:
  10.8 92.5 all-gather.1

commit v2 on v1

--- a/solution.py
+++ b/solution.py
@@ -11,6 +11,7 @@
 BF = jnp.bfloat16
 F32 = jnp.float32
 VMEM_LIMIT = 48 * 1024 * 1024
+PLANE = 4
 
 
 def dot(a, b, dims=((1,), (0,))):
@@ -25,13 +26,15 @@
     return lax.broadcasted_iota(jnp.int32, shape, dim)
 
 
-def call(kernel, out_shape, flops, moved, scratch=(), in_specs=None, transcendentals=0):
+def call(
+    kernel, out_shape, flops, moved, scratch=(), in_specs=None, transcendentals=0, limit=VMEM_LIMIT
+):
     kwargs = {} if in_specs is None else {"in_specs": in_specs}
     return pl.pallas_call(
         kernel,
         out_shape=out_shape,
         scratch_shapes=scratch,
-        compiler_params=pltpu.CompilerParams(vmem_limit_bytes=VMEM_LIMIT),
+        compiler_params=pltpu.CompilerParams(vmem_limit_bytes=limit),
         cost_estimate=pl.CostEstimate(
             flops=flops, bytes_accessed=moved, transcendentals=transcendentals
         ),
@@ -39,7 +42,17 @@
     )
 
 
-def pack_kernel(obs, inst, route, cell, table, out, *, tiles, cap):
+def pack_kernel(*refs, tiles, cap):
+    inputs, out, local, arrivals = refs[:5], refs[5], refs[6:11], refs[11]
+    copies = [
+        pltpu.make_async_copy(source, target, arrivals.at[i])
+        for i, (source, target) in enumerate(zip(inputs, local, strict=True))
+    ]
+    for copy in copies:
+        copy.start()
+    for copy in copies:
+        copy.wait()
+    obs, inst, route, cell, table = local
     rows, channels = obs.shape
     kinds = (iota((table.shape[0], rows), 0) == inst[...]).astype(F32).astype(BF)
     embedded = (obs[...].astype(F32) + dot(kinds, table[...], ((0,), (0,)))).astype(BF)
@@ -133,6 +146,7 @@
 
 
 def window_kernel(
+    me,
     stream_in,
     before,
     top,
@@ -143,13 +157,9 @@
     w_up,
     stream_out,
     hidden,
-    sliced,
-    around,
-    kv,
-    q,
-    add,
-    mixed,
+    *refs,
 ):
+    sliced, (around, kv, q, add, mixed) = refs[:-5], refs[-5:]
     cells, width = stream_in.shape
     reach = cells // 2
     for i, part in enumerate((before, top, bottom, after)):
@@ -175,14 +185,13 @@
     stream = stream_in[...] + dot(mixed[...], w_out[...])
     stream_out[...] = stream
     normed = rms_norm(stream).astype(BF)
-    tiles, _, part = sliced.shape
-    step = 512
-    for first in range(0, hidden.shape[1], step):
-        block = jax.nn.gelu(dot(normed, w_up[:, first : first + step])).astype(BF)
-        hidden[:, first : first + step] = block
-        if part == LANES:
-            for i in range(step // LANES):
-                sliced[first // LANES + i] = block[:, i * LANES : (i + 1) * LANES]
+    step = hidden.shape[1] // PLANE
+    for j in range(PLANE):
+        at = pl.multiple_of(((me[0] % PLANE) ^ j) * step, step)
+        block = jax.nn.gelu(dot(normed, w_up[:, pl.ds(at, step)])).astype(BF)
+        hidden[:, pl.ds(at, step)] = block
+        if sliced:
+            sliced[j][...] = block
 
 
 def down_kernel(stream, hidden, w_down, out):
@@ -191,6 +200,18 @@
 
 def gradient_kernel(hidden, cotangent, out):
     out[...] = dot(hidden[...], cotangent[...], ((0,), (0,))).astype(BF)
+
+
+def plane_kernel(me, *refs):
+    hidden, cotangent = refs[:PLANE], refs[PLANE : 2 * PLANE]
+    own, others, total = refs[2 * PLANE], refs[2 * PLANE + 1 : -1], refs[-1]
+    total[...] = sum(
+        dot(h[...], c[...], ((0,), (0,))) for h, c in zip(hidden, cotangent, strict=True)
+    )
+    rows = own.shape[0]
+    for i, out in enumerate((own, *others)):
+        at = pl.multiple_of(((me[0] // PLANE) ^ i) * rows, rows)
+        out[...] = total[pl.ds(at, rows), :].astype(out.dtype)
 
 
 def clip_kernel(me, *refs, order):
@@ -203,23 +224,25 @@
     factor = jnp.minimum(1.0, 0.5 / jnp.sqrt(total / (out.shape[0] * out.shape[1]) + 1e-06))
     for piece, steps in zip(pieces, order, strict=True):
         rows = piece.shape[1]
-        for i, (flip, base, stride) in enumerate(steps):
-            at = pl.multiple_of((me[0] ^ flip) * stride + base, rows)
+        for i, step in enumerate(steps):
+            at = 0
+            if step is not None:
+                flip, base, stride = step
+                tile = me[0] ^ flip
+                at = pl.multiple_of(
+                    ((tile % PLANE) * PLANE + tile // PLANE) * stride + base, rows
+                )
             out[pl.ds(at, rows), :] = piece[i].astype(F32) * factor
 
 
-def gathered(part, axis):
-    count = lax.axis_size(axis)
+def flipped(value, k):
+    return lax.ppermute(value, "tile", [(i, i ^ k) for i in range(PLANE * PLANE)])
+
+
+def gathered(part):
     rows = part.shape[0]
-    if count != 16 or rows % 32:
-        whole = lax.all_gather(part, axis, axis=0)
-        return [whole.reshape(1, count * rows, -1)], [[(0, 0, 0)]]
-
-    def flipped(value, k):
-        return lax.ppermute(value, axis, [(i, i ^ k) for i in range(count)])
-
     half = rows // 2
-    column = (0, 4, 8, 12)
+    column = tuple(PLANE * i for i in range(PLANE))
     stack = jnp.stack([part] + [flipped(part, k) for k in column[1:]], axis=0)
     first, second = stack[:, :half], stack[:, half:]
     first_1, second_1 = flipped(first, 1), flipped(second, 2)
@@ -267,6 +290,16 @@
         shape((tiles, block_rows, LANES), BF),
         2 * keys * count * channels,
         2 * keys * channels + 2 * count * channels,
+        in_specs=[pl.BlockSpec(memory_space=pltpu.HBM)] * 5,
+        limit=62 * 1024 * 1024,
+        scratch=[
+            pltpu.VMEM((count, channels), BF),
+            pltpu.VMEM((1, count), jnp.int32),
+            pltpu.VMEM((1, count), jnp.int32),
+            pltpu.VMEM((1, count), jnp.int32),
+            pltpu.VMEM(inst_table.shape, BF),
+            pltpu.SemaphoreType.DMA((5,)),
+        ],
     )(
         observations,
         instrument.reshape(1, count),
@@ -275,7 +308,6 @@
         inst_table,
     )
     arrived = lax.all_to_all(payload, "tile", split_axis=0, concat_axis=0, tiled=True)
-    cot_all = lax.all_gather(cotangent, "tile", axis=0, tiled=True)
     marks = arrived[:, split * cap, :cap].reshape(1, keys).astype(F32)
 
     stream1, top, bottom = call(
@@ -303,13 +335,16 @@
     after = lax.ppermute(top, "tile", backward)
 
     part = hidden_width // tiles
-    direct = part == LANES
-    stream2, hidden, sliced = call(
+    me = lax.axis_index("tile").reshape(1)
+    scalar, whole = pl.BlockSpec(memory_space=pltpu.SMEM), pl.BlockSpec(memory_space=pltpu.VMEM)
+    fast = tiles == PLANE * PLANE
+    quarter = hidden_width // PLANE
+    stream2, hidden, *sliced = call(
         window_kernel,
         (
             shape((cells, width), F32),
             shape((cells, hidden_width), BF),
-            shape((tiles, cells, part) if direct else (1, 16, LANES + 1), BF),
+            *([shape((cells, quarter), BF)] * (PLANE if fast else 0)),
         ),
         2 * cells * width * (5 * width + hidden_width) + 8 * cells * cells * width,
         2 * width * (4 * width + hidden_width) + 4 * cells * hidden_width,
@@ -320,32 +355,57 @@
             pltpu.VMEM((cells, 2 * cells), F32),
             pltpu.VMEM((cells, width), BF),
         ],
+        in_specs=[scalar] + [whole] * 8,
         transcendentals=2 * H * cells * cells + cells * hidden_width,
-    )(stream1, before, top, bottom, after, w_win_qkv, w_win_out, w_up)
-    if not direct:
-        sliced = hidden.reshape(cells, tiles, part).transpose(1, 0, 2)
-    swapped = lax.all_to_all(sliced, "tile", split_axis=0, concat_axis=0, tiled=True)
+    )(me, stream1, before, top, bottom, after, w_win_qkv, w_win_out, w_up)
+    received = [flipped(sliced[j], j) for j in range(1, PLANE)] if fast else []
     latent_out = call(
         down_kernel,
         shape((cells, width), BF),
         2 * cells * width * hidden_width,
         2 * width * hidden_width + 2 * cells * hidden_width,
     )(stream2, hidden, w_down)
-    gradient = call(
-        gradient_kernel,
-        shape((part, width), BF),
-        2 * tiles * cells * part * width,
-        2 * tiles * cells * (part + width),
-    )(swapped.reshape(tiles * cells, part), cot_all)
-    pieces, order = gathered(gradient, "tile")
+    if fast:
+        late, _ = lax.optimization_barrier((cotangent, arrived))
+        cotangents = [cotangent] + [flipped(late, j) for j in range(1, PLANE)]
+        own, latent_out = lax.optimization_barrier((sliced[0], latent_out))
+        mine, *others = call(
+            plane_kernel,
+            (shape((part, width), F32), *([shape((part, width), BF)] * (PLANE - 1))),
+            2 * PLANE * cells * quarter * width,
+            2 * PLANE * cells * (quarter + width) + 2 * quarter * width,
+            scratch=[pltpu.VMEM((quarter, width), F32)],
+            in_specs=[scalar] + [whole] * (2 * PLANE),
+        )(me, own, *received, *cotangents)
+        for i, other in enumerate(others, 1):
+            mine = mine + flipped(other, PLANE * i).astype(F32)
+        pieces, order = gathered(mine.astype(BF))
+    else:
+        swapped = lax.all_to_all(
+            hidden.reshape(cells, tiles, part).transpose(1, 0, 2),
+            "tile",
+            split_axis=0,
+            concat_axis=0,
+            tiled=True,
+        )
+        gradient = call(
+            gradient_kernel,
+            shape((part, width), BF),
+            2 * tiles * cells * part * width,
+            2 * tiles * cells * (part + width),
+        )(
+            swapped.reshape(tiles * cells, part),
+            lax.all_gather(cotangent, "tile", axis=0, tiled=True),
+        )
+        pieces = [lax.all_gather(gradient, "tile", axis=0, tiled=True)[None]]
+        order = [[None]]
     clipped = call(
         functools.partial(clip_kernel, order=order),
         shape((hidden_width, width), F32),
         4 * hidden_width * width,
         6 * hidden_width * width,
-        in_specs=[pl.BlockSpec(memory_space=pltpu.SMEM)]
-        + [pl.BlockSpec(memory_space=pltpu.VMEM)] * len(pieces),
-    )(lax.axis_index("tile").reshape(1), *pieces)
+        in_specs=[scalar] + [whole] * len(pieces),
+    )(me, *pieces)
     return (latent_out, clipped)
 
 

time: 175 us -> 132 us (0.75)
  blocking collectives: 80.5 us -> 36.5 us
  between operations: 14.2 us -> 0.82 us
  starting transfers between devices: 14.2 us -> 25.8 us
  waiting for transfers between devices: 29.8 us -> 39.5 us
  local copies, waits for them, and re-layouts: 10.1 us -> 1.92 us
    all_to_all x1 -> x0, blocking collectives: 27.5 us -> none  [on_device(): lax.all_to_all(sliced, 'tile', split_axis=0, concat_axis=0, tiled=True)]
    ppermute x7 -> x16, waiting for transfers between devices: 21.2 us -> 39.3 us  [flipped(): lax.ppermute(value, 'tile', [(i, i ^ k) for i in range(PLANE * PLANE)])]
    all_to_all x1, blocking collectives: 53 us -> 36.5 us  [on_device(): lax.all_to_all(payload, 'tile', split_axis=0, concat_axis=0, tiled=True)]
    ppermute x7 -> x16, starting transfers between devices: 8.46 us -> 20.2 us  [flipped(): lax.ppermute(value, 'tile', [(i, i ^ k) for i in range(PLANE * PLANE)])]
    unnamed x34 -> x20, local copies, waits for them, and re-layouts: 10.1 us -> 1.88 us
    ppermute x1, waiting for transfers between devices: 5.73 us -> 0.01 us  [on_device(): before = lax.ppermute(bottom, 'tile', forward)]
    pallas_call x1, Pallas kernels: 1.7 us -> 3.78 us  [on_device(): call(functools.partial(pack_kernel, tiles=tiles, cap=cap), shape((tiles,...]
    ppermute x1, waiting for transfers between devices: 2.18 us -> 0.15 us  [on_device(): after = lax.ppermute(top, 'tile', backward)]
  transfers between devices with their start and end apart: 10 -> 18, of which waited for: 7 -> 10; matrix products, arithmetic and copies ran while one was open for 0% -> 0% of each run, Pallas kernels for 12% -> 6%
where the time goes in v2:
time: 132 us; the launch traced here: 131 us
  waiting for transfers between devices  39.5 us (30%)
  blocking collectives  36.5 us (28%)
  Pallas kernels  26.5 us (20%)
  starting transfers between devices  25.8 us (20%)
  local copies, waits for them, and re-layouts  1.92 us (1%)
    ppermute x16, waiting for transfers between devices, flipped(): lax.ppermute(value, 'tile', [(i, i ^ k) for i in range(PLANE * PLANE)])  39.3 us
    all_to_all x1, blocking collectives, on_device(): lax.all_to_all(payload, 'tile', split_axis=0, concat_axis=0, tiled=True)  36.5 us
    ppermute x16, starting transfers between devices, flipped(): lax.ppermute(value, 'tile', [(i, i ^ k) for i in range(PLANE * PLANE)])  20.2 us
    pallas_call x1, Pallas kernels, on_device(): call(functools.partial(cross_kernel, cap=cap), (shape((cells, width), F32...  11.1 us
    pallas_call x1, Pallas kernels, on_device(): call(window_kernel, (shape((cells, width), F32), shape((cells, hidden_wid...  6.78 us
    ppermute x1, starting transfers between devices, on_device(): after = lax.ppermute(top, 'tile', backward)  5.06 us
    pallas_call x1, Pallas kernels, on_device(): call(functools.partial(pack_kernel, tiles=tiles, cap=cap), shape((tiles,...  3.78 us
  transfers between devices with their start and end apart: 18, of which 10 were waited for; matrix products, arithmetic and copies ran while one was open for 0% of the time, Pallas kernels for 6%

profile of v2, /device:TPU:0, one launch (start us, length us, event | category | flops | bytes accessed | tf_op | source)
XLA Modules:
  0.0 131.3 jit_solution(11483872095619544943)
XLA Ops:
  0.6 3.8 %shard_map.149 = bf16[16,264,128]{2,1,0:T(8,128)(2,1)} custom-call(bf16[1024,256]{1,0:T(8,128)(2,1)} %refs_0_.1, s32[1,1024]{1,0:T(1,128)} %bitcast.17, s32[1,1024]{1,0:T(1,128)} %bitcast.18, s32[1,1024]{1,0:T(1,128)} %bitcast.19, bf16[32,256]{1,0:T(8,128)(2,1)} %refs_4_.2), custom_call_target="tpu_custom_call" | custom-call | flops 1073741824 | bytes 1572864 | tf_op jit(solution)/shard_map/pallas_call | solution.py:288
  4.5 36.5 %all_to_all.5.arrived = bf16[16,264,128]{2,1,0:T(8,128)(2,1)S(1)} all-to-all(bf16[16,264,128]{2,1,0:T(8,128)(2,1)} %shard_map.149), channel_id=1, replica_groups=mesh['tile'=16,'dp'=2] {'tile'}, dimensions={0} | all-to-all | bytes 2162688 | tf_op jit(solution)/shard_map/all_to_all | solution.py:310
  41.1 11.1 %shard_map.150 = (f32[256,512]{1,0:T(8,128)S(1)}, bf16[128,512]{1,0:T(8,128)(2,1)S(1)}, bf16[128,512]{1,0:T(8,128)(2,1)S(1)}) custom-call(bf16[16,264,128]{2,1,0:T(8,128)(2,1)S(1)} %all_to_all.5.arrived, f32[1,2048]{1,0:T(1,128)S(1)} %fusion.marks, bf16[256,512]{1,0:T(8,128)(2,1)S(1)} %copy-done.7, bf16[256,1024]{1,0:T(8,128)(2,1)S(1)} %copy-done.3, ...), custom_call_target="tpu_custom_call" | custom-call | flops 2147483648 | bytes 2621440 | tf_op jit(solution)/shard_map/pallas_call | solution.py:313
  53.5 5.1 %collective-permute-start.1 = (bf16[128,512]{1,0:T(8,128)(2,1)S(1)}, bf16[128,512]{1,0:T(8,128)(2,1)S(1)}, u32[]{:S(2)}, u32[]{:S(2)}) collective-permute-start(bf16[128,512]{1,0:T(8,128)(2,1)S(1)} %get-tuple-element.20.top), channel_id=1, source_target_pairs={{2,0},{4,2},{6,4},{8,6},{10,8},{12,10},{14,12},{16,14},{18,16},{20... | collective-permute-start | bytes 393224 | tf_op jit(solution)/shard_map/ppermute | solution.py:335
  58.6 3.5 %collective-permute-start.5 = (bf16[256,512]{1,0:T(8,128)(2,1)S(1)}, bf16[256,512]{1,0:T(8,128)(2,1)S(1)}, u32[]{:S(2)}, u32[]{:S(2)}) collective-permute-start(bf16[256,512]{1,0:T(8,128)(2,1)S(1)} %copy-done.1), channel_id=1, source_target_pairs={{0,2},{2,0},{4,6},{6,4},{8,10},{10,8},{12,14},{14,12},{16,18},{18,... | collective-permute-start | bytes 786440 | tf_op jit(solution)/shard_map/ppermute | solution.py:239
  62.2 1.0 copy-done.9
  63.3 6.8 %shard_map.151 = (f32[256,512]{1,0:T(8,128)S(1)}, bf16[256,2048]{1,0:T(8,128)(2,1)S(1)}, bf16[256,512]{1,0:T(8,128)(2,1)S(1)}, bf16[256,512]{1,0:T(8,128)(2,1)S(...) custom-call(s32[1]{0:T(128)} %bitcast.me, f32[256,512]{1,0:T(8,128)S(1)} %copy-done.9, ...), custom_call_target="tpu_custom_call" | custom-call | flops 1476395008 | bytes 6291456 | tf_op jit(solution)/shard_map/pallas_call | solution.py:342
  71.4 2.3 %collective-permute-start.4 = (bf16[256,512]{1,0:T(8,128)(2,1)S(1)}, bf16[256,512]{1,0:T(8,128)(2,1)S(1)}, u32[]{:S(2)}, u32[]{:S(2)}) collective-permute-start(bf16[256,512]{1,0:T(8,128)(2,1)S(1)} %get-tuple-element.28), channel_id=1, source_target_pairs={{0,6},{2,4},{4,2},{6,0},{8,14},{10,12},{12,10},{14,8},{16,22},{18,... | collective-permute-start | bytes 786440 | tf_op jit(solution)/shard_map/ppermute | solution.py:239
  73.6 1.4 %shard_map.152 = bf16[256,512]{1,0:T(8,128)(2,1)} custom-call(f32[256,512]{1,0:T(8,128)S(1)} %get-tuple-element.22.stream, bf16[256,2048]{1,0:T(8,128)(2,1)S(1)} %get-tuple-element.23.hidden, bf16[2048,512]{1,0:T(8,128)(2,1)S(1)} %copy-done), custom_call_target="tpu_custom_call" | custom-call | flops 536870912 | bytes 3145728 | tf_op jit(solution)/shard_map/pallas_call | solution.py:362
  75.0 4.3 %collective-permute-done.2.refs_1_ = bf16[256,512]{1,0:T(8,128)(2,1)S(1)} collective-permute-done((bf16[256,512]{1,0:T(8,128)(2,1)S(1)}, bf16[256,512]{1,0:T(8,128)(2,1)S(1)}, u32[]{:S(2)}, u32[]{:S(2)}) %collective-permute-start.2) | collective-permute-done | bytes 262176 | tf_op jit(solution)/shard_map/ppermute | solution.py:239
  79.4 4.8 %collective-permute-done.4.refs_3_ = bf16[256,512]{1,0:T(8,128)(2,1)S(1)} collective-permute-done((bf16[256,512]{1,0:T(8,128)(2,1)S(1)}, bf16[256,512]{1,0:T(8,128)(2,1)S(1)}, u32[]{:S(2)}, u32[]{:S(2)}) %collective-permute-start.4) | collective-permute-done | bytes 262176 | tf_op jit(solution)/shard_map/ppermute | solution.py:239
  85.2 2.5 %collective-permute-start.9 = (bf16[128,512]{1,0:T(8,128)(2,1)S(1)}, bf16[128,512]{1,0:T(8,128)(2,1)S(1)}, u32[]{:S(2)}, u32[]{:S(2)}) collective-permute-start(bf16[128,512]{1,0:T(8,128)(2,1)S(1)} %get-tuple-element.32), channel_id=1, source_target_pairs={{0,16},{2,18},{4,20},{6,22},{8,24},{10,26},{12,28},{14,30},{16,0},... | collective-permute-start | bytes 393224 | tf_op jit(solution)/shard_map/ppermute | solution.py:239
  87.7 1.7 %collective-permute-start.10 = (bf16[128,512]{1,0:T(8,128)(2,1)S(1)}, bf16[128,512]{1,0:T(8,128)(2,1)S(1)}, u32[]{:S(2)}, u32[]{:S(2)}) collective-permute-start(bf16[128,512]{1,0:T(8,128)(2,1)S(1)} %get-tuple-element.33), channel_id=1, source_target_pairs={{0,24},{2,26},{4,28},{6,30},{8,16},{10,18},{12,20},{14,22},{16,8},... | collective-permute-start | bytes 393224 | tf_op jit(solution)/shard_map/ppermute | solution.py:239
  89.4 1.4 %collective-permute-done.8 = bf16[128,512]{1,0:T(8,128)(2,1)S(1)} collective-permute-done((bf16[128,512]{1,0:T(8,128)(2,1)S(1)}, bf16[128,512]{1,0:T(8,128)(2,1)S(1)}, u32[]{:S(2)}, u32[]{:S(2)}) %collective-permute-start.8) | collective-permute-done | bytes 131104 | tf_op jit(solution)/shard_map/ppermute | solution.py:239
  90.8 6.7 %collective-permute-done.9 = bf16[128,512]{1,0:T(8,128)(2,1)S(1)} collective-permute-done((bf16[128,512]{1,0:T(8,128)(2,1)S(1)}, bf16[128,512]{1,0:T(8,128)(2,1)S(1)}, u32[]{:S(2)}, u32[]{:S(2)}) %collective-permute-start.9) | collective-permute-done | bytes 131104 | tf_op jit(solution)/shard_map/ppermute | solution.py:239
  97.6 2.0 %collective-permute-start.13 = (bf16[128,512]{1,0:T(8,128)(2,1)S(1)}, bf16[128,512]{1,0:T(8,128)(2,1)S(1)}, u32[]{:S(2)}, u32[]{:S(2)}) collective-permute-start(bf16[128,512]{1,0:T(8,128)(2,1)S(1)} %add_convert_fusion), channel_id=1, source_target_pairs={{0,24},{2,26},{4,28},{6,30},{8,16},{10,18},{12,20},{14,22},{16,8},... | collective-permute-start | bytes 393224 | tf_op jit(solution)/shard_map/ppermute | solution.py:239
  99.5 1.5 %collective-permute-start.12 = (bf16[128,512]{1,0:T(8,128)(2,1)S(1)}, bf16[128,512]{1,0:T(8,128)(2,1)S(1)}, u32[]{:S(2)}, u32[]{:S(2)}) collective-permute-start(bf16[128,512]{1,0:T(8,128)(2,1)S(1)} %add_convert_fusion), channel_id=1, source_target_pairs={{0,16},{2,18},{4,20},{6,22},{8,24},{10,26},{12,28},{14,30},{16,0},... | collective-permute-start | bytes 393224 | tf_op jit(solution)/shard_map/ppermute | solution.py:239
  102.0 3.6 %collective-permute-done.13 = bf16[128,512]{1,0:T(8,128)(2,1)S(1)} collective-permute-done((bf16[128,512]{1,0:T(8,128)(2,1)S(1)}, bf16[128,512]{1,0:T(8,128)(2,1)S(1)}, u32[]{:S(2)}, u32[]{:S(2)}) %collective-permute-start.13) | collective-permute-done | bytes 131104 | tf_op jit(solution)/shard_map/ppermute | solution.py:239
  105.7 5.1 %collective-permute-done.12 = bf16[128,512]{1,0:T(8,128)(2,1)S(1)} collective-permute-done((bf16[128,512]{1,0:T(8,128)(2,1)S(1)}, bf16[128,512]{1,0:T(8,128)(2,1)S(1)}, u32[]{:S(2)}, u32[]{:S(2)}) %collective-permute-start.12) | collective-permute-done | bytes 131104 | tf_op jit(solution)/shard_map/ppermute | solution.py:239
  110.9 1.4 %collective-permute-start.16 = (bf16[4,64,512]{2,1,0:T(8,128)(2,1)S(1)}, bf16[4,64,512]{2,1,0:T(8,128)(2,1)S(1)}, u32[]{:S(2)}, u32[]{:S(2)}) collective-permute-start(bf16[4,64,512]{2,1,0:T(8,128)(2,1)S(1)} %get-tuple-element.34), channel_id=1, source_target_pairs={{0,4},{2,6},{4,0},{6,2},{8,12},{10,14},{12,8},{14,10},{16,20},{18,... | collective-permute-start | bytes 786440 | tf_op jit(solution)/shard_map/ppermute | solution.py:239
  112.3 4.9 %collective-permute-done.14 = bf16[4,64,512]{2,1,0:T(8,128)(2,1)S(1)} collective-permute-done((bf16[4,64,512]{2,1,0:T(8,128)(2,1)S(1)}, bf16[4,64,512]{2,1,0:T(8,128)(2,1)S(1)}, u32[]{:S(2)}, u32[]{:S(2)}) %collective-permute-start.14) | collective-permute-done | bytes 262176 | tf_op jit(solution)/shard_map/ppermute | solution.py:239
  117.9 2.7 %collective-permute-start.17 = (bf16[8,64,512]{2,1,0:T(8,128)(2,1)S(1)}, bf16[8,64,512]{2,1,0:T(8,128)(2,1)S(1)}, u32[]{:S(2)}, u32[]{:S(2)}) collective-permute-start(bf16[8,64,512]{2,1,0:T(8,128)(2,1)S(1)} %pad_maximum_fusion.2.refs_2_), channel_id=1, source_target_pairs={{0,2},{2,0},{4,6},{6,4},{8,10},{10,8},{12,14},{14,12},{16,18},{18,... | collective-permute-start | bytes 1572872 | tf_op jit(solution)/shard_map/ppermute | solution.py:239
  120.6 8.0 %collective-permute-done.15.refs_1_ = bf16[8,64,512]{2,1,0:T(8,128)(2,1)S(1)} collective-permute-done((bf16[8,64,512]{2,1,0:T(8,128)(2,1)S(1)}, bf16[8,64,512]{2,1,0:T(8,128)(2,1)S(1)}, u32[]{:S(2)}, u32[]{:S(2)}) %collective-permute-start.15) | collective-permute-done | bytes 524320 | tf_op jit(solution)/shard_map/ppermute | solution.py:239
  128.7 2.6 %shard_map.154 = f32[2048,512]{1,0:T(8,128)} custom-call(s32[1]{0:T(128)} %bitcast.me, bf16[8,64,512]{2,1,0:T(8,128)(2,1)S(1)} %pad_maximum_fusion.1.refs_0_, bf16[8,64,512]{2,1,0:T(8,128)(2,1)S(1)} %collective-permute-done.15.refs_1_, bf16[8,64,512]{2,1,0:T(8,128)(2,1)S(1)} %pad_maximum_fusion.2.refs_2_, bf16[8,64,512]{2,1,0:T(8,128)(2,1)S(1)} %collective-permute-done.17.refs_3_), custom_call_target="tpu_custom_call" | custom-call | flops 4194304 | bytes 6291456 | tf_op jit(solution)/shard_map/pallas_call | solution.py:402
  (45 shorter events, 5.8 us)
Async XLA Ops:
  4.4 36.6 %copy-start.3 = (bf16[256,1024]{1,0:T(8,128)(2,1)S(1)}, bf16[256,1024]{1,0:T(8,128)(2,1)}, u32[]{:S(2)}) copy-start(bf16[256,1024]{1,0:T(8,128)(2,1)} %w_kv.1) | copy-start | bytes 1572868
  4.4 36.6 %copy-start.4 = (bf16[512,512]{1,0:T(8,128)(2,1)S(1)}, bf16[512,512]{1,0:T(8,128)(2,1)}, u32[]{:S(2)}) copy-start(bf16[512,512]{1,0:T(8,128)(2,1)} %w_q.1) | copy-start | bytes 1572868
  4.4 36.6 %copy-start.5 = (bf16[512,512]{1,0:T(8,128)(2,1)S(1)}, bf16[512,512]{1,0:T(8,128)(2,1)}, u32[]{:S(2)}) copy-start(bf16[512,512]{1,0:T(8,128)(2,1)} %w_out.2) | copy-start | bytes 1572868
  4.5 36.6 %copy-start.7 = (bf16[256,512]{1,0:T(8,128)(2,1)S(1)}, bf16[256,512]{1,0:T(8,128)(2,1)}, u32[]{:S(2)}) copy-start(bf16[256,512]{1,0:T(8,128)(2,1)} %latent.1) | copy-start | bytes 786436
  41.0 21.2 %copy-start.2 = (bf16[512,1536]{1,0:T(8,128)(2,1)S(1)}, bf16[512,1536]{1,0:T(8,128)(2,1)}, u32[]{:S(2)}) copy-start(bf16[512,1536]{1,0:T(8,128)(2,1)} %w_qkv.1) | copy-start | bytes 4718596
  41.0 21.2 %copy-start.6 = (bf16[512,512]{1,0:T(8,128)(2,1)S(1)}, bf16[512,512]{1,0:T(8,128)(2,1)}, u32[]{:S(2)}) copy-start(bf16[512,512]{1,0:T(8,128)(2,1)} %w_out.3) | copy-start | bytes 1572868
  53.0 9.1 %collective-permute-start = (bf16[128,512]{1,0:T(8,128)(2,1)S(1)}, bf16[128,512]{1,0:T(8,128)(2,1)S(1)}, u32[]{:S(2)}, u32[]{:S(2)}) collective-permute-start(bf16[128,512]{1,0:T(8,128)(2,1)S(1)} %get-tuple-element.19.bottom), channel_id=1, source_target_pairs={{0,2},{2,4},{4,6},{6,8},{8,10},{10,12},{12,14},{14,16},{16,18},{18... | collective-permute-start | bytes 393224 | tf_op jit(solution)/shard_map/ppermute | solution.py:334
  53.5 8.7 %collective-permute-start.1 = (bf16[128,512]{1,0:T(8,128)(2,1)S(1)}, bf16[128,512]{1,0:T(8,128)(2,1)S(1)}, u32[]{:S(2)}, u32[]{:S(2)}) collective-permute-start(bf16[128,512]{1,0:T(8,128)(2,1)S(1)} %get-tuple-element.20.top), channel_id=1, source_target_pairs={{2,0},{4,2},{6,4},{8,6},{10,8},{12,10},{14,12},{16,14},{18,16},{20... | collective-permute-start | bytes 393224 | tf_op jit(solution)/shard_map/ppermute | solution.py:335
  58.6 12.8 %collective-permute-start.7 = (bf16[256,512]{1,0:T(8,128)(2,1)S(1)}, bf16[256,512]{1,0:T(8,128)(2,1)S(1)}, u32[]{:S(2)}, u32[]{:S(2)}) collective-permute-start(bf16[256,512]{1,0:T(8,128)(2,1)S(1)} %copy-done.1), channel_id=1, source_target_pairs={{0,6},{2,4},{4,2},{6,0},{8,14},{10,12},{12,10},{14,8},{16,22},{18,... | collective-permute-start | bytes 786440 | tf_op jit(solution)/shard_map/ppermute | solution.py:239
  58.6 16.5 %collective-permute-start.6 = (bf16[256,512]{1,0:T(8,128)(2,1)S(1)}, bf16[256,512]{1,0:T(8,128)(2,1)S(1)}, u32[]{:S(2)}, u32[]{:S(2)}) collective-permute-start(bf16[256,512]{1,0:T(8,128)(2,1)S(1)} %copy-done.1), channel_id=1, source_target_pairs={{0,4},{2,6},{4,0},{6,2},{8,12},{10,14},{12,8},{14,10},{16,20},{18,... | collective-permute-start | bytes 786440 | tf_op jit(solution)/shard_map/ppermute | solution.py:239
  58.6 16.4 %collective-permute-start.5 = (bf16[256,512]{1,0:T(8,128)(2,1)S(1)}, bf16[256,512]{1,0:T(8,128)(2,1)S(1)}, u32[]{:S(2)}, u32[]{:S(2)}) collective-permute-start(bf16[256,512]{1,0:T(8,128)(2,1)S(1)} %copy-done.1), channel_id=1, source_target_pairs={{0,2},{2,0},{4,6},{6,4},{8,10},{10,8},{12,14},{14,12},{16,18},{18,... | collective-permute-start | bytes 786440 | tf_op jit(solution)/shard_map/ppermute | solution.py:239
  70.1 9.3 %collective-permute-start.2 = (bf16[256,512]{1,0:T(8,128)(2,1)S(1)}, bf16[256,512]{1,0:T(8,128)(2,1)S(1)}, u32[]{:S(2)}, u32[]{:S(2)}) collective-permute-start(bf16[256,512]{1,0:T(8,128)(2,1)S(1)} %get-tuple-element.26), channel_id=1, source_target_pairs={{0,2},{2,0},{4,6},{6,4},{8,10},{10,8},{12,14},{14,12},{16,18},{18,... | collective-permute-start | bytes 786440 | tf_op jit(solution)/shard_map/ppermute | solution.py:239
  70.6 8.8 %collective-permute-start.3 = (bf16[256,512]{1,0:T(8,128)(2,1)S(1)}, bf16[256,512]{1,0:T(8,128)(2,1)S(1)}, u32[]{:S(2)}, u32[]{:S(2)}) collective-permute-start(bf16[256,512]{1,0:T(8,128)(2,1)S(1)} %get-tuple-element.27), channel_id=1, source_target_pairs={{0,4},{2,6},{4,0},{6,2},{8,12},{10,14},{12,8},{14,10},{16,20},{18,... | collective-permute-start | bytes 786440 | tf_op jit(solution)/shard_map/ppermute | solution.py:239
  71.4 12.8 %collective-permute-start.4 = (bf16[256,512]{1,0:T(8,128)(2,1)S(1)}, bf16[256,512]{1,0:T(8,128)(2,1)S(1)}, u32[]{:S(2)}, u32[]{:S(2)}) collective-permute-start(bf16[256,512]{1,0:T(8,128)(2,1)S(1)} %get-tuple-element.28), channel_id=1, source_target_pairs={{0,6},{2,4},{4,2},{6,0},{8,14},{10,12},{12,10},{14,8},{16,22},{18,... | collective-permute-start | bytes 786440 | tf_op jit(solution)/shard_map/ppermute | solution.py:239
  84.9 5.8 %collective-permute-start.8 = (bf16[128,512]{1,0:T(8,128)(2,1)S(1)}, bf16[128,512]{1,0:T(8,128)(2,1)S(1)}, u32[]{:S(2)}, u32[]{:S(2)}) collective-permute-start(bf16[128,512]{1,0:T(8,128)(2,1)S(1)} %get-tuple-element.31), channel_id=1, source_target_pairs={{0,8},{2,10},{4,12},{6,14},{8,0},{10,2},{12,4},{14,6},{16,24},{18,... | collective-permute-start | bytes 393224 | tf_op jit(solution)/shard_map/ppermute | solution.py:239
  85.2 12.3 %collective-permute-start.9 = (bf16[128,512]{1,0:T(8,128)(2,1)S(1)}, bf16[128,512]{1,0:T(8,128)(2,1)S(1)}, u32[]{:S(2)}, u32[]{:S(2)}) collective-permute-start(bf16[128,512]{1,0:T(8,128)(2,1)S(1)} %get-tuple-element.32), channel_id=1, source_target_pairs={{0,16},{2,18},{4,20},{6,22},{8,24},{10,26},{12,28},{14,30},{16,0},... | collective-permute-start | bytes 393224 | tf_op jit(solution)/shard_map/ppermute | solution.py:239
  87.7 9.8 %collective-permute-start.10 = (bf16[128,512]{1,0:T(8,128)(2,1)S(1)}, bf16[128,512]{1,0:T(8,128)(2,1)S(1)}, u32[]{:S(2)}, u32[]{:S(2)}) collective-permute-start(bf16[128,512]{1,0:T(8,128)(2,1)S(1)} %get-tuple-element.33), channel_id=1, source_target_pairs={{0,24},{2,26},{4,28},{6,30},{8,16},{10,18},{12,20},{14,22},{16,8},... | collective-permute-start | bytes 393224 | tf_op jit(solution)/shard_map/ppermute | solution.py:239
  97.6 8.1 %collective-permute-start.13 = (bf16[128,512]{1,0:T(8,128)(2,1)S(1)}, bf16[128,512]{1,0:T(8,128)(2,1)S(1)}, u32[]{:S(2)}, u32[]{:S(2)}) collective-permute-start(bf16[128,512]{1,0:T(8,128)(2,1)S(1)} %add_convert_fusion), channel_id=1, source_target_pairs={{0,24},{2,26},{4,28},{6,30},{8,16},{10,18},{12,20},{14,22},{16,8},... | collective-permute-start | bytes 393224 | tf_op jit(solution)/shard_map/ppermute | solution.py:239
  99.5 11.2 %collective-permute-start.12 = (bf16[128,512]{1,0:T(8,128)(2,1)S(1)}, bf16[128,512]{1,0:T(8,128)(2,1)S(1)}, u32[]{:S(2)}, u32[]{:S(2)}) collective-permute-start(bf16[128,512]{1,0:T(8,128)(2,1)S(1)} %add_convert_fusion), channel_id=1, source_target_pairs={{0,16},{2,18},{4,20},{6,22},{8,24},{10,26},{12,28},{14,30},{16,0},... | collective-permute-start | bytes 393224 | tf_op jit(solution)/shard_map/ppermute | solution.py:239
  101.1 9.7 %collective-permute-start.11 = (bf16[128,512]{1,0:T(8,128)(2,1)S(1)}, bf16[128,512]{1,0:T(8,128)(2,1)S(1)}, u32[]{:S(2)}, u32[]{:S(2)}) collective-permute-start(bf16[128,512]{1,0:T(8,128)(2,1)S(1)} %add_convert_fusion), channel_id=1, source_target_pairs={{0,8},{2,10},{4,12},{6,14},{8,0},{10,2},{12,4},{14,6},{16,24},{18,... | collective-permute-start | bytes 393224 | tf_op jit(solution)/shard_map/ppermute | solution.py:239
  110.9 6.4 %collective-permute-start.14 = (bf16[4,64,512]{2,1,0:T(8,128)(2,1)S(1)}, bf16[4,64,512]{2,1,0:T(8,128)(2,1)S(1)}, u32[]{:S(2)}, u32[]{:S(2)}) collective-permute-start(bf16[4,64,512]{2,1,0:T(8,128)(2,1)S(1)} %get-tuple-element.35), channel_id=1, source_target_pairs={{0,2},{2,0},{4,6},{6,4},{8,10},{10,8},{12,14},{14,12},{16,18},{18,... | collective-permute-start | bytes 786440 | tf_op jit(solution)/shard_map/ppermute | solution.py:239
  110.9 6.9 %collective-permute-start.16 = (bf16[4,64,512]{2,1,0:T(8,128)(2,1)S(1)}, bf16[4,64,512]{2,1,0:T(8,128)(2,1)S(1)}, u32[]{:S(2)}, u32[]{:S(2)}) collective-permute-start(bf16[4,64,512]{2,1,0:T(8,128)(2,1)S(1)} %get-tuple-element.34), channel_id=1, source_target_pairs={{0,4},{2,6},{4,0},{6,2},{8,12},{10,14},{12,8},{14,10},{16,20},{18,... | collective-permute-start | bytes 786440 | tf_op jit(solution)/shard_map/ppermute | solution.py:239
  117.3 11.3 %collective-permute-start.15 = (bf16[8,64,512]{2,1,0:T(8,128)(2,1)S(1)}, bf16[8,64,512]{2,1,0:T(8,128)(2,1)S(1)}, u32[]{:S(2)}, u32[]{:S(2)}) collective-permute-start(bf16[8,64,512]{2,1,0:T(8,128)(2,1)S(1)} %pad_maximum_fusion.1.refs_0_), channel_id=1, source_target_pairs={{0,4},{2,6},{4,0},{6,2},{8,12},{10,14},{12,8},{14,10},{16,20},{18,... | collective-permute-start | bytes 1572872 | tf_op jit(solution)/shard_map/ppermute | solution.py:239
  117.9 10.7 %collective-permute-start.17 = (bf16[8,64,512]{2,1,0:T(8,128)(2,1)S(1)}, bf16[8,64,512]{2,1,0:T(8,128)(2,1)S(1)}, u32[]{:S(2)}, u32[]{:S(2)}) collective-permute-start(bf16[8,64,512]{2,1,0:T(8,128)(2,1)S(1)} %pad_maximum_fusion.2.refs_2_), channel_id=1, source_target_pairs={{0,2},{2,0},{4,6},{6,4},{8,10},{10,8},{12,14},{14,12},{16,18},{18,... | collective-permute-start | bytes 1572872 | tf_op jit(solution)/shard_map/ppermute | solution.py:239
  (4 other events, 29.7 us)

commit v3 on v2

v3 whole, which is shorter than its diff:
```python
import functools
import jax
import jax.numpy as jnp
from jax import lax
from jax.experimental import pallas as pl
from jax.experimental.pallas import tpu as pltpu
from jax.sharding import PartitionSpec as P

H = 8
LANES = 128
PLANE = 4
CHUNKS = 2
BF = jnp.bfloat16
F32 = jnp.float32
MIB = 1024 * 1024
NO_KEY = -1e30


def started(sources, targets, semaphores):
    copies = [
        pltpu.make_async_copy(source, target, semaphores.at[i])
        for i, (source, target) in enumerate(zip(sources, targets, strict=True))
    ]
    for copy in copies:
        copy.start()
    return copies


def dot(a, b, dims=((1,), (0,))):
    return lax.dot_general(a, b, (dims, ((), ())), preferred_element_type=F32)


def rms_norm(values):
    return values * lax.rsqrt(jnp.mean(values * values, axis=-1, keepdims=True) + 1e-06)


def iota(shape, dim):
    return lax.broadcasted_iota(jnp.int32, shape, dim)


SCALAR = pl.BlockSpec(memory_space=pltpu.SMEM)
WHOLE = pl.BlockSpec(memory_space=pltpu.VMEM)
FAR = pl.BlockSpec(memory_space=pltpu.HBM)


def call(kernel, out_shape, flops, moved, specs, scratch=(), transcendentals=0, *, limit):
    return pl.pallas_call(
        kernel,
        out_shape=out_shape,
        in_specs=specs,
        scratch_shapes=scratch,
        compiler_params=pltpu.CompilerParams(vmem_limit_bytes=limit * MIB),
        cost_estimate=pl.CostEstimate(
            flops=flops, bytes_accessed=moved, transcendentals=transcendentals
        ),
    )


def pack_kernel(*refs, tiles, cap):
    inputs, out, local, arrivals = refs[:5], refs[5], refs[6:11], refs[11]
    for copy in started(inputs, local, arrivals):
        copy.wait()
    obs, inst, route, cell, table = local
    rows, channels = obs.shape
    kinds = (iota((table.shape[0], rows), 0) == inst[...]).astype(F32).astype(BF)
    embedded = (obs[...].astype(F32) + dot(kinds, table[...], ((0,), (0,)))).astype(BF)
    chosen = (iota((tiles, rows), 0) == route[...]).astype(F32)
    pieces = rows // LANES
    stacked = jnp.concatenate(
        [chosen[:, i * LANES : (i + 1) * LANES] for i in range(pieces)], axis=0
    )
    upto = (iota((LANES, LANES), 0) <= iota((LANES, LANES), 1)).astype(F32).astype(BF)
    counted = dot(stacked.astype(BF), upto)
    base = jnp.zeros((tiles, 1), F32)
    parts = []
    for i in range(pieces):
        part = counted[i * tiles : (i + 1) * tiles]
        parts.append(part + base)
        base = base + part[:, LANES - 1 :]
    place = jnp.concatenate(parts, axis=1)
    rank = (jnp.sum(chosen * place, axis=0, keepdims=True) - 1.0).astype(jnp.int32)
    mark = chosen * (cell[...] + 1).astype(F32)
    at_rank = (iota((cap, rows), 0) == rank).astype(F32).astype(BF)
    marks = dot(mark.astype(BF), at_rank, ((1,), (1,)))
    slot = route[...] * cap + rank
    split = channels // LANES
    step = min(256, tiles * cap)
    if cap < LANES:
        marks = jnp.concatenate([marks, jnp.zeros((tiles, LANES - cap), F32)], axis=1)
    for first in range(0, tiles * cap, step):
        pick = (iota((step, rows), 0) + first == slot).astype(F32).astype(BF)
        moved = dot(pick, embedded).astype(BF)
        for i in range(step // cap):
            t = first // cap + i
            for c in range(split):
                out[t, c * cap : (c + 1) * cap, :] = moved[
                    i * cap : (i + 1) * cap, c * LANES : (c + 1) * LANES
                ]
            out[t, split * cap :, :] = jnp.broadcast_to(
                marks[t : t + 1, :], (out.shape[1] - split * cap, LANES)
            ).astype(BF)


def heads_pair(query, keys, values, add, earlier=None):
    low = iota(query.shape, 1) < query.shape[1] // 2
    zero = jnp.zeros_like(query)
    lanes = query.shape[1]
    with_ones = jnp.concatenate([values, jnp.ones_like(values)], axis=1)
    results = []
    for i, q in enumerate((jnp.where(low, query, zero), jnp.where(low, zero, query))):
        scores = dot(q, keys, ((1,), (1,))) + add
        peak = jnp.max(scores, axis=1, keepdims=True)
        if earlier is not None:
            at = i * (lanes // 2)
            peak = jnp.maximum(peak, earlier[0][:, at : at + 1])
        mixed = dot(jnp.exp(scores - peak).astype(BF), with_ones)
        results.append((jnp.broadcast_to(peak, query.shape), mixed[:, :lanes], mixed[:, lanes:]))
    peak, mixed, total = (jnp.where(low, a, b) for a, b in zip(*results, strict=True))
    if earlier is not None:
        weight = jnp.exp(earlier[0] - peak)
        mixed, total = mixed + weight * earlier[1], total + weight * earlier[2]
    return peak, mixed, total


def pairs(width, body):
    for at in range(0, width, LANES):
        body(slice(at, at + LANES), slice(width + at, width + at + LANES))


def project_query(normed, weights, width):
    scaled = dot(normed, weights).astype(BF).astype(F32) * (width // H) ** -0.5
    return scaled.astype(BF)


def unpack(blocks, x, cap):
    for s, block in enumerate(blocks):
        for c in range(x.shape[1] // LANES):
            x[s * cap : (s + 1) * cap, c * LANES : (c + 1) * LANES] = block[
                c * cap : (c + 1) * cap, :
            ]


def distance(mark, cells):
    positions = iota((cells, 1), 0).astype(F32)
    return jnp.where(mark > 0.5, -4.0 * jnp.abs(positions - (mark - 1.0)) / cells, NO_KEY)


def block_marks(blocks, row):
    return jnp.concatenate([block[row : row + 1, :] for block in blocks], axis=1).astype(F32)


def query_kernel(latent, w_q, q):
    normed = rms_norm(latent[...].astype(F32)).astype(BF)
    q[...] = project_query(normed, w_q[...], q.shape[1])


def cross_kernel(*refs, cap, inputs):
    (stream_out, top, bottom), refs, far = refs[inputs : inputs + 3], refs[inputs + 3 :], refs[:inputs]
    local, (x, kv, add, cross, arrivals) = refs[:inputs], refs[inputs:]
    copies = started(far, local, arrivals)
    arrived, w_kv, q, latent, w_out = local[:5]
    cells, width = latent.shape
    for i in (0, 1, *range(5, inputs)):
        copies[i].wait()
    blocks = [arrived.at[s] for s in range(arrived.shape[0])]
    unpack(blocks, x, cap)
    mark = local[5][...] if cap % LANES else block_marks(blocks, (x.shape[1] // LANES) * cap)
    kv[...] = dot(x[...], w_kv[...]).astype(BF)
    add[...] = distance(mark, cells)
    for i in (2, 3, 4):
        copies[i].wait()

    def body(at, beside):
        _, value, weight = heads_pair(q[:, at], kv[:, at], kv[:, beside], add[...])
        cross[:, at] = (value / weight).astype(BF)

    pairs(width, body)
    stream = latent[...].astype(F32) + dot(cross[...], w_out[...])
    stream_out[...] = stream
    normed = rms_norm(stream).astype(BF)
    top[...] = normed[: cells // 2]
    bottom[...] = normed[cells // 2 :]


def inner_kernel(top, bottom, w_qkv, q, peak, mixed, total, kv, own, add):
    cells, width = q.shape
    reach = cells // 2
    own[:reach, :] = top[...]
    own[reach:, :] = bottom[...]
    q[...] = project_query(own[...], w_qkv[:, :width], width)
    kv[...] = dot(own[...], w_qkv[:, width:]).astype(BF)
    offsets = iota(add.shape, 1) - iota(add.shape, 0)
    add[...] = jnp.where((offsets >= -reach) & (offsets <= reach), 0.0, NO_KEY)

    def body(at, beside):
        peak[:, at], mixed[:, at], total[:, at] = heads_pair(
            q[:, at], kv[:, at], kv[:, beside], add[...]
        )

    pairs(width, body)


def outer_kernel(
    stream_in, before, after, w_qkv, w_out, q, peak, mixed, total, stream_out, normed, kv, windowed
):
    cells, width = stream_in.shape
    reach = cells // 2
    kv[:reach, :] = dot(before[...], w_qkv[:, width:]).astype(BF)
    kv[reach:, :] = dot(after[...], w_qkv[:, width:]).astype(BF)
    offsets = iota((reach, reach), 1) - iota((reach, reach), 0)
    adds = [jnp.where(seen, 0.0, NO_KEY) for seen in (offsets >= 0, offsets <= 0)]

    def body(at, beside):
        for half in range(2):
            rows = slice(half * reach, (half + 1) * reach)
            _, value, weight = heads_pair(
                q[rows, at],
                kv[rows, at],
                kv[rows, beside],
                adds[half],
                (peak[rows, at], mixed[rows, at], total[rows, at]),
            )
            windowed[rows, at] = (value / weight).astype(BF)

    pairs(width, body)
    stream = stream_in[...] + dot(windowed[...], w_out[...])
    stream_out[...] = stream
    normed[...] = rms_norm(stream).astype(BF)


def up_kernel(me, normed, w_up, *outs, chunk):
    step = outs[0].shape[1]
    for j, out in enumerate(outs):
        first = ((me[0] % PLANE) ^ j) * (CHUNKS * step) + chunk * step
        at = pl.ds(pl.multiple_of(first, step), step)
        out[...] = jax.nn.gelu(dot(normed[...], w_up[:, at])).astype(BF)


def down_kernel(me, stream, w_down, *refs):
    hidden, out = refs[:-1], refs[-1]
    step = hidden[0].shape[1]
    total = stream[...]
    for i, block in enumerate(hidden):
        chunk, j = divmod(i, PLANE)
        first = ((me[0] % PLANE) ^ j) * (CHUNKS * step) + chunk * step
        total += dot(block[...], w_down[pl.ds(pl.multiple_of(first, step), step), :])
    out[...] = total.astype(BF)


def gradient_kernel(hidden, cotangent, out):
    out[...] = dot(hidden[...], cotangent[...], ((0,), (0,))).astype(BF)


def plane_kernel(me, *refs):
    hidden, cotangent, (own, other, total) = refs[:PLANE], refs[PLANE : 2 * PLANE], refs[2 * PLANE :]
    total[...] = sum(
        dot(h[...], c[...], ((0,), (0,))) for h, c in zip(hidden, cotangent, strict=True)
    )
    rows = own.shape[0]
    for i, out in enumerate((own, other)):
        at = pl.multiple_of(((me[0] // PLANE + i) % 2) * rows, rows)
        out[...] = total[pl.ds(at, rows), :].astype(out.dtype)


def clip_kernel(me, *refs, order, unit):
    pieces, out, sums = refs[:-2], refs[-2], refs[-1]
    quarter = out.shape[0] // PLANE
    where = []
    for piece, steps in zip(pieces, order, strict=True):
        for i, (flip, base, other) in enumerate(steps):
            tile = me[0] ^ flip
            half = (tile // PLANE + other) % 2
            where.append(((tile % PLANE) * quarter + base + half * unit, piece, i))
    for at, piece, i in where:
        v = piece[i].astype(F32)
        sums[pl.ds(at // unit, 1), :] = jnp.sum(v * v, axis=0, keepdims=True)
    total = jnp.sum(jnp.sum(sums[...], axis=0, keepdims=True), axis=1, keepdims=True)
    factor = jnp.minimum(1.0, 0.5 / jnp.sqrt(total / (out.shape[0] * out.shape[1]) + 1e-06))
    for at, piece, i in where:
        out[pl.ds(pl.multiple_of(at, unit), unit), :] = piece[i].astype(F32) * factor


def clip_whole_kernel(gradient, out):
    v = gradient[...].astype(F32)
    total = jnp.sum(jnp.sum(v * v, axis=0, keepdims=True), axis=1, keepdims=True)
    factor = jnp.minimum(1.0, 0.5 / jnp.sqrt(total / (out.shape[0] * out.shape[1]) + 1e-06))
    out[...] = v * factor


def flipped(value, k):
    return lax.ppermute(value, "tile", [(i, i ^ k) for i in range(PLANE * PLANE)])


def narrow(value):
    return value.astype(BF)


def reduced(own, other, base):
    own = narrow(own + flipped(other, PLANE).astype(F32))
    own = narrow(own.astype(F32) + flipped(own, 2 * PLANE).astype(F32))
    other = flipped(own, PLANE)
    own_x, other_y = flipped(own, 1), flipped(other, 2)
    own, other = jnp.stack([own, own_x]), jnp.stack([other, other_y])
    own_y, other_x = flipped(own, 2), flipped(other, 1)
    return [own, own_y, other, other_x], [
        [(0, base, 0), (1, base, 0)],
        [(2, base, 0), (3, base, 0)],
        [(0, base, 1), (2, base, 1)],
        [(1, base, 1), (3, base, 1)],
    ]


def on_device(
    observations,
    instrument,
    route,
    cell_index,
    latent,
    inst_table,
    w_obs_kv,
    w_cross_q,
    w_cross_out,
    w_win_qkv,
    w_win_out,
    w_up,
    w_down,
    cotangent,
):
    tiles = lax.axis_size("tile")
    count, channels = observations.shape
    cells, width = latent.shape
    hidden_width = w_up.shape[1]
    cap = 2 * count // tiles
    split = channels // LANES
    rows = split * cap + 8
    fast = tiles == PLANE * PLANE and cap == LANES
    me = lax.axis_index("tile").reshape(1) if fast else jnp.zeros((1,), jnp.int32)
    shape = jax.ShapeDtypeStruct
    stream_shape = shape((cells, width), F32)
    half_shape = shape((cells // 2, width), BF)
    query_shape = shape((cells, width), BF)

    packed = call(
        functools.partial(pack_kernel, tiles=tiles, cap=cap),
        shape((tiles, rows, LANES), BF),
        2 * tiles * cap * count * channels,
        2 * tiles * cap * channels + 2 * count * channels,
        [FAR] * 5,
        scratch=[
            pltpu.VMEM((count, channels), BF),
            pltpu.VMEM((1, count), jnp.int32),
            pltpu.VMEM((1, count), jnp.int32),
            pltpu.VMEM((1, count), jnp.int32),
            pltpu.VMEM(inst_table.shape, BF),
            pltpu.SemaphoreType.DMA((5,)),
        ],
        limit=62,
    )(
        observations,
        instrument.reshape(1, count),
        route.reshape(1, count),
        cell_index.reshape(1, count),
        inst_table,
    )

    keys = tiles * cap
    arrived = lax.all_to_all(packed, "tile", split_axis=0, concat_axis=0, tiled=True)
    if fast:
        cotangents = [flipped(cotangent, j) for j in range(1, PLANE)]
        arrived, *cotangents = lax.optimization_barrier((arrived, *cotangents))
        cotangents = [cotangent, *cotangents]
    query = call(
        query_kernel,
        query_shape,
        2 * cells * width * width,
        2 * width * width + 4 * cells * width,
        [WHOLE] * 2,
        limit=8,
    )(latent, w_cross_q)
    marks = [arrived[:, split * cap, :cap].reshape(1, keys).astype(F32)] if cap % LANES else []
    operands = (arrived, w_obs_kv, query, latent, w_cross_out, *marks)
    stream1, top, bottom = call(
        functools.partial(cross_kernel, cap=cap, inputs=len(operands)),
        (stream_shape, half_shape, half_shape),
        4 * keys * channels * width + 4 * cells * keys * width,
        2 * keys * channels + 6 * width * width,
        [FAR] * len(operands),
        scratch=[pltpu.VMEM(operand.shape, operand.dtype) for operand in operands]
        + [
            pltpu.VMEM((keys, channels), BF),
            pltpu.VMEM((keys, 2 * width), BF),
            pltpu.VMEM((cells, keys), F32),
            pltpu.VMEM((cells, width), BF),
            pltpu.SemaphoreType.DMA((len(operands),)),
        ],
        transcendentals=H * cells * keys,
        limit=62,
    )(*operands)

    forward = [(i, (i + 1) % tiles) for i in range(tiles)]
    backward = [(b, a) for a, b in forward]
    before = lax.ppermute(bottom, "tile", forward)
    after = lax.ppermute(top, "tile", backward)
    partial = call(
        inner_kernel,
        (query_shape, stream_shape, stream_shape, stream_shape),
        6 * cells * width * width + 4 * cells * cells * width,
        6 * width * width + 16 * cells * width,
        [WHOLE] * 3,
        scratch=[
            pltpu.VMEM((cells, 2 * width), BF),
            pltpu.VMEM((cells, width), BF),
            pltpu.VMEM((cells, cells), F32),
        ],
        transcendentals=H * cells * cells,
        limit=20,
    )(top, bottom, w_win_qkv)
    stream2, normed = call(
        outer_kernel,
        (stream_shape, query_shape),
        6 * cells * width * width + 2 * cells * cells * width,
        8 * width * width + 24 * cells * width,
        [WHOLE] * 9,
        scratch=[pltpu.VMEM((cells, 2 * width), BF), pltpu.VMEM((cells, width), BF)],
        transcendentals=H * cells * cells // 2,
        limit=20,
    )(stream1, before, after, w_win_qkv, w_win_out, *partial)

    step = hidden_width // (CHUNKS * PLANE)
    hidden = [
        call(
            functools.partial(up_kernel, chunk=c),
            [shape((cells, step), BF)] * PLANE,
            2 * cells * width * hidden_width // CHUNKS,
            2 * width * hidden_width // CHUNKS + 2 * cells * hidden_width // CHUNKS,
            [SCALAR, WHOLE, WHOLE],
            transcendentals=cells * hidden_width // CHUNKS,
            limit=12,
        )(me, normed, w_up)
        for c in range(CHUNKS)
    ]
    if fast:
        received = [[h[0]] + [flipped(h[j], j) for j in range(1, PLANE)] for h in hidden]
    latent_out = call(
        down_kernel,
        query_shape,
        2 * cells * width * hidden_width,
        2 * width * hidden_width + 2 * cells * hidden_width,
        [SCALAR] + [WHOLE] * (2 + CHUNKS * PLANE),
        limit=12,
    )(me, stream2, w_down, *[block for h in hidden for block in h])
    part = hidden_width // tiles
    if fast:
        received[0][0], latent_out = lax.optimization_barrier((received[0][0], latent_out))
        half = shape((step // 2, width), F32)
        pieces, order = [], []
        for c in range(CHUNKS):
            own, other = call(
                plane_kernel,
                (half, shape(half.shape, BF)),
                2 * PLANE * cells * step * width,
                2 * PLANE * cells * (step + width) + 2 * step * width,
                [SCALAR] + [WHOLE] * (2 * PLANE),
                scratch=[pltpu.VMEM((step, width), F32)],
                limit=12,
            )(me, *received[c], *cotangents)
            more, places = reduced(own, other, c * step)
            pieces, order = pieces + more, order + places
        clipped = call(
            functools.partial(clip_kernel, order=order, unit=step // 2),
            shape((hidden_width, width), F32),
            4 * hidden_width * width,
            6 * hidden_width * width,
            [SCALAR] + [WHOLE] * len(pieces),
            scratch=[pltpu.VMEM((2 * CHUNKS * PLANE, width), F32)],
            limit=24,
        )(me, *pieces)
    else:
        whole = jnp.concatenate([hidden[c][j] for j in range(PLANE) for c in range(CHUNKS)], 1)
        swapped = lax.all_to_all(
            whole.reshape(cells, tiles, part).transpose(1, 0, 2),
            "tile",
            split_axis=0,
            concat_axis=0,
            tiled=True,
        )
        gradient = call(
            gradient_kernel,
            shape((part, width), BF),
            2 * tiles * cells * part * width,
            2 * tiles * cells * (part + width),
            [WHOLE] * 2,
            limit=60,
        )(
            swapped.reshape(tiles * cells, part),
            lax.all_gather(cotangent, "tile", axis=0, tiled=True),
        )
        clipped = call(
            clip_whole_kernel,
            shape((hidden_width, width), F32),
            4 * hidden_width * width,
            6 * hidden_width * width,
            [WHOLE],
            limit=24,
        )(lax.all_gather(gradient, "tile", axis=0, tiled=True))
    return (latent_out, clipped)


def solution(mesh):
    split = P(("dp", "tile"))
    rows = P(("dp", "tile"), None)
    return jax.shard_map(
        on_device,
        mesh=mesh,
        in_specs=(rows, split, rows, split, rows, P(), P(), P(), P(), P(), P(), P(), P(), rows),
        out_specs=(rows, P("dp", None)),
        check_vma=False,
    )
```

time: 132 us -> 118 us (0.89)
  blocking collectives: 36.5 us -> 0 us
  starting transfers between devices: 25.8 us -> 44.4 us
  waiting for transfers between devices: 39.5 us -> 43.3 us
  local copies, waits for them, and re-layouts: 1.92 us -> 4.69 us
  Pallas kernels: 26.5 us -> 24.6 us
    all_to_all x1 -> x0, blocking collectives: 36.5 us -> none  [on_device(): lax.all_to_all(payload, 'tile', split_axis=0, concat_axis=0, tiled=True)]
    ppermute x16 -> x23, starting transfers between devices: 20.2 us -> 30.3 us  [flipped(): lax.ppermute(value, 'tile', [(i, i ^ k) for i in range(PLANE * PLANE)])]
    all_to_all x0 -> x1, starting transfers between devices: none -> 8.37 us  [on_device(): lax.all_to_all(packed, 'tile', split_axis=0, concat_axis=0, tiled=True)]
    ppermute x16 -> x23, waiting for transfers between devices: 39.3 us -> 43.3 us  [flipped(): lax.ppermute(value, 'tile', [(i, i ^ k) for i in range(PLANE * PLANE)])]
    unnamed x20 -> x34, local copies, waits for them, and re-layouts: 1.88 us -> 4.69 us
    pallas_call x5 -> x10, Pallas kernels: 22.7 us -> 20.7 us  [the longest x1 10.4 us: on_device(): call(functools.partial(cross_kernel, cap=cap, inputs=len(operands)), (str...]
  transfers between devices with their start and end apart: 18 -> 26, of which waited for: 10 -> 15; matrix products, arithmetic and copies ran while one was open for 0% -> 0% of each run, Pallas kernels for 6% -> 4%
where the time goes in v3:
time: 118 us
  starting transfers between devices  44.4 us (38%)
  waiting for transfers between devices  43.3 us (37%)
  Pallas kernels  24.6 us (21%)
  local copies, waits for them, and re-layouts  4.69 us (4%)
    ppermute x23, waiting for transfers between devices, flipped(): lax.ppermute(value, 'tile', [(i, i ^ k) for i in range(PLANE * PLANE)])  43.3 us
    ppermute x23, starting transfers between devices, flipped(): lax.ppermute(value, 'tile', [(i, i ^ k) for i in range(PLANE * PLANE)])  30.3 us
    pallas_call x1, Pallas kernels, on_device(): call(functools.partial(cross_kernel, cap=cap, inputs=len(operands)), (str...  10.4 us
    all_to_all x1, starting transfers between devices, on_device(): lax.all_to_all(packed, 'tile', split_axis=0, concat_axis=0, tiled=True)  8.37 us
    ppermute x1, starting transfers between devices, on_device(): after = lax.ppermute(top, 'tile', backward)  4.87 us
    unnamed x34, local copies, waits for them, and re-layouts  4.69 us
    pallas_call x1, Pallas kernels, on_device(): call(functools.partial(pack_kernel, tiles=tiles, cap=cap), shape((tiles,...  3.86 us
    pallas_call x1, Pallas kernels, on_device(): call(functools.partial(clip_kernel, order=order, unit=step // 2), shape((...  2.56 us
  transfers between devices with their start and end apart: 26, of which 15 were waited for; matrix products, arithmetic and copies ran while one was open for 0% of the time, Pallas kernels for 4%

profile of v3, /device:TPU:0, one launch (start us, length us, event | category | flops | bytes accessed | tf_op | source)
XLA Modules:
  0.0 118.1 jit_solution(13425584993170185539)
XLA Ops:
  0.7 3.9 %shard_map.149 = bf16[16,264,128]{2,1,0:T(8,128)(2,1)} custom-call(bf16[1024,256]{1,0:T(8,128)(2,1)} %refs_0_.1, s32[1,1024]{1,0:T(1,128)} %bitcast.20, s32[1,1024]{1,0:T(1,128)} %bitcast.21, s32[1,1024]{1,0:T(1,128)} %bitcast.22, bf16[32,256]{1,0:T(8,128)(2,1)} %refs_4_.4), custom_call_target="tpu_custom_call" | custom-call | flops 1073741824 | bytes 1572864 | tf_op jit(solution)/shard_map/pallas_call | solution.py:343
  4.5 8.4 %all-to-all-start = ((bf16[16,264,128]{2,1,0:T(8,128)(2,1)}), bf16[16,264,128]{2,1,0:T(8,128)(2,1)}, u32[]{:S(2)}, u32[]{:S(2)}) async-start(bf16[16,264,128]{2,1,0:T(8,128)(2,1)} %shard_map.149), calls=%async_computation | async-start | bytes 2162688 | tf_op jit(solution)/shard_map/all_to_all | solution.py:367
  12.9 2.8 %collective-permute-start.2 = (bf16[256,512]{1,0:T(8,128)(2,1)S(1)}, bf16[256,512]{1,0:T(8,128)(2,1)S(1)}, u32[]{:S(2)}, u32[]{:S(2)}) collective-permute-start(bf16[256,512]{1,0:T(8,128)(2,1)S(1)} %copy-done.3), channel_id=1, source_target_pairs={{0,6},{2,4},{4,2},{6,0},{8,14},{10,12},{12,10},{14,8},{16,22},{18,... | collective-permute-start | bytes 786440 | tf_op jit(solution)/shard_map/ppermute | solution.py:291
  17.6 15.4 %collective-permute-done.2.refs_7_ = bf16[256,512]{1,0:T(8,128)(2,1)S(1)} collective-permute-done((bf16[256,512]{1,0:T(8,128)(2,1)S(1)}, bf16[256,512]{1,0:T(8,128)(2,1)S(1)}, u32[]{:S(2)}, u32[]{:S(2)}) %collective-permute-start.2) | collective-permute-done | bytes 262176 | tf_op jit(solution)/shard_map/ppermute | solution.py:291
  33.7 4.4 %collective-permute-done.1.refs_6_ = bf16[256,512]{1,0:T(8,128)(2,1)S(1)} collective-permute-done((bf16[256,512]{1,0:T(8,128)(2,1)S(1)}, bf16[256,512]{1,0:T(8,128)(2,1)S(1)}, u32[]{:S(2)}, u32[]{:S(2)}) %collective-permute-start.1) | collective-permute-done | bytes 262176 | tf_op jit(solution)/shard_map/ppermute | solution.py:291
  40.0 10.4 %shard_map.151 = (f32[256,512]{1,0:T(8,128)}, bf16[128,512]{1,0:T(8,128)(2,1)}, bf16[128,512]{1,0:T(8,128)(2,1)}) custom-call(bf16[16,264,128]{2,1,0:T(8,128)(2,1)} %all-to-all-done.refs_0_, bf16[256,1024]{1,0:T(8,128)(2,1)} %refs_1_.1, bf16[256,512]{1,0:T(8,128)(2,1)} %copy-done.14, bf16[256,512]{1,0:T(8,128)(2,1)} %refs_3_.1, bf16[512,512]{1,0:T(8,128)(2,1)} %refs_4_.5), custom_call_target="tpu_custom_call" | custom-call | flops 2147483648 | bytes 2621440 | tf_op jit(solution)/shard_map/pallas_call | solution.py:382
  51.4 4.9 %collective-permute-start.4 = (bf16[128,512]{1,0:T(8,128)(2,1)}, bf16[128,512]{1,0:T(8,128)(2,1)S(1)}, u32[]{:S(2)}, u32[]{:S(2)}) collective-permute-start(bf16[128,512]{1,0:T(8,128)(2,1)} %get-tuple-element.32.top), channel_id=1, source_target_pairs={{2,0},{4,2},{6,4},{8,6},{10,8},{12,10},{14,12},{16,14},{18,16},{20... | collective-permute-start | bytes 393224 | tf_op jit(solution)/shard_map/ppermute | solution.py:403
  59.5 2.3 %shard_map.153 = (f32[256,512]{1,0:T(8,128)S(1)}, bf16[256,512]{1,0:T(8,128)(2,1)S(1)}) custom-call(f32[256,512]{1,0:T(8,128)S(1)} %copy-done.11, bf16[128,512]{1,0:T(8,128)(2,1)S(1)} %collective-permute-done.3.before, bf16[128,512]{1,0:T(8,128)(2,1)S(1)} %collective-permute-done.4.after, bf16[512,1536]{1,0:T(8,128)(2,1)S(1)} %copy-done.2, ...), custom_call_target="tpu_custom_call" | custom-call | flops 469762048 | bytes 5242880 | tf_op jit(solution)/shard_map/pallas_call | solution.py:418
  62.6 2.0 %collective-permute-start.6 = (bf16[256,256]{1,0:T(8,128)(2,1)S(1)}, bf16[256,256]{1,0:T(8,128)(2,1)S(1)}, u32[]{:S(2)}, u32[]{:S(2)}) collective-permute-start(bf16[256,256]{1,0:T(8,128)(2,1)S(1)} %get-tuple-element.41.refs_2_), channel_id=1, source_target_pairs={{0,4},{2,6},{4,0},{6,2},{8,12},{10,14},{12,8},{14,10},{16,20},{18,... | collective-permute-start | bytes 393224 | tf_op jit(solution)/shard_map/ppermute | solution.py:291
  64.6 1.4 %collective-permute-start.7 = (bf16[256,256]{1,0:T(8,128)(2,1)S(1)}, bf16[256,256]{1,0:T(8,128)(2,1)S(1)}, u32[]{:S(2)}, u32[]{:S(2)}) collective-permute-start(bf16[256,256]{1,0:T(8,128)(2,1)S(1)} %get-tuple-element.42.refs_3_), channel_id=1, source_target_pairs={{0,6},{2,4},{4,2},{6,0},{8,14},{10,12},{12,10},{14,8},{16,22},{18,... | collective-permute-start | bytes 393224 | tf_op jit(solution)/shard_map/ppermute | solution.py:291
  66.8 2.0 %collective-permute-start.16 = (bf16[256,256]{1,0:T(8,128)(2,1)S(1)}, bf16[256,256]{1,0:T(8,128)(2,1)S(1)}, u32[]{:S(2)}, u32[]{:S(2)}) collective-permute-start(bf16[256,256]{1,0:T(8,128)(2,1)S(1)} %get-tuple-element.45.refs_6_), channel_id=1, source_target_pairs={{0,4},{2,6},{4,0},{6,2},{8,12},{10,14},{12,8},{14,10},{16,20},{18,... | collective-permute-start | bytes 393224 | tf_op jit(solution)/shard_map/ppermute | solution.py:291
  68.8 1.4 %shard_map.156 = bf16[256,512]{1,0:T(8,128)(2,1)} custom-call(s32[1]{0:T(128)} %bitcast.me, f32[256,512]{1,0:T(8,128)S(1)} %get-tuple-element.39.stream, bf16[2048,512]{1,0:T(8,128)(2,1)S(1)} %copy-done.1, bf16[256,256]{1,0:T(8,128)(2,1)S(1)} %get-tuple-element.48.refs_0_, bf16[256,256]{1,0:T(8,128)(2,1)S(1)} %get-tuple-element.40.refs_1_, ...), custom_call_target="tpu_custom_call" | custom-call | flops 536870912 | bytes 3145728 | tf_op jit(solution)/shard_map/pallas_call | solution.py:444
  70.2 1.4 %collective-permute-start.17 = (bf16[256,256]{1,0:T(8,128)(2,1)S(1)}, bf16[256,256]{1,0:T(8,128)(2,1)S(1)}, u32[]{:S(2)}, u32[]{:S(2)}) collective-permute-start(bf16[256,256]{1,0:T(8,128)(2,1)S(1)} %get-tuple-element.46.refs_7_), channel_id=1, source_target_pairs={{0,6},{2,4},{4,2},{6,0},{8,14},{10,12},{12,10},{14,8},{16,22},{18,... | collective-permute-start | bytes 393224 | tf_op jit(solution)/shard_map/ppermute | solution.py:291
  74.0 2.1 %collective-permute-done.17.refs_3_ = bf16[256,256]{1,0:T(8,128)(2,1)S(1)} collective-permute-done((bf16[256,256]{1,0:T(8,128)(2,1)S(1)}, bf16[256,256]{1,0:T(8,128)(2,1)S(1)}, u32[]{:S(2)}, u32[]{:S(2)}) %collective-permute-start.17) | collective-permute-done | bytes 131104 | tf_op jit(solution)/shard_map/ppermute | solution.py:291
  76.6 1.4 %collective-permute-start.18 = (bf16[128,512]{1,0:T(8,128)(2,1)S(1)}, bf16[128,512]{1,0:T(8,128)(2,1)S(1)}, u32[]{:S(2)}, u32[]{:S(2)}) collective-permute-start(bf16[128,512]{1,0:T(8,128)(2,1)S(1)} %get-tuple-element.55), channel_id=1, source_target_pairs={{0,8},{2,10},{4,12},{6,14},{8,0},{10,2},{12,4},{14,6},{16,24},{18,... | collective-permute-start | bytes 393224 | tf_op jit(solution)/shard_map/ppermute | solution.py:291
  78.8 4.5 %collective-permute-start.9 = (bf16[128,512]{1,0:T(8,128)(2,1)S(1)}, bf16[128,512]{1,0:T(8,128)(2,1)S(1)}, u32[]{:S(2)}, u32[]{:S(2)}) collective-permute-start(bf16[128,512]{1,0:T(8,128)(2,1)S(1)} %add_convert_fusion.3), channel_id=1, source_target_pairs={{0,16},{2,18},{4,20},{6,22},{8,24},{10,26},{12,28},{14,30},{16,0},... | collective-permute-start | bytes 393224 | tf_op jit(solution)/shard_map/ppermute | solution.py:291
  83.3 1.9 %collective-permute-start.19 = (bf16[128,512]{1,0:T(8,128)(2,1)S(1)}, bf16[128,512]{1,0:T(8,128)(2,1)S(1)}, u32[]{:S(2)}, u32[]{:S(2)}) collective-permute-start(bf16[128,512]{1,0:T(8,128)(2,1)S(1)} %add_convert_fusion.1), channel_id=1, source_target_pairs={{0,16},{2,18},{4,20},{6,22},{8,24},{10,26},{12,28},{14,30},{16,0},... | collective-permute-start | bytes 393224 | tf_op jit(solution)/shard_map/ppermute | solution.py:291
  85.2 4.6 %collective-permute-done.9 = bf16[128,512]{1,0:T(8,128)(2,1)S(1)} collective-permute-done((bf16[128,512]{1,0:T(8,128)(2,1)S(1)}, bf16[128,512]{1,0:T(8,128)(2,1)S(1)}, u32[]{:S(2)}, u32[]{:S(2)}) %collective-permute-start.9) | collective-permute-done | bytes 131104 | tf_op jit(solution)/shard_map/ppermute | solution.py:291
  89.8 2.2 %collective-permute-start.12 = (bf16[128,512]{1,0:T(8,128)(2,1)S(1)}, bf16[128,512]{1,0:T(8,128)(2,1)S(1)}, u32[]{:S(2)}, u32[]{:S(2)}) collective-permute-start(bf16[128,512]{1,0:T(8,128)(2,1)S(1)} %add_convert_fusion.2), channel_id=1, source_target_pairs={{0,8},{2,10},{4,12},{6,14},{8,0},{10,2},{12,4},{14,6},{16,24},{18,... | collective-permute-start | bytes 393224 | tf_op jit(solution)/shard_map/ppermute | solution.py:291
  99.3 1.6 %collective-permute-start.21 = (bf16[2,128,512]{2,1,0:T(8,128)(2,1)S(1)}, bf16[2,128,512]{2,1,0:T(8,128)(2,1)S(1)}, u32[]{:S(2)}, u32[]{:S(2)}) collective-permute-start(bf16[2,128,512]{2,1,0:T(8,128)(2,1)S(1)} %pad_maximum_fusion.2.refs_4_), channel_id=1, source_target_pairs={{0,4},{2,6},{4,0},{6,2},{8,12},{10,14},{12,8},{14,10},{16,20},{18,... | collective-permute-start | bytes 786440 | tf_op jit(solution)/shard_map/ppermute | solution.py:291
  103.2 5.9 %collective-permute-done.23 = bf16[128,512]{1,0:T(8,128)(2,1)S(1)} collective-permute-done((bf16[128,512]{1,0:T(8,128)(2,1)S(1)}, bf16[128,512]{1,0:T(8,128)(2,1)S(1)}, u32[]{:S(2)}, u32[]{:S(2)}) %collective-permute-start.23) | collective-permute-done | bytes 131104 | tf_op jit(solution)/shard_map/ppermute | solution.py:291
  110.3 1.6 %collective-permute-done.21.refs_5_ = bf16[2,128,512]{2,1,0:T(8,128)(2,1)S(1)} collective-permute-done((bf16[2,128,512]{2,1,0:T(8,128)(2,1)S(1)}, bf16[2,128,512]{2,1,0:T(8,128)(2,1)S(1)}, u32[]{:S(2)}, u32[]{:S(2)}) %collective-permute-start.21) | collective-permute-done | bytes 262176 | tf_op jit(solution)/shard_map/ppermute | solution.py:291
  111.9 3.7 %collective-permute-done.24.refs_7_ = bf16[2,128,512]{2,1,0:T(8,128)(2,1)S(1)} collective-permute-done((bf16[2,128,512]{2,1,0:T(8,128)(2,1)S(1)}, bf16[2,128,512]{2,1,0:T(8,128)(2,1)S(1)}, u32[]{:S(2)}, u32[]{:S(2)}) %collective-permute-start.24) | collective-permute-done | bytes 262176 | tf_op jit(solution)/shard_map/ppermute | solution.py:291
  115.6 2.6 %shard_map.159 = f32[2048,512]{1,0:T(8,128)} custom-call(s32[1]{0:T(128)} %bitcast.me, bf16[2,128,512]{2,1,0:T(8,128)(2,1)S(1)} %pad_maximum_fusion.refs_0_, bf16[2,128,512]{2,1,0:T(8,128)(2,1)S(1)} %collective-permute-done.11.refs_1_, bf16[2,128,512]{2,1,0:T(8,128)(2,1)S(1)} %pad_maximum_fusion.1.refs_2_, ...), custom_call_target="tpu_custom_call" | custom-call | flops 4194304 | bytes 6291456 | tf_op jit(solution)/shard_map/pallas_call | solution.py:469
  (81 shorter events, 24.4 us)
Async XLA Ops:
  4.5 35.5 %all-to-all-start = ((bf16[16,264,128]{2,1,0:T(8,128)(2,1)}), bf16[16,264,128]{2,1,0:T(8,128)(2,1)}, u32[]{:S(2)}, u32[]{:S(2)}) async-start(bf16[16,264,128]{2,1,0:T(8,128)(2,1)} %shard_map.149), calls=%async_computation | async-start | bytes 2162688 | tf_op jit(solution)/shard_map/all_to_all | solution.py:367
  12.9 20.1 %collective-permute-start.2 = (bf16[256,512]{1,0:T(8,128)(2,1)S(1)}, bf16[256,512]{1,0:T(8,128)(2,1)S(1)}, u32[]{:S(2)}, u32[]{:S(2)}) collective-permute-start(bf16[256,512]{1,0:T(8,128)(2,1)S(1)} %copy-done.3), channel_id=1, source_target_pairs={{0,6},{2,4},{4,2},{6,0},{8,14},{10,12},{12,10},{14,8},{16,22},{18,... | collective-permute-start | bytes 786440 | tf_op jit(solution)/shard_map/ppermute | solution.py:291
  15.8 22.4 %collective-permute-start.1 = (bf16[256,512]{1,0:T(8,128)(2,1)S(1)}, bf16[256,512]{1,0:T(8,128)(2,1)S(1)}, u32[]{:S(2)}, u32[]{:S(2)}) collective-permute-start(bf16[256,512]{1,0:T(8,128)(2,1)S(1)} %copy-done.3), channel_id=1, source_target_pairs={{0,4},{2,6},{4,0},{6,2},{8,12},{10,14},{12,8},{14,10},{16,20},{18,... | collective-permute-start | bytes 786440 | tf_op jit(solution)/shard_map/ppermute | solution.py:291
  16.3 23.0 %collective-permute-start = (bf16[256,512]{1,0:T(8,128)(2,1)S(1)}, bf16[256,512]{1,0:T(8,128)(2,1)S(1)}, u32[]{:S(2)}, u32[]{:S(2)}) collective-permute-start(bf16[256,512]{1,0:T(8,128)(2,1)S(1)} %copy-done.3), channel_id=1, source_target_pairs={{0,2},{2,0},{4,6},{6,4},{8,10},{10,8},{12,14},{14,12},{16,18},{18,... | collective-permute-start | bytes 786440 | tf_op jit(solution)/shard_map/ppermute | solution.py:291
  50.5 9.0 %collective-permute-start.3 = (bf16[128,512]{1,0:T(8,128)(2,1)}, bf16[128,512]{1,0:T(8,128)(2,1)S(1)}, u32[]{:S(2)}, u32[]{:S(2)}) collective-permute-start(bf16[128,512]{1,0:T(8,128)(2,1)} %get-tuple-element.31.bottom), channel_id=1, source_target_pairs={{0,2},{2,4},{4,6},{6,8},{8,10},{10,12},{12,14},{14,16},{16,18},{18... | collective-permute-start | bytes 393224 | tf_op jit(solution)/shard_map/ppermute | solution.py:402
  51.4 8.1 %collective-permute-start.4 = (bf16[128,512]{1,0:T(8,128)(2,1)}, bf16[128,512]{1,0:T(8,128)(2,1)S(1)}, u32[]{:S(2)}, u32[]{:S(2)}) collective-permute-start(bf16[128,512]{1,0:T(8,128)(2,1)} %get-tuple-element.32.top), channel_id=1, source_target_pairs={{2,0},{4,2},{6,4},{8,6},{10,8},{12,10},{14,12},{16,14},{18,16},{20... | collective-permute-start | bytes 393224 | tf_op jit(solution)/shard_map/ppermute | solution.py:403
  62.5 7.7 %collective-permute-start.5 = (bf16[256,256]{1,0:T(8,128)(2,1)S(1)}, bf16[256,256]{1,0:T(8,128)(2,1)S(1)}, u32[]{:S(2)}, u32[]{:S(2)}) collective-permute-start(bf16[256,256]{1,0:T(8,128)(2,1)S(1)} %get-tuple-element.40.refs_1_), channel_id=1, source_target_pairs={{0,2},{2,0},{4,6},{6,4},{8,10},{10,8},{12,14},{14,12},{16,18},{18,... | collective-permute-start | bytes 393224 | tf_op jit(solution)/shard_map/ppermute | solution.py:291
  62.6 9.1 %collective-permute-start.6 = (bf16[256,256]{1,0:T(8,128)(2,1)S(1)}, bf16[256,256]{1,0:T(8,128)(2,1)S(1)}, u32[]{:S(2)}, u32[]{:S(2)}) collective-permute-start(bf16[256,256]{1,0:T(8,128)(2,1)S(1)} %get-tuple-element.41.refs_2_), channel_id=1, source_target_pairs={{0,4},{2,6},{4,0},{6,2},{8,12},{10,14},{12,8},{14,10},{16,20},{18,... | collective-permute-start | bytes 393224 | tf_op jit(solution)/shard_map/ppermute | solution.py:291
  64.6 7.3 %collective-permute-start.7 = (bf16[256,256]{1,0:T(8,128)(2,1)S(1)}, bf16[256,256]{1,0:T(8,128)(2,1)S(1)}, u32[]{:S(2)}, u32[]{:S(2)}) collective-permute-start(bf16[256,256]{1,0:T(8,128)(2,1)S(1)} %get-tuple-element.42.refs_3_), channel_id=1, source_target_pairs={{0,6},{2,4},{4,2},{6,0},{8,14},{10,12},{12,10},{14,8},{16,22},{18,... | collective-permute-start | bytes 393224 | tf_op jit(solution)/shard_map/ppermute | solution.py:291
  66.7 7.3 %collective-permute-start.15 = (bf16[256,256]{1,0:T(8,128)(2,1)S(1)}, bf16[256,256]{1,0:T(8,128)(2,1)S(1)}, u32[]{:S(2)}, u32[]{:S(2)}) collective-permute-start(bf16[256,256]{1,0:T(8,128)(2,1)S(1)} %get-tuple-element.44.refs_5_), channel_id=1, source_target_pairs={{0,2},{2,0},{4,6},{6,4},{8,10},{10,8},{12,14},{14,12},{16,18},{18,... | collective-permute-start | bytes 393224 | tf_op jit(solution)/shard_map/ppermute | solution.py:291
  66.8 7.2 %collective-permute-start.16 = (bf16[256,256]{1,0:T(8,128)(2,1)S(1)}, bf16[256,256]{1,0:T(8,128)(2,1)S(1)}, u32[]{:S(2)}, u32[]{:S(2)}) collective-permute-start(bf16[256,256]{1,0:T(8,128)(2,1)S(1)} %get-tuple-element.45.refs_6_), channel_id=1, source_target_pairs={{0,4},{2,6},{4,0},{6,2},{8,12},{10,14},{12,8},{14,10},{16,20},{18,... | collective-permute-start | bytes 393224 | tf_op jit(solution)/shard_map/ppermute | solution.py:291
  70.2 5.9 %collective-permute-start.17 = (bf16[256,256]{1,0:T(8,128)(2,1)S(1)}, bf16[256,256]{1,0:T(8,128)(2,1)S(1)}, u32[]{:S(2)}, u32[]{:S(2)}) collective-permute-start(bf16[256,256]{1,0:T(8,128)(2,1)S(1)} %get-tuple-element.46.refs_7_), channel_id=1, source_target_pairs={{0,6},{2,4},{4,2},{6,0},{8,14},{10,12},{12,10},{14,8},{16,22},{18,... | collective-permute-start | bytes 393224 | tf_op jit(solution)/shard_map/ppermute | solution.py:291
  72.4 6.4 %collective-permute-start.8 = (bf16[128,512]{1,0:T(8,128)(2,1)S(1)}, bf16[128,512]{1,0:T(8,128)(2,1)S(1)}, u32[]{:S(2)}, u32[]{:S(2)}) collective-permute-start(bf16[128,512]{1,0:T(8,128)(2,1)S(1)} %get-tuple-element.53), channel_id=1, source_target_pairs={{0,8},{2,10},{4,12},{6,14},{8,0},{10,2},{12,4},{14,6},{16,24},{18,... | collective-permute-start | bytes 393224 | tf_op jit(solution)/shard_map/ppermute | solution.py:291
  76.6 6.7 %collective-permute-start.18 = (bf16[128,512]{1,0:T(8,128)(2,1)S(1)}, bf16[128,512]{1,0:T(8,128)(2,1)S(1)}, u32[]{:S(2)}, u32[]{:S(2)}) collective-permute-start(bf16[128,512]{1,0:T(8,128)(2,1)S(1)} %get-tuple-element.55), channel_id=1, source_target_pairs={{0,8},{2,10},{4,12},{6,14},{8,0},{10,2},{12,4},{14,6},{16,24},{18,... | collective-permute-start | bytes 393224 | tf_op jit(solution)/shard_map/ppermute | solution.py:291
  78.8 11.0 %collective-permute-start.9 = (bf16[128,512]{1,0:T(8,128)(2,1)S(1)}, bf16[128,512]{1,0:T(8,128)(2,1)S(1)}, u32[]{:S(2)}, u32[]{:S(2)}) collective-permute-start(bf16[128,512]{1,0:T(8,128)(2,1)S(1)} %add_convert_fusion.3), channel_id=1, source_target_pairs={{0,16},{2,18},{4,20},{6,22},{8,24},{10,26},{12,28},{14,30},{16,0},... | collective-permute-start | bytes 393224 | tf_op jit(solution)/shard_map/ppermute | solution.py:291
  83.3 9.6 %collective-permute-start.19 = (bf16[128,512]{1,0:T(8,128)(2,1)S(1)}, bf16[128,512]{1,0:T(8,128)(2,1)S(1)}, u32[]{:S(2)}, u32[]{:S(2)}) collective-permute-start(bf16[128,512]{1,0:T(8,128)(2,1)S(1)} %add_convert_fusion.1), channel_id=1, source_target_pairs={{0,16},{2,18},{4,20},{6,22},{8,24},{10,26},{12,28},{14,30},{16,0},... | collective-permute-start | bytes 393224 | tf_op jit(solution)/shard_map/ppermute | solution.py:291
  89.8 5.9 %collective-permute-start.12 = (bf16[128,512]{1,0:T(8,128)(2,1)S(1)}, bf16[128,512]{1,0:T(8,128)(2,1)S(1)}, u32[]{:S(2)}, u32[]{:S(2)}) collective-permute-start(bf16[128,512]{1,0:T(8,128)(2,1)S(1)} %add_convert_fusion.2), channel_id=1, source_target_pairs={{0,8},{2,10},{4,12},{6,14},{8,0},{10,2},{12,4},{14,6},{16,24},{18,... | collective-permute-start | bytes 393224 | tf_op jit(solution)/shard_map/ppermute | solution.py:291
  93.4 5.9 %collective-permute-start.20 = (bf16[128,512]{1,0:T(8,128)(2,1)S(1)}, bf16[128,512]{1,0:T(8,128)(2,1)S(1)}, u32[]{:S(2)}, u32[]{:S(2)}) collective-permute-start(bf16[128,512]{1,0:T(8,128)(2,1)S(1)} %add_convert_fusion), channel_id=1, source_target_pairs={{0,2},{2,0},{4,6},{6,4},{8,10},{10,8},{12,14},{14,12},{16,18},{18,... | collective-permute-start | bytes 393224 | tf_op jit(solution)/shard_map/ppermute | solution.py:291
  95.7 6.4 %collective-permute-start.13 = (bf16[128,512]{1,0:T(8,128)(2,1)S(1)}, bf16[128,512]{1,0:T(8,128)(2,1)S(1)}, u32[]{:S(2)}, u32[]{:S(2)}) collective-permute-start(bf16[128,512]{1,0:T(8,128)(2,1)S(1)} %collective-permute-done.12), channel_id=1, source_target_pairs={{0,4},{2,6},{4,0},{6,2},{8,12},{10,14},{12,8},{14,10},{16,20},{18,... | collective-permute-start | bytes 393224 | tf_op jit(solution)/shard_map/ppermute | solution.py:291
  97.2 13.1 %collective-permute-start.11 = (bf16[2,128,512]{2,1,0:T(8,128)(2,1)S(1)}, bf16[2,128,512]{2,1,0:T(8,128)(2,1)S(1)}, u32[]{:S(2)}, u32[]{:S(2)}) collective-permute-start(bf16[2,128,512]{2,1,0:T(8,128)(2,1)S(1)} %pad_maximum_fusion.refs_0_), channel_id=1, source_target_pairs={{0,4},{2,6},{4,0},{6,2},{8,12},{10,14},{12,8},{14,10},{16,20},{18,... | collective-permute-start | bytes 786440 | tf_op jit(solution)/shard_map/ppermute | solution.py:291
  98.0 11.1 %collective-permute-start.23 = (bf16[128,512]{1,0:T(8,128)(2,1)S(1)}, bf16[128,512]{1,0:T(8,128)(2,1)S(1)}, u32[]{:S(2)}, u32[]{:S(2)}) collective-permute-start(bf16[128,512]{1,0:T(8,128)(2,1)S(1)} %collective-permute-done.22), channel_id=1, source_target_pairs={{0,4},{2,6},{4,0},{6,2},{8,12},{10,14},{12,8},{14,10},{16,20},{18,... | collective-permute-start | bytes 393224 | tf_op jit(solution)/shard_map/ppermute | solution.py:291
  99.3 12.6 %collective-permute-start.21 = (bf16[2,128,512]{2,1,0:T(8,128)(2,1)S(1)}, bf16[2,128,512]{2,1,0:T(8,128)(2,1)S(1)}, u32[]{:S(2)}, u32[]{:S(2)}) collective-permute-start(bf16[2,128,512]{2,1,0:T(8,128)(2,1)S(1)} %pad_maximum_fusion.2.refs_4_), channel_id=1, source_target_pairs={{0,4},{2,6},{4,0},{6,2},{8,12},{10,14},{12,8},{14,10},{16,20},{18,... | collective-permute-start | bytes 786440 | tf_op jit(solution)/shard_map/ppermute | solution.py:291
  102.2 9.7 %collective-permute-start.14 = (bf16[2,128,512]{2,1,0:T(8,128)(2,1)S(1)}, bf16[2,128,512]{2,1,0:T(8,128)(2,1)S(1)}, u32[]{:S(2)}, u32[]{:S(2)}) collective-permute-start(bf16[2,128,512]{2,1,0:T(8,128)(2,1)S(1)} %pad_maximum_fusion.1.refs_2_), channel_id=1, source_target_pairs={{0,2},{2,0},{4,6},{6,4},{8,10},{10,8},{12,14},{14,12},{16,18},{18,... | collective-permute-start | bytes 786440 | tf_op jit(solution)/shard_map/ppermute | solution.py:291
  109.1 6.4 %collective-permute-start.24 = (bf16[2,128,512]{2,1,0:T(8,128)(2,1)S(1)}, bf16[2,128,512]{2,1,0:T(8,128)(2,1)S(1)}, u32[]{:S(2)}, u32[]{:S(2)}) collective-permute-start(bf16[2,128,512]{2,1,0:T(8,128)(2,1)S(1)} %pad_maximum_fusion.3.refs_6_), channel_id=1, source_target_pairs={{0,2},{2,0},{4,6},{6,4},{8,10},{10,8},{12,14},{14,12},{16,18},{18,... | collective-permute-start | bytes 786440 | tf_op jit(solution)/shard_map/ppermute | solution.py:291
  (19 other events, 132.9 us)

commit v4 on v3

--- a/solution.py
+++ b/solution.py
@@ -10,6 +10,7 @@
 LANES = 128
 PLANE = 4
 CHUNKS = 2
+DIRECT = (1,)
 BF = jnp.bfloat16
 F32 = jnp.float32
 MIB = 1024 * 1024
@@ -43,10 +44,12 @@
 FAR = pl.BlockSpec(memory_space=pltpu.HBM)
 
 
-def call(kernel, out_shape, flops, moved, specs, scratch=(), transcendentals=0, *, limit):
+def call(kernel, out_shape, flops, moved, specs, scratch=(), transcendentals=0, out_spec=None, *, limit):
+    kwargs = {} if out_spec is None else {"out_specs": out_spec}
     return pl.pallas_call(
         kernel,
         out_shape=out_shape,
+        **kwargs,
         in_specs=specs,
         scratch_shapes=scratch,
         compiler_params=pltpu.CompilerParams(vmem_limit_bytes=limit * MIB),
@@ -263,7 +266,7 @@
 
 
 def clip_kernel(me, *refs, order, unit):
-    pieces, out, sums = refs[:-2], refs[-2], refs[-1]
+    pieces, (out, sums, scaled, sent) = refs[:-4], refs[-4:]
     quarter = out.shape[0] // PLANE
     where = []
     for piece, steps in zip(pieces, order, strict=True):
@@ -276,8 +279,14 @@
         sums[pl.ds(at // unit, 1), :] = jnp.sum(v * v, axis=0, keepdims=True)
     total = jnp.sum(jnp.sum(sums[...], axis=0, keepdims=True), axis=1, keepdims=True)
     factor = jnp.minimum(1.0, 0.5 / jnp.sqrt(total / (out.shape[0] * out.shape[1]) + 1e-06))
-    for at, piece, i in where:
-        out[pl.ds(pl.multiple_of(at, unit), unit), :] = piece[i].astype(F32) * factor
+    copies = []
+    for n, (at, piece, i) in enumerate(where):
+        scaled[n] = piece[i].astype(F32) * factor
+        rows = pl.ds(pl.multiple_of(at, unit), unit)
+        copies.append(pltpu.make_async_copy(scaled.at[n], out.at[rows, :], sent.at[n]))
+        copies[-1].start()
+    for copy in copies:
+        copy.wait()
 
 
 def clip_whole_kernel(gradient, out):
@@ -295,19 +304,33 @@
     return value.astype(BF)
 
 
-def reduced(own, other, base):
+def reduced(own, other, base, wait_for, direct):
     own = narrow(own + flipped(other, PLANE).astype(F32))
-    own = narrow(own.astype(F32) + flipped(own, 2 * PLANE).astype(F32))
+    across = flipped(own, 2 * PLANE)
+    own = narrow(own.astype(F32) + across.astype(F32))
+    if direct:
+        owns = [own] + [flipped(own, j) for j in range(1, PLANE)]
+        other = flipped(own, PLANE)
+        others = [other] + [flipped(other, j) for j in range(1, PLANE)]
+        return (
+            [across],
+            [half[None] for half in owns + others],
+            [[(j, base, n)] for n in range(2) for j in range(PLANE)],
+        )
     other = flipped(own, PLANE)
     own_x, other_y = flipped(own, 1), flipped(other, 2)
     own, other = jnp.stack([own, own_x]), jnp.stack([other, other_y])
     own_y, other_x = flipped(own, 2), flipped(other, 1)
-    return [own, own_y, other, other_x], [
-        [(0, base, 0), (1, base, 0)],
-        [(2, base, 0), (3, base, 0)],
-        [(0, base, 1), (2, base, 1)],
-        [(1, base, 1), (3, base, 1)],
-    ]
+    return (
+        [across],
+        [own, own_y, other, other_x],
+        [
+            [(0, base, 0), (1, base, 0)],
+            [(2, base, 0), (3, base, 0)],
+            [(0, base, 1), (2, base, 1)],
+            [(1, base, 1), (3, base, 1)],
+        ],
+    )
 
 
 def on_device(
@@ -441,19 +464,11 @@
     ]
     if fast:
         received = [[h[0]] + [flipped(h[j], j) for j in range(1, PLANE)] for h in hidden]
-    latent_out = call(
-        down_kernel,
-        query_shape,
-        2 * cells * width * hidden_width,
-        2 * width * hidden_width + 2 * cells * hidden_width,
-        [SCALAR] + [WHOLE] * (2 + CHUNKS * PLANE),
-        limit=12,
-    )(me, stream2, w_down, *[block for h in hidden for block in h])
     part = hidden_width // tiles
     if fast:
-        received[0][0], latent_out = lax.optimization_barrier((received[0][0], latent_out))
+        received[0][0], received[1][0] = lax.optimization_barrier((received[0][0], received[1][0]))
         half = shape((step // 2, width), F32)
-        pieces, order = [], []
+        last, pieces, order = [], [], []
         for c in range(CHUNKS):
             own, other = call(
                 plane_kernel,
@@ -464,7 +479,9 @@
                 scratch=[pltpu.VMEM((step, width), F32)],
                 limit=12,
             )(me, *received[c], *cotangents)
-            more, places = reduced(own, other, c * step)
+            if c == 0:
+                stream2, own = lax.optimization_barrier((stream2, own))
+            last, more, places = reduced(own, other, c * step, last, c in DIRECT)
             pieces, order = pieces + more, order + places
         clipped = call(
             functools.partial(clip_kernel, order=order, unit=step // 2),
@@ -472,7 +489,12 @@
             4 * hidden_width * width,
             6 * hidden_width * width,
             [SCALAR] + [WHOLE] * len(pieces),
-            scratch=[pltpu.VMEM((2 * CHUNKS * PLANE, width), F32)],
+            scratch=[
+                pltpu.VMEM((2 * CHUNKS * PLANE, width), F32),
+                pltpu.VMEM((2 * CHUNKS * PLANE, step // 2, width), F32),
+                pltpu.SemaphoreType.DMA((2 * CHUNKS * PLANE,)),
+            ],
+            out_spec=FAR,
             limit=24,
         )(me, *pieces)
     else:
@@ -503,6 +525,14 @@
             [WHOLE],
             limit=24,
         )(lax.all_gather(gradient, "tile", axis=0, tiled=True))
+    latent_out = call(
+        down_kernel,
+        query_shape,
+        2 * cells * width * hidden_width,
+        2 * width * hidden_width + 2 * cells * hidden_width,
+        [SCALAR] + [WHOLE] * (2 + CHUNKS * PLANE),
+        limit=12,
+    )(me, stream2, w_down, *[block for h in hidden for block in h])
     return (latent_out, clipped)
 
 

time: 118 us -> 114 us (0.966)
  waiting for transfers between devices: 43.3 us -> 32.6 us
  starting transfers between devices: 44.4 us -> 51 us
    ppermute x23 -> x25, waiting for transfers between devices: 43.3 us -> 32.6 us  [flipped(): lax.ppermute(value, 'tile', [(i, i ^ k) for i in range(PLANE * PLANE)])]
    ppermute x23 -> x25, starting transfers between devices: 30.3 us -> 36.9 us  [flipped(): lax.ppermute(value, 'tile', [(i, i ^ k) for i in range(PLANE * PLANE)])]
  transfers between devices with their start and end apart: 26 -> 28, of which waited for: 15 -> 13; matrix products, arithmetic and copies ran while one was open for 0% -> 0% of each run, Pallas kernels for 4% -> 4%
where the time goes in v4:
time: 114 us
  starting transfers between devices  51 us (45%)
  waiting for transfers between devices  32.6 us (29%)
  Pallas kernels  24.4 us (21%)
  local copies, waits for them, and re-layouts  4.7 us (4%)
    ppermute x25, starting transfers between devices, flipped(): lax.ppermute(value, 'tile', [(i, i ^ k) for i in range(PLANE * PLANE)])  36.9 us
    ppermute x25, waiting for transfers between devices, flipped(): lax.ppermute(value, 'tile', [(i, i ^ k) for i in range(PLANE * PLANE)])  32.6 us
    pallas_call x1, Pallas kernels, on_device(): call(functools.partial(cross_kernel, cap=cap, inputs=len(operands)), (str...  10.4 us
    all_to_all x1, starting transfers between devices, on_device(): lax.all_to_all(packed, 'tile', split_axis=0, concat_axis=0, tiled=True)  8.37 us
    ppermute x1, starting transfers between devices, on_device(): after = lax.ppermute(top, 'tile', backward)  4.87 us
    unnamed x34, local copies, waits for them, and re-layouts  4.7 us
    pallas_call x1, Pallas kernels, on_device(): call(functools.partial(pack_kernel, tiles=tiles, cap=cap), shape((tiles,...  3.86 us
    pallas_call x1, Pallas kernels, on_device(): call(functools.partial(clip_kernel, order=order, unit=step // 2), shape((...  2.43 us
  transfers between devices with their start and end apart: 28, of which 13 were waited for; matrix products, arithmetic and copies ran while one was open for 0% of the time, Pallas kernels for 4%

profile of v4, /device:TPU:0, one launch (start us, length us, event | category | flops | bytes accessed | tf_op | source)
XLA Modules:
  0.0 114.0 jit_solution(15465114837557438899)
XLA Ops:
  0.7 3.9 %shard_map.149 = bf16[16,264,128]{2,1,0:T(8,128)(2,1)} custom-call(bf16[1024,256]{1,0:T(8,128)(2,1)} %refs_0_.1, s32[1,1024]{1,0:T(1,128)} %bitcast.28, s32[1,1024]{1,0:T(1,128)} %bitcast.29, s32[1,1024]{1,0:T(1,128)} %bitcast.30, bf16[32,256]{1,0:T(8,128)(2,1)} %refs_4_.4), custom_call_target="tpu_custom_call" | custom-call | flops 1073741824 | bytes 1572864 | tf_op jit(solution)/shard_map/pallas_call | solution.py:366
  4.5 8.4 %all-to-all-start = ((bf16[16,264,128]{2,1,0:T(8,128)(2,1)}), bf16[16,264,128]{2,1,0:T(8,128)(2,1)}, u32[]{:S(2)}, u32[]{:S(2)}) async-start(bf16[16,264,128]{2,1,0:T(8,128)(2,1)} %shard_map.149), calls=%async_computation | async-start | bytes 2162688 | tf_op jit(solution)/shard_map/all_to_all | solution.py:390
  12.9 2.8 %collective-permute-start.2 = (bf16[256,512]{1,0:T(8,128)(2,1)S(1)}, bf16[256,512]{1,0:T(8,128)(2,1)S(1)}, u32[]{:S(2)}, u32[]{:S(2)}) collective-permute-start(bf16[256,512]{1,0:T(8,128)(2,1)S(1)} %copy-done.3), channel_id=1, source_target_pairs={{0,6},{2,4},{4,2},{6,0},{8,14},{10,12},{12,10},{14,8},{16,22},{18,... | collective-permute-start | bytes 786440 | tf_op jit(solution)/shard_map/ppermute | solution.py:300
  17.6 15.4 %collective-permute-done.2.refs_7_ = bf16[256,512]{1,0:T(8,128)(2,1)S(1)} collective-permute-done((bf16[256,512]{1,0:T(8,128)(2,1)S(1)}, bf16[256,512]{1,0:T(8,128)(2,1)S(1)}, u32[]{:S(2)}, u32[]{:S(2)}) %collective-permute-start.2) | collective-permute-done | bytes 262176 | tf_op jit(solution)/shard_map/ppermute | solution.py:300
  33.7 4.4 %collective-permute-done.1.refs_6_ = bf16[256,512]{1,0:T(8,128)(2,1)S(1)} collective-permute-done((bf16[256,512]{1,0:T(8,128)(2,1)S(1)}, bf16[256,512]{1,0:T(8,128)(2,1)S(1)}, u32[]{:S(2)}, u32[]{:S(2)}) %collective-permute-start.1) | collective-permute-done | bytes 262176 | tf_op jit(solution)/shard_map/ppermute | solution.py:300
  40.0 10.4 %shard_map.151 = (f32[256,512]{1,0:T(8,128)}, bf16[128,512]{1,0:T(8,128)(2,1)}, bf16[128,512]{1,0:T(8,128)(2,1)}) custom-call(bf16[16,264,128]{2,1,0:T(8,128)(2,1)} %all-to-all-done.refs_0_, bf16[256,1024]{1,0:T(8,128)(2,1)} %refs_1_.1, bf16[256,512]{1,0:T(8,128)(2,1)} %copy-done.14, bf16[256,512]{1,0:T(8,128)(2,1)} %refs_3_.1, bf16[512,512]{1,0:T(8,128)(2,1)} %refs_4_.5), custom_call_target="tpu_custom_call" | custom-call | flops 2147483648 | bytes 2621440 | tf_op jit(solution)/shard_map/pallas_call | solution.py:405
  51.4 4.9 %collective-permute-start.4 = (bf16[128,512]{1,0:T(8,128)(2,1)}, bf16[128,512]{1,0:T(8,128)(2,1)S(1)}, u32[]{:S(2)}, u32[]{:S(2)}) collective-permute-start(bf16[128,512]{1,0:T(8,128)(2,1)} %get-tuple-element.34.top), channel_id=1, source_target_pairs={{2,0},{4,2},{6,4},{8,6},{10,8},{12,10},{14,12},{16,14},{18,16},{20... | collective-permute-start | bytes 393224 | tf_op jit(solution)/shard_map/ppermute | solution.py:426
  59.6 2.3 %shard_map.153 = (f32[256,512]{1,0:T(8,128)S(1)}, bf16[256,512]{1,0:T(8,128)(2,1)S(1)}) custom-call(f32[256,512]{1,0:T(8,128)S(1)} %copy-done.11, bf16[128,512]{1,0:T(8,128)(2,1)S(1)} %collective-permute-done.3.before, bf16[128,512]{1,0:T(8,128)(2,1)S(1)} %collective-permute-done.4.after, bf16[512,1536]{1,0:T(8,128)(2,1)S(1)} %copy-done.2, ...), custom_call_target="tpu_custom_call" | custom-call | flops 469762048 | bytes 5242880 | tf_op jit(solution)/shard_map/pallas_call | solution.py:441
  62.6 2.0 %collective-permute-start.6 = (bf16[256,256]{1,0:T(8,128)(2,1)S(1)}, bf16[256,256]{1,0:T(8,128)(2,1)S(1)}, u32[]{:S(2)}, u32[]{:S(2)}) collective-permute-start(bf16[256,256]{1,0:T(8,128)(2,1)S(1)} %get-tuple-element.45.refs_2_), channel_id=1, source_target_pairs={{0,4},{2,6},{4,0},{6,2},{8,12},{10,14},{12,8},{14,10},{16,20},{18,... | collective-permute-start | bytes 393224 | tf_op jit(solution)/shard_map/ppermute | solution.py:300
  66.7 1.7 %collective-permute-done.5.refs_1_ = bf16[256,256]{1,0:T(8,128)(2,1)S(1)} collective-permute-done((bf16[256,256]{1,0:T(8,128)(2,1)S(1)}, bf16[256,256]{1,0:T(8,128)(2,1)S(1)}, u32[]{:S(2)}, u32[]{:S(2)}) %collective-permute-start.5) | collective-permute-done | bytes 131104 | tf_op jit(solution)/shard_map/ppermute | solution.py:300
  68.4 2.1 %collective-permute-done.7.refs_3_ = bf16[256,256]{1,0:T(8,128)(2,1)S(1)} collective-permute-done((bf16[256,256]{1,0:T(8,128)(2,1)S(1)}, bf16[256,256]{1,0:T(8,128)(2,1)S(1)}, u32[]{:S(2)}, u32[]{:S(2)}) %collective-permute-start.7) | collective-permute-done | bytes 131104 | tf_op jit(solution)/shard_map/ppermute | solution.py:300
  73.8 2.1 %collective-permute-start.17 = (bf16[256,256]{1,0:T(8,128)(2,1)S(1)}, bf16[256,256]{1,0:T(8,128)(2,1)S(1)}, u32[]{:S(2)}, u32[]{:S(2)}) collective-permute-start(bf16[256,256]{1,0:T(8,128)(2,1)S(1)} %get-tuple-element.54.refs_7_), channel_id=1, source_target_pairs={{0,6},{2,4},{4,2},{6,0},{8,14},{10,12},{12,10},{14,8},{16,22},{18,... | collective-permute-start | bytes 393224 | tf_op jit(solution)/shard_map/ppermute | solution.py:300
  76.1 3.7 %collective-permute-start.9 = (bf16[128,512]{1,0:T(8,128)(2,1)S(1)}, bf16[128,512]{1,0:T(8,128)(2,1)S(1)}, u32[]{:S(2)}, u32[]{:S(2)}) collective-permute-start(bf16[128,512]{1,0:T(8,128)(2,1)S(1)} %add_convert_fusion.3), channel_id=1, source_target_pairs={{0,16},{2,18},{4,20},{6,22},{8,24},{10,26},{12,28},{14,30},{16,0},... | collective-permute-start | bytes 393224 | tf_op jit(solution)/shard_map/ppermute | solution.py:300
  80.3 1.9 %collective-permute-start.18 = (bf16[128,512]{1,0:T(8,128)(2,1)S(1)}, bf16[128,512]{1,0:T(8,128)(2,1)S(1)}, u32[]{:S(2)}, u32[]{:S(2)}) collective-permute-start(bf16[128,512]{1,0:T(8,128)(2,1)S(1)} %get-tuple-element.59), channel_id=1, source_target_pairs={{0,8},{2,10},{4,12},{6,14},{8,0},{10,2},{12,4},{14,6},{16,24},{18,... | collective-permute-start | bytes 393224 | tf_op jit(solution)/shard_map/ppermute | solution.py:300
  83.4 2.0 %collective-permute-start.12 = (bf16[128,512]{1,0:T(8,128)(2,1)S(1)}, bf16[128,512]{1,0:T(8,128)(2,1)S(1)}, u32[]{:S(2)}, u32[]{:S(2)}) collective-permute-start(bf16[128,512]{1,0:T(8,128)(2,1)S(1)} %add_convert_fusion.2), channel_id=1, source_target_pairs={{0,8},{2,10},{4,12},{6,14},{8,0},{10,2},{12,4},{14,6},{16,24},{18,... | collective-permute-start | bytes 393224 | tf_op jit(solution)/shard_map/ppermute | solution.py:300
  85.9 3.8 %collective-permute-start.19 = (bf16[128,512]{1,0:T(8,128)(2,1)S(1)}, bf16[128,512]{1,0:T(8,128)(2,1)S(1)}, u32[]{:S(2)}, u32[]{:S(2)}) collective-permute-start(bf16[128,512]{1,0:T(8,128)(2,1)S(1)} %add_convert_fusion.1), channel_id=1, source_target_pairs={{0,16},{2,18},{4,20},{6,22},{8,24},{10,26},{12,28},{14,30},{16,0},... | collective-permute-start | bytes 393224 | tf_op jit(solution)/shard_map/ppermute | solution.py:300
  90.9 2.3 %collective-permute-start.13 = (bf16[128,512]{1,0:T(8,128)(2,1)S(1)}, bf16[128,512]{1,0:T(8,128)(2,1)S(1)}, u32[]{:S(2)}, u32[]{:S(2)}) collective-permute-start(bf16[128,512]{1,0:T(8,128)(2,1)S(1)} %collective-permute-done.12), channel_id=1, source_target_pairs={{0,4},{2,6},{4,0},{6,2},{8,12},{10,14},{12,8},{14,10},{16,20},{18,... | collective-permute-start | bytes 393224 | tf_op jit(solution)/shard_map/ppermute | solution.py:300
  93.2 2.6 %collective-permute-start.23 = (bf16[128,512]{1,0:T(8,128)(2,1)S(1)}, bf16[128,512]{1,0:T(8,128)(2,1)S(1)}, u32[]{:S(2)}, u32[]{:S(2)}) collective-permute-start(bf16[128,512]{1,0:T(8,128)(2,1)S(1)} %add_convert_fusion), channel_id=1, source_target_pairs={{0,8},{2,10},{4,12},{6,14},{8,0},{10,2},{12,4},{14,6},{16,24},{18,... | collective-permute-start | bytes 393224 | tf_op jit(solution)/shard_map/ppermute | solution.py:300
  96.3 1.5 %collective-permute-start.21 = (bf16[128,512]{1,0:T(8,128)(2,1)S(1)}, bf16[128,512]{1,0:T(8,128)(2,1)S(1)}, u32[]{:S(2)}, u32[]{:S(2)}) collective-permute-start(bf16[128,512]{1,0:T(8,128)(2,1)S(1)} %add_convert_fusion), channel_id=1, source_target_pairs={{0,4},{2,6},{4,0},{6,2},{8,12},{10,14},{12,8},{14,10},{16,20},{18,... | collective-permute-start | bytes 393224 | tf_op jit(solution)/shard_map/ppermute | solution.py:300
  97.9 1.5 %collective-permute-start.20 = (bf16[128,512]{1,0:T(8,128)(2,1)S(1)}, bf16[128,512]{1,0:T(8,128)(2,1)S(1)}, u32[]{:S(2)}, u32[]{:S(2)}) collective-permute-start(bf16[128,512]{1,0:T(8,128)(2,1)S(1)} %add_convert_fusion), channel_id=1, source_target_pairs={{0,2},{2,0},{4,6},{6,4},{8,10},{10,8},{12,14},{14,12},{16,18},{18,... | collective-permute-start | bytes 393224 | tf_op jit(solution)/shard_map/ppermute | solution.py:300
  100.6 2.6 %collective-permute-done.22 = bf16[128,512]{1,0:T(8,128)(2,1)S(1)} collective-permute-done((bf16[128,512]{1,0:T(8,128)(2,1)S(1)}, bf16[128,512]{1,0:T(8,128)(2,1)S(1)}, u32[]{:S(2)}, u32[]{:S(2)}) %collective-permute-start.22) | collective-permute-done | bytes 131104 | tf_op jit(solution)/shard_map/ppermute | solution.py:300
  103.7 1.9 %collective-permute-done.21 = bf16[128,512]{1,0:T(8,128)(2,1)S(1)} collective-permute-done((bf16[128,512]{1,0:T(8,128)(2,1)S(1)}, bf16[128,512]{1,0:T(8,128)(2,1)S(1)}, u32[]{:S(2)}, u32[]{:S(2)}) %collective-permute-start.21) | collective-permute-done | bytes 131104 | tf_op jit(solution)/shard_map/ppermute | solution.py:300
  106.3 1.5 %collective-permute-start.24 = (bf16[128,512]{1,0:T(8,128)(2,1)S(1)}, bf16[128,512]{1,0:T(8,128)(2,1)S(1)}, u32[]{:S(2)}, u32[]{:S(2)}) collective-permute-start(bf16[128,512]{1,0:T(8,128)(2,1)S(1)} %collective-permute-done.23), channel_id=1, source_target_pairs={{0,2},{2,0},{4,6},{6,4},{8,10},{10,8},{12,14},{14,12},{16,18},{18,... | collective-permute-start | bytes 393224 | tf_op jit(solution)/shard_map/ppermute | solution.py:300
  111.4 2.4 %shard_map.159 = f32[2048,512]{1,0:T(8,128)} custom-call(s32[1]{0:T(128)} %bitcast.me, bf16[2,128,512]{2,1,0:T(8,128)(2,1)S(1)} %pad_maximum_fusion.refs_0_, bf16[2,128,512]{2,1,0:T(8,128)(2,1)S(1)} %collective-permute-done.11.refs_1_, bf16[2,128,512]{2,1,0:T(8,128)(2,1)S(1)} %pad_maximum_fusion.1.refs_2_, ...), custom_call_target="tpu_custom_call" | custom-call | flops 4194304 | bytes 6291456 | tf_op jit(solution)/shard_map/pallas_call | solution.py:486
  (83 shorter events, 24.8 us)
Async XLA Ops:
  4.5 35.5 %all-to-all-start = ((bf16[16,264,128]{2,1,0:T(8,128)(2,1)}), bf16[16,264,128]{2,1,0:T(8,128)(2,1)}, u32[]{:S(2)}, u32[]{:S(2)}) async-start(bf16[16,264,128]{2,1,0:T(8,128)(2,1)} %shard_map.149), calls=%async_computation | async-start | bytes 2162688 | tf_op jit(solution)/shard_map/all_to_all | solution.py:390
  12.9 20.1 %collective-permute-start.2 = (bf16[256,512]{1,0:T(8,128)(2,1)S(1)}, bf16[256,512]{1,0:T(8,128)(2,1)S(1)}, u32[]{:S(2)}, u32[]{:S(2)}) collective-permute-start(bf16[256,512]{1,0:T(8,128)(2,1)S(1)} %copy-done.3), channel_id=1, source_target_pairs={{0,6},{2,4},{4,2},{6,0},{8,14},{10,12},{12,10},{14,8},{16,22},{18,... | collective-permute-start | bytes 786440 | tf_op jit(solution)/shard_map/ppermute | solution.py:300
  15.8 22.4 %collective-permute-start.1 = (bf16[256,512]{1,0:T(8,128)(2,1)S(1)}, bf16[256,512]{1,0:T(8,128)(2,1)S(1)}, u32[]{:S(2)}, u32[]{:S(2)}) collective-permute-start(bf16[256,512]{1,0:T(8,128)(2,1)S(1)} %copy-done.3), channel_id=1, source_target_pairs={{0,4},{2,6},{4,0},{6,2},{8,12},{10,14},{12,8},{14,10},{16,20},{18,... | collective-permute-start | bytes 786440 | tf_op jit(solution)/shard_map/ppermute | solution.py:300
  16.3 23.0 %collective-permute-start = (bf16[256,512]{1,0:T(8,128)(2,1)S(1)}, bf16[256,512]{1,0:T(8,128)(2,1)S(1)}, u32[]{:S(2)}, u32[]{:S(2)}) collective-permute-start(bf16[256,512]{1,0:T(8,128)(2,1)S(1)} %copy-done.3), channel_id=1, source_target_pairs={{0,2},{2,0},{4,6},{6,4},{8,10},{10,8},{12,14},{14,12},{16,18},{18,... | collective-permute-start | bytes 786440 | tf_op jit(solution)/shard_map/ppermute | solution.py:300
  50.5 9.0 %collective-permute-start.3 = (bf16[128,512]{1,0:T(8,128)(2,1)}, bf16[128,512]{1,0:T(8,128)(2,1)S(1)}, u32[]{:S(2)}, u32[]{:S(2)}) collective-permute-start(bf16[128,512]{1,0:T(8,128)(2,1)} %get-tuple-element.33.bottom), channel_id=1, source_target_pairs={{0,2},{2,4},{4,6},{6,8},{8,10},{10,12},{12,14},{14,16},{16,18},{18... | collective-permute-start | bytes 393224 | tf_op jit(solution)/shard_map/ppermute | solution.py:425
  51.4 8.1 %collective-permute-start.4 = (bf16[128,512]{1,0:T(8,128)(2,1)}, bf16[128,512]{1,0:T(8,128)(2,1)S(1)}, u32[]{:S(2)}, u32[]{:S(2)}) collective-permute-start(bf16[128,512]{1,0:T(8,128)(2,1)} %get-tuple-element.34.top), channel_id=1, source_target_pairs={{2,0},{4,2},{6,4},{8,6},{10,8},{12,10},{14,12},{16,14},{18,16},{20... | collective-permute-start | bytes 393224 | tf_op jit(solution)/shard_map/ppermute | solution.py:426
  62.5 5.8 %collective-permute-start.5 = (bf16[256,256]{1,0:T(8,128)(2,1)S(1)}, bf16[256,256]{1,0:T(8,128)(2,1)S(1)}, u32[]{:S(2)}, u32[]{:S(2)}) collective-permute-start(bf16[256,256]{1,0:T(8,128)(2,1)S(1)} %get-tuple-element.44.refs_1_), channel_id=1, source_target_pairs={{0,2},{2,0},{4,6},{6,4},{8,10},{10,8},{12,14},{14,12},{16,18},{18,... | collective-permute-start | bytes 393224 | tf_op jit(solution)/shard_map/ppermute | solution.py:300
  64.6 5.9 %collective-permute-start.7 = (bf16[256,256]{1,0:T(8,128)(2,1)S(1)}, bf16[256,256]{1,0:T(8,128)(2,1)S(1)}, u32[]{:S(2)}, u32[]{:S(2)}) collective-permute-start(bf16[256,256]{1,0:T(8,128)(2,1)S(1)} %get-tuple-element.46.refs_3_), channel_id=1, source_target_pairs={{0,6},{2,4},{4,2},{6,0},{8,14},{10,12},{12,10},{14,8},{16,22},{18,... | collective-permute-start | bytes 393224 | tf_op jit(solution)/shard_map/ppermute | solution.py:300
  72.5 7.3 %collective-permute-start.15 = (bf16[256,256]{1,0:T(8,128)(2,1)S(1)}, bf16[256,256]{1,0:T(8,128)(2,1)S(1)}, u32[]{:S(2)}, u32[]{:S(2)}) collective-permute-start(bf16[256,256]{1,0:T(8,128)(2,1)S(1)} %get-tuple-element.52.refs_5_), channel_id=1, source_target_pairs={{0,2},{2,0},{4,6},{6,4},{8,10},{10,8},{12,14},{14,12},{16,18},{18,... | collective-permute-start | bytes 393224 | tf_op jit(solution)/shard_map/ppermute | solution.py:300
  72.7 7.1 %collective-permute-start.16 = (bf16[256,256]{1,0:T(8,128)(2,1)S(1)}, bf16[256,256]{1,0:T(8,128)(2,1)S(1)}, u32[]{:S(2)}, u32[]{:S(2)}) collective-permute-start(bf16[256,256]{1,0:T(8,128)(2,1)S(1)} %get-tuple-element.53.refs_6_), channel_id=1, source_target_pairs={{0,4},{2,6},{4,0},{6,2},{8,12},{10,14},{12,8},{14,10},{16,20},{18,... | collective-permute-start | bytes 393224 | tf_op jit(solution)/shard_map/ppermute | solution.py:300
  73.8 6.0 %collective-permute-start.17 = (bf16[256,256]{1,0:T(8,128)(2,1)S(1)}, bf16[256,256]{1,0:T(8,128)(2,1)S(1)}, u32[]{:S(2)}, u32[]{:S(2)}) collective-permute-start(bf16[256,256]{1,0:T(8,128)(2,1)S(1)} %get-tuple-element.54.refs_7_), channel_id=1, source_target_pairs={{0,6},{2,4},{4,2},{6,0},{8,14},{10,12},{12,10},{14,8},{16,22},{18,... | collective-permute-start | bytes 393224 | tf_op jit(solution)/shard_map/ppermute | solution.py:300
  76.1 7.3 %collective-permute-start.9 = (bf16[128,512]{1,0:T(8,128)(2,1)S(1)}, bf16[128,512]{1,0:T(8,128)(2,1)S(1)}, u32[]{:S(2)}, u32[]{:S(2)}) collective-permute-start(bf16[128,512]{1,0:T(8,128)(2,1)S(1)} %add_convert_fusion.3), channel_id=1, source_target_pairs={{0,16},{2,18},{4,20},{6,22},{8,24},{10,26},{12,28},{14,30},{16,0},... | collective-permute-start | bytes 393224 | tf_op jit(solution)/shard_map/ppermute | solution.py:300
  83.4 7.4 %collective-permute-start.12 = (bf16[128,512]{1,0:T(8,128)(2,1)S(1)}, bf16[128,512]{1,0:T(8,128)(2,1)S(1)}, u32[]{:S(2)}, u32[]{:S(2)}) collective-permute-start(bf16[128,512]{1,0:T(8,128)(2,1)S(1)} %add_convert_fusion.2), channel_id=1, source_target_pairs={{0,8},{2,10},{4,12},{6,14},{8,0},{10,2},{12,4},{14,6},{16,24},{18,... | collective-permute-start | bytes 393224 | tf_op jit(solution)/shard_map/ppermute | solution.py:300
  85.9 7.3 %collective-permute-start.19 = (bf16[128,512]{1,0:T(8,128)(2,1)S(1)}, bf16[128,512]{1,0:T(8,128)(2,1)S(1)}, u32[]{:S(2)}, u32[]{:S(2)}) collective-permute-start(bf16[128,512]{1,0:T(8,128)(2,1)S(1)} %add_convert_fusion.1), channel_id=1, source_target_pairs={{0,16},{2,18},{4,20},{6,22},{8,24},{10,26},{12,28},{14,30},{16,0},... | collective-permute-start | bytes 393224 | tf_op jit(solution)/shard_map/ppermute | solution.py:300
  89.7 8.2 %collective-permute-start.10 = (bf16[128,512]{1,0:T(8,128)(2,1)S(1)}, bf16[128,512]{1,0:T(8,128)(2,1)S(1)}, u32[]{:S(2)}, u32[]{:S(2)}) collective-permute-start(bf16[128,512]{1,0:T(8,128)(2,1)S(1)} %add_convert_fusion.2), channel_id=1, source_target_pairs={{0,2},{2,0},{4,6},{6,4},{8,10},{10,8},{12,14},{14,12},{16,18},{18,... | collective-permute-start | bytes 393224 | tf_op jit(solution)/shard_map/ppermute | solution.py:300
  90.9 8.5 %collective-permute-start.13 = (bf16[128,512]{1,0:T(8,128)(2,1)S(1)}, bf16[128,512]{1,0:T(8,128)(2,1)S(1)}, u32[]{:S(2)}, u32[]{:S(2)}) collective-permute-start(bf16[128,512]{1,0:T(8,128)(2,1)S(1)} %collective-permute-done.12), channel_id=1, source_target_pairs={{0,4},{2,6},{4,0},{6,2},{8,12},{10,14},{12,8},{14,10},{16,20},{18,... | collective-permute-start | bytes 393224 | tf_op jit(solution)/shard_map/ppermute | solution.py:300
  93.2 7.0 %collective-permute-start.23 = (bf16[128,512]{1,0:T(8,128)(2,1)S(1)}, bf16[128,512]{1,0:T(8,128)(2,1)S(1)}, u32[]{:S(2)}, u32[]{:S(2)}) collective-permute-start(bf16[128,512]{1,0:T(8,128)(2,1)S(1)} %add_convert_fusion), channel_id=1, source_target_pairs={{0,8},{2,10},{4,12},{6,14},{8,0},{10,2},{12,4},{14,6},{16,24},{18,... | collective-permute-start | bytes 393224 | tf_op jit(solution)/shard_map/ppermute | solution.py:300
  95.8 7.4 %collective-permute-start.22 = (bf16[128,512]{1,0:T(8,128)(2,1)S(1)}, bf16[128,512]{1,0:T(8,128)(2,1)S(1)}, u32[]{:S(2)}, u32[]{:S(2)}) collective-permute-start(bf16[128,512]{1,0:T(8,128)(2,1)S(1)} %add_convert_fusion), channel_id=1, source_target_pairs={{0,6},{2,4},{4,2},{6,0},{8,14},{10,12},{12,10},{14,8},{16,22},{18,... | collective-permute-start | bytes 393224 | tf_op jit(solution)/shard_map/ppermute | solution.py:300
  96.3 9.2 %collective-permute-start.21 = (bf16[128,512]{1,0:T(8,128)(2,1)S(1)}, bf16[128,512]{1,0:T(8,128)(2,1)S(1)}, u32[]{:S(2)}, u32[]{:S(2)}) collective-permute-start(bf16[128,512]{1,0:T(8,128)(2,1)S(1)} %add_convert_fusion), channel_id=1, source_target_pairs={{0,4},{2,6},{4,0},{6,2},{8,12},{10,14},{12,8},{14,10},{16,20},{18,... | collective-permute-start | bytes 393224 | tf_op jit(solution)/shard_map/ppermute | solution.py:300
  97.9 8.5 %collective-permute-start.20 = (bf16[128,512]{1,0:T(8,128)(2,1)S(1)}, bf16[128,512]{1,0:T(8,128)(2,1)S(1)}, u32[]{:S(2)}, u32[]{:S(2)}) collective-permute-start(bf16[128,512]{1,0:T(8,128)(2,1)S(1)} %add_convert_fusion), channel_id=1, source_target_pairs={{0,2},{2,0},{4,6},{6,4},{8,10},{10,8},{12,14},{14,12},{16,18},{18,... | collective-permute-start | bytes 393224 | tf_op jit(solution)/shard_map/ppermute | solution.py:300
  99.4 12.1 %collective-permute-start.11 = (bf16[2,128,512]{2,1,0:T(8,128)(2,1)S(1)}, bf16[2,128,512]{2,1,0:T(8,128)(2,1)S(1)}, u32[]{:S(2)}, u32[]{:S(2)}) collective-permute-start(bf16[2,128,512]{2,1,0:T(8,128)(2,1)S(1)} %pad_maximum_fusion.refs_0_), channel_id=1, source_target_pairs={{0,4},{2,6},{4,0},{6,2},{8,12},{10,14},{12,8},{14,10},{16,20},{18,... | collective-permute-start | bytes 786440 | tf_op jit(solution)/shard_map/ppermute | solution.py:300
  100.3 11.2 %collective-permute-start.14 = (bf16[2,128,512]{2,1,0:T(8,128)(2,1)S(1)}, bf16[2,128,512]{2,1,0:T(8,128)(2,1)S(1)}, u32[]{:S(2)}, u32[]{:S(2)}) collective-permute-start(bf16[2,128,512]{2,1,0:T(8,128)(2,1)S(1)} %pad_maximum_fusion.1.refs_2_), channel_id=1, source_target_pairs={{0,2},{2,0},{4,6},{6,4},{8,10},{10,8},{12,14},{14,12},{16,18},{18,... | collective-permute-start | bytes 786440 | tf_op jit(solution)/shard_map/ppermute | solution.py:300
  103.2 6.8 %collective-permute-start.26 = (bf16[128,512]{1,0:T(8,128)(2,1)S(1)}, bf16[128,512]{1,0:T(8,128)(2,1)S(1)}, u32[]{:S(2)}, u32[]{:S(2)}) collective-permute-start(bf16[128,512]{1,0:T(8,128)(2,1)S(1)} %collective-permute-done.23), channel_id=1, source_target_pairs={{0,6},{2,4},{4,2},{6,0},{8,14},{10,12},{12,10},{14,8},{16,22},{18,... | collective-permute-start | bytes 393224 | tf_op jit(solution)/shard_map/ppermute | solution.py:300
  105.6 5.8 %collective-permute-start.25 = (bf16[128,512]{1,0:T(8,128)(2,1)S(1)}, bf16[128,512]{1,0:T(8,128)(2,1)S(1)}, u32[]{:S(2)}, u32[]{:S(2)}) collective-permute-start(bf16[128,512]{1,0:T(8,128)(2,1)S(1)} %collective-permute-done.23), channel_id=1, source_target_pairs={{0,4},{2,6},{4,0},{6,2},{8,12},{10,14},{12,8},{14,10},{16,20},{18,... | collective-permute-start | bytes 393224 | tf_op jit(solution)/shard_map/ppermute | solution.py:300
  (21 other events, 186.9 us)

commit v5 on v4

--- a/solution.py
+++ b/solution.py
@@ -10,7 +10,7 @@
 LANES = 128
 PLANE = 4
 CHUNKS = 2
-DIRECT = (1,)
+HOPS = ((True, True), (False, False))
 BF = jnp.bfloat16
 F32 = jnp.float32
 MIB = 1024 * 1024
@@ -60,13 +60,11 @@
 
 
 def pack_kernel(*refs, tiles, cap):
-    inputs, out, local, arrivals = refs[:5], refs[5], refs[6:11], refs[11]
-    for copy in started(inputs, local, arrivals):
-        copy.wait()
-    obs, inst, route, cell, table = local
+    inputs, out, local, (packed, arrivals, leaving) = refs[:5], refs[5], refs[6:11], refs[11:]
+    copies = started(inputs, local, arrivals)
+    route, cell, inst, table, obs = local
     rows, channels = obs.shape
-    kinds = (iota((table.shape[0], rows), 0) == inst[...]).astype(F32).astype(BF)
-    embedded = (obs[...].astype(F32) + dot(kinds, table[...], ((0,), (0,)))).astype(BF)
+    copies[0].wait()
     chosen = (iota((tiles, rows), 0) == route[...]).astype(F32)
     pieces = rows // LANES
     stacked = jnp.concatenate(
@@ -82,26 +80,39 @@
         base = base + part[:, LANES - 1 :]
     place = jnp.concatenate(parts, axis=1)
     rank = (jnp.sum(chosen * place, axis=0, keepdims=True) - 1.0).astype(jnp.int32)
+    slot = route[...] * cap + rank
+    copies[1].wait()
     mark = chosen * (cell[...] + 1).astype(F32)
     at_rank = (iota((cap, rows), 0) == rank).astype(F32).astype(BF)
     marks = dot(mark.astype(BF), at_rank, ((1,), (1,)))
-    slot = route[...] * cap + rank
+    if cap < LANES:
+        marks = jnp.concatenate([marks, jnp.zeros((tiles, LANES - cap), F32)], axis=1)
+    for copy in copies[2:]:
+        copy.wait()
+    kinds = (iota((table.shape[0], rows), 0) == inst[...]).astype(F32).astype(BF)
+    embedded = (obs[...].astype(F32) + dot(kinds, table[...], ((0,), (0,)))).astype(BF)
     split = channels // LANES
     step = min(256, tiles * cap)
-    if cap < LANES:
-        marks = jnp.concatenate([marks, jnp.zeros((tiles, LANES - cap), F32)], axis=1)
+    sent = []
     for first in range(0, tiles * cap, step):
         pick = (iota((step, rows), 0) + first == slot).astype(F32).astype(BF)
         moved = dot(pick, embedded).astype(BF)
+        here = slice(first // cap, (first + step) // cap)
         for i in range(step // cap):
             t = first // cap + i
             for c in range(split):
-                out[t, c * cap : (c + 1) * cap, :] = moved[
+                packed[t, c * cap : (c + 1) * cap, :] = moved[
                     i * cap : (i + 1) * cap, c * LANES : (c + 1) * LANES
                 ]
-            out[t, split * cap :, :] = jnp.broadcast_to(
-                marks[t : t + 1, :], (out.shape[1] - split * cap, LANES)
+            packed[t, split * cap :, :] = jnp.broadcast_to(
+                marks[t : t + 1, :], (packed.shape[1] - split * cap, LANES)
             ).astype(BF)
+        sent.append(
+            pltpu.make_async_copy(packed.at[here], out.at[here], leaving.at[first // step])
+        )
+        sent[-1].start()
+    for copy in sent:
+        copy.wait()
 
 
 def heads_pair(query, keys, values, add, earlier=None):
@@ -158,7 +169,7 @@
 
 
 def cross_kernel(*refs, cap, inputs):
-    (stream_out, top, bottom), refs, far = refs[inputs : inputs + 3], refs[inputs + 3 :], refs[:inputs]
+    far, (stream_out, normed, top, bottom), refs = refs[:inputs], refs[inputs : inputs + 4], refs[inputs + 4 :]
     local, (x, kv, add, cross, arrivals) = refs[:inputs], refs[inputs:]
     copies = started(far, local, arrivals)
     arrived, w_kv, q, latent, w_out = local[:5]
@@ -180,16 +191,21 @@
     pairs(width, body)
     stream = latent[...].astype(F32) + dot(cross[...], w_out[...])
     stream_out[...] = stream
-    normed = rms_norm(stream).astype(BF)
-    top[...] = normed[: cells // 2]
-    bottom[...] = normed[cells // 2 :]
-
-
-def inner_kernel(top, bottom, w_qkv, q, peak, mixed, total, kv, own, add):
+    rows = rms_norm(stream).astype(BF)
+    normed[...] = rows
+    top[...] = rows[: cells // 2]
+    bottom[...] = rows[cells // 2 :]
+
+
+def inner_kernel(w_qkv, cells_far, *refs, fetched):
+    far, (q, peak, mixed, total), near = refs[:fetched], refs[fetched : fetched + 4], refs[fetched + 4 :]
+    near, (kv, own, add, arrivals) = near[:fetched], near[fetched:]
     cells, width = q.shape
     reach = cells // 2
-    own[:reach, :] = top[...]
-    own[reach:, :] = bottom[...]
+    cells_in = started((cells_far,), (own,), arrivals)
+    copies = started(far, near, arrivals.at[1:]) if fetched else []
+    for copy in cells_in:
+        copy.wait()
     q[...] = project_query(own[...], w_qkv[:, :width], width)
     kv[...] = dot(own[...], w_qkv[:, width:]).astype(BF)
     offsets = iota(add.shape, 1) - iota(add.shape, 0)
@@ -201,6 +217,8 @@
         )
 
     pairs(width, body)
+    for copy in copies:
+        copy.wait()
 
 
 def outer_kernel(
@@ -304,33 +322,20 @@
     return value.astype(BF)
 
 
-def reduced(own, other, base, wait_for, direct):
+def reduced(own, other, base, hops):
     own = narrow(own + flipped(other, PLANE).astype(F32))
-    across = flipped(own, 2 * PLANE)
-    own = narrow(own.astype(F32) + across.astype(F32))
-    if direct:
-        owns = [own] + [flipped(own, j) for j in range(1, PLANE)]
-        other = flipped(own, PLANE)
-        others = [other] + [flipped(other, j) for j in range(1, PLANE)]
-        return (
-            [across],
-            [half[None] for half in owns + others],
-            [[(j, base, n)] for n in range(2) for j in range(PLANE)],
-        )
-    other = flipped(own, PLANE)
-    own_x, other_y = flipped(own, 1), flipped(other, 2)
-    own, other = jnp.stack([own, own_x]), jnp.stack([other, other_y])
-    own_y, other_x = flipped(own, 2), flipped(other, 1)
-    return (
-        [across],
-        [own, own_y, other, other_x],
-        [
-            [(0, base, 0), (1, base, 0)],
-            [(2, base, 0), (3, base, 0)],
-            [(0, base, 1), (2, base, 1)],
-            [(1, base, 1), (3, base, 1)],
-        ],
-    )
+    own = narrow(own.astype(F32) + flipped(own, 2 * PLANE).astype(F32))
+    pieces, order = [], []
+    for n, (first, two) in enumerate(zip((1, 2), hops, strict=True)):
+        half = flipped(own, PLANE) if n else own
+        if two:
+            pair = jnp.stack([half, flipped(half, first)])
+            pieces += [pair, flipped(pair, 3 - first)]
+            order += [[(0, base, n), (first, base, n)], [(3 - first, base, n), (3, base, n)]]
+        else:
+            pieces += [half[None]] + [flipped(half, j)[None] for j in range(1, PLANE)]
+            order += [[(j, base, n)] for j in range(PLANE)]
+    return pieces, order
 
 
 def on_device(
@@ -370,28 +375,29 @@
         2 * tiles * cap * channels + 2 * count * channels,
         [FAR] * 5,
         scratch=[
-            pltpu.VMEM((count, channels), BF),
             pltpu.VMEM((1, count), jnp.int32),
             pltpu.VMEM((1, count), jnp.int32),
             pltpu.VMEM((1, count), jnp.int32),
             pltpu.VMEM(inst_table.shape, BF),
+            pltpu.VMEM((count, channels), BF),
+            pltpu.VMEM((tiles, rows, LANES), BF),
             pltpu.SemaphoreType.DMA((5,)),
+            pltpu.SemaphoreType.DMA((-(-tiles * cap // 256),)),
         ],
+        out_spec=FAR,
         limit=62,
     )(
-        observations,
-        instrument.reshape(1, count),
         route.reshape(1, count),
         cell_index.reshape(1, count),
+        instrument.reshape(1, count),
         inst_table,
+        observations,
     )
 
     keys = tiles * cap
     arrived = lax.all_to_all(packed, "tile", split_axis=0, concat_axis=0, tiled=True)
     if fast:
         cotangents = [flipped(cotangent, j) for j in range(1, PLANE)]
-        arrived, *cotangents = lax.optimization_barrier((arrived, *cotangents))
-        cotangents = [cotangent, *cotangents]
     query = call(
         query_kernel,
         query_shape,
@@ -402,9 +408,9 @@
     )(latent, w_cross_q)
     marks = [arrived[:, split * cap, :cap].reshape(1, keys).astype(F32)] if cap % LANES else []
     operands = (arrived, w_obs_kv, query, latent, w_cross_out, *marks)
-    stream1, top, bottom = call(
+    stream1, own, top, bottom = call(
         functools.partial(cross_kernel, cap=cap, inputs=len(operands)),
-        (stream_shape, half_shape, half_shape),
+        (stream_shape, query_shape, half_shape, half_shape),
         4 * keys * channels * width + 4 * cells * keys * width,
         2 * keys * channels + 6 * width * width,
         [FAR] * len(operands),
@@ -420,24 +426,32 @@
         limit=62,
     )(*operands)
 
+    if not fast:
+        cotangents = []
+    else:
+        top, bottom, *cotangents = lax.optimization_barrier((top, bottom, *cotangents))
+        cotangents = [cotangent, *cotangents]
     forward = [(i, (i + 1) % tiles) for i in range(tiles)]
     backward = [(b, a) for a, b in forward]
     before = lax.ppermute(bottom, "tile", forward)
     after = lax.ppermute(top, "tile", backward)
+    fetched = len(cotangents)
     partial = call(
-        inner_kernel,
-        (query_shape, stream_shape, stream_shape, stream_shape),
+        functools.partial(inner_kernel, fetched=fetched),
+        (query_shape, stream_shape, stream_shape, stream_shape, *([query_shape] * fetched)),
         6 * cells * width * width + 4 * cells * cells * width,
         6 * width * width + 16 * cells * width,
-        [WHOLE] * 3,
+        [WHOLE] + [FAR] * (1 + fetched),
         scratch=[
             pltpu.VMEM((cells, 2 * width), BF),
             pltpu.VMEM((cells, width), BF),
             pltpu.VMEM((cells, cells), F32),
+            pltpu.SemaphoreType.DMA((1 + fetched,)),
         ],
         transcendentals=H * cells * cells,
         limit=20,
-    )(top, bottom, w_win_qkv)
+    )(w_win_qkv, own, *cotangents)
+    partial, cotangents = partial[:4], partial[4:]
     stream2, normed = call(
         outer_kernel,
         (stream_shape, query_shape),
@@ -468,7 +482,7 @@
     if fast:
         received[0][0], received[1][0] = lax.optimization_barrier((received[0][0], received[1][0]))
         half = shape((step // 2, width), F32)
-        last, pieces, order = [], [], []
+        pieces, order = [], []
         for c in range(CHUNKS):
             own, other = call(
                 plane_kernel,
@@ -481,7 +495,7 @@
             )(me, *received[c], *cotangents)
             if c == 0:
                 stream2, own = lax.optimization_barrier((stream2, own))
-            last, more, places = reduced(own, other, c * step, last, c in DIRECT)
+            more, places = reduced(own, other, c * step, HOPS[c])
             pieces, order = pieces + more, order + places
         clipped = call(
             functools.partial(clip_kernel, order=order, unit=step // 2),

time: 114 us -> 113 us (level)
  waiting for transfers between devices: 32.6 us -> 36.4 us
  local copies, waits for them, and re-layouts: 4.7 us -> 1.69 us
  starting transfers between devices: 51 us -> 49.4 us
    all_to_all x1, waiting for transfers between devices: 0.01 us -> 20.7 us  [on_device(): lax.all_to_all(packed, 'tile', split_axis=0, concat_axis=0, tiled=True)]
    ppermute x25, waiting for transfers between devices: 32.6 us -> 14.9 us  [flipped(): lax.ppermute(value, 'tile', [(i, i ^ k) for i in range(PLANE * PLANE)])]
    unnamed x34 -> x18, local copies, waits for them, and re-layouts: 4.7 us -> 1.69 us
    ppermute x25, starting transfers between devices: 36.9 us -> 35.3 us  [flipped(): lax.ppermute(value, 'tile', [(i, i ^ k) for i in range(PLANE * PLANE)])]
  transfers between devices with their start and end apart: 28 -> 28, of which waited for: 13 -> 12; matrix products, arithmetic and copies ran while one was open for 0% -> 0% of each run, Pallas kernels for 4% -> 13%
where the time goes in v5:
time: 113 us
  starting transfers between devices  49.4 us (44%)
  waiting for transfers between devices  36.4 us (32%)
  Pallas kernels  24.3 us (22%)
  local copies, waits for them, and re-layouts  1.69 us (1%)
    ppermute x25, starting transfers between devices, flipped(): lax.ppermute(value, 'tile', [(i, i ^ k) for i in range(PLANE * PLANE)])  35.3 us
    all_to_all x1, waiting for transfers between devices, on_device(): lax.all_to_all(packed, 'tile', split_axis=0, concat_axis=0, tiled=True)  20.7 us
    ppermute x25, waiting for transfers between devices, flipped(): lax.ppermute(value, 'tile', [(i, i ^ k) for i in range(PLANE * PLANE)])  14.9 us
    pallas_call x1, Pallas kernels, on_device(): call(functools.partial(cross_kernel, cap=cap, inputs=len(operands)), (str...  10.5 us
    all_to_all x1, starting transfers between devices, on_device(): lax.all_to_all(packed, 'tile', split_axis=0, concat_axis=0, tiled=True)  8.37 us
    ppermute x1, starting transfers between devices, on_device(): after = lax.ppermute(top, 'tile', backward)  4.93 us
    pallas_call x1, Pallas kernels, on_device(): call(functools.partial(pack_kernel, tiles=tiles, cap=cap), shape((tiles,...  3.52 us
    pallas_call x1, Pallas kernels, on_device(): call(functools.partial(clip_kernel, order=order, unit=step // 2), shape((...  2.43 us
  transfers between devices with their start and end apart: 28, of which 12 were waited for; matrix products, arithmetic and copies ran while one was open for 0% of the time, Pallas kernels for 13%

profile of v5, /device:TPU:0, one launch (start us, length us, event | category | flops | bytes accessed | tf_op | source)
XLA Modules:
  0.0 112.9 jit_solution(2299215755013601490)
XLA Ops:
  0.7 3.5 %shard_map.149 = bf16[16,264,128]{2,1,0:T(8,128)(2,1)} custom-call(s32[1,1024]{1,0:T(1,128)} %bitcast.28, s32[1,1024]{1,0:T(1,128)} %bitcast.29, s32[1,1024]{1,0:T(1,128)} %bitcast.30, bf16[32,256]{1,0:T(8,128)(2,1)} %refs_3_.2, bf16[1024,256]{1,0:T(8,128)(2,1)} %refs_4_.2), custom_call_target="tpu_custom_call" | custom-call | flops 1073741824 | bytes 1572864 | tf_op jit(solution)/shard_map/pallas_call | solution.py:371
  4.2 8.4 %all-to-all-start = ((bf16[16,264,128]{2,1,0:T(8,128)(2,1)}), bf16[16,264,128]{2,1,0:T(8,128)(2,1)}, u32[]{:S(2)}, u32[]{:S(2)}) async-start(bf16[16,264,128]{2,1,0:T(8,128)(2,1)} %shard_map.149), calls=%async_computation | async-start | bytes 2162688 | tf_op jit(solution)/shard_map/all_to_all | solution.py:398
  12.6 1.9 %collective-permute-start.1 = (bf16[256,512]{1,0:T(8,128)(2,1)}, bf16[256,512]{1,0:T(8,128)(2,1)}, u32[]{:S(2)}, u32[]{:S(2)}) collective-permute-start(bf16[256,512]{1,0:T(8,128)(2,1)} %refs_0_.1), channel_id=1, source_target_pairs={{0,4},{2,6},{4,0},{6,2},{8,12},{10,14},{12,8},{14,10},{16,20},{18,... | collective-permute-start | bytes 786440 | tf_op jit(solution)/shard_map/ppermute | solution.py:318
  14.4 1.5 %collective-permute-start = (bf16[256,512]{1,0:T(8,128)(2,1)}, bf16[256,512]{1,0:T(8,128)(2,1)}, u32[]{:S(2)}, u32[]{:S(2)}) collective-permute-start(bf16[256,512]{1,0:T(8,128)(2,1)} %refs_0_.1), channel_id=1, source_target_pairs={{0,2},{2,0},{4,6},{6,4},{8,10},{10,8},{12,14},{14,12},{16,18},{18,... | collective-permute-start | bytes 786440 | tf_op jit(solution)/shard_map/ppermute | solution.py:318
  17.2 20.7 %all-to-all-done.refs_0_ = bf16[16,264,128]{2,1,0:T(8,128)(2,1)} async-done(((bf16[16,264,128]{2,1,0:T(8,128)(2,1)}), bf16[16,264,128]{2,1,0:T(8,128)(2,1)}, u32[]{:S(2)}, u32[]{:S(2)}) %all-to-all-start) | async-done | bytes 1081376 | tf_op jit(solution)/shard_map/all_to_all | solution.py:398
  37.9 10.5 %shard_map.151 = (f32[256,512]{1,0:T(8,128)}, bf16[256,512]{1,0:T(8,128)(2,1)}, bf16[128,512]{1,0:T(8,128)(2,1)}, bf16[128,512]{1,0:T(8,128)(2,1)}) custom-call(bf16[16,264,128]{2,1,0:T(8,128)(2,1)} %all-to-all-done.refs_0_, bf16[256,1024]{1,0:T(8,128)(2,1)} %refs_1_.1, bf16[256,512]{1,0:T(8,128)(2,1)} %copy-done.7, bf16[256,512]{1,0:T(8,128)(2,1)} %refs_3_.3, ...), custom_call_target="tpu_custom_call" | custom-call | flops 2147483648 | bytes 2621440 | tf_op jit(solution)/shard_map/pallas_call | solution.py:411
  49.2 4.9 %collective-permute-start.4 = (bf16[128,512]{1,0:T(8,128)(2,1)}, bf16[128,512]{1,0:T(8,128)(2,1)S(1)}, u32[]{:S(2)}, u32[]{:S(2)}) collective-permute-start(bf16[128,512]{1,0:T(8,128)(2,1)} %get-tuple-element.41), channel_id=1, source_target_pairs={{2,0},{4,2},{6,4},{8,6},{10,8},{12,10},{14,12},{16,14},{18,16},{20... | collective-permute-start | bytes 393224 | tf_op jit(solution)/shard_map/ppermute | solution.py:437
  55.1 1.5 %shard_map.152 = (bf16[256,512]{1,0:T(8,128)(2,1)S(1)}, f32[256,512]{1,0:T(8,128)S(1)}, f32[256,512]{1,0:T(8,128)S(1)}, f32[256,512]{1,0:T(8,128)S(1)}, bf16[256...) custom-call(bf16[512,1536]{1,0:T(8,128)(2,1)S(1)} %copy-done.1, ...), custom_call_target="tpu_custom_call" | custom-call | flops 536870912 | bytes 3670016 | tf_op jit(solution)/shard_map/pallas_call | solution.py:439
  57.4 2.3 %shard_map.153 = (f32[256,512]{1,0:T(8,128)S(1)}, bf16[256,512]{1,0:T(8,128)(2,1)S(1)}) custom-call(f32[256,512]{1,0:T(8,128)S(1)} %copy-done.4, bf16[128,512]{1,0:T(8,128)(2,1)S(1)} %collective-permute-done.3.before, bf16[128,512]{1,0:T(8,128)(2,1)S(1)} %collective-permute-done.4.after, bf16[512,1536]{1,0:T(8,128)(2,1)S(1)} %copy-done.1, ...), custom_call_target="tpu_custom_call" | custom-call | flops 469762048 | bytes 5242880 | tf_op jit(solution)/shard_map/pallas_call | solution.py:455
  60.9 3.5 %collective-permute-start.6 = (bf16[256,256]{1,0:T(8,128)(2,1)S(1)}, bf16[256,256]{1,0:T(8,128)(2,1)S(1)}, u32[]{:S(2)}, u32[]{:S(2)}) collective-permute-start(bf16[256,256]{1,0:T(8,128)(2,1)S(1)} %get-tuple-element.56.refs_2_), channel_id=1, source_target_pairs={{0,4},{2,6},{4,0},{6,2},{8,12},{10,14},{12,8},{14,10},{16,20},{18,... | collective-permute-start | bytes 393224 | tf_op jit(solution)/shard_map/ppermute | solution.py:318
  65.6 2.7 %collective-permute-done.6.refs_2_ = bf16[256,256]{1,0:T(8,128)(2,1)S(1)} collective-permute-done((bf16[256,256]{1,0:T(8,128)(2,1)S(1)}, bf16[256,256]{1,0:T(8,128)(2,1)S(1)}, u32[]{:S(2)}, u32[]{:S(2)}) %collective-permute-start.6) | collective-permute-done | bytes 131104 | tf_op jit(solution)/shard_map/ppermute | solution.py:318
  68.3 1.9 %collective-permute-done.7.refs_3_ = bf16[256,256]{1,0:T(8,128)(2,1)S(1)} collective-permute-done((bf16[256,256]{1,0:T(8,128)(2,1)S(1)}, bf16[256,256]{1,0:T(8,128)(2,1)S(1)}, u32[]{:S(2)}, u32[]{:S(2)}) %collective-permute-start.7) | collective-permute-done | bytes 131104 | tf_op jit(solution)/shard_map/ppermute | solution.py:318
  72.9 2.7 %collective-permute-start.17 = (bf16[256,256]{1,0:T(8,128)(2,1)S(1)}, bf16[256,256]{1,0:T(8,128)(2,1)S(1)}, u32[]{:S(2)}, u32[]{:S(2)}) collective-permute-start(bf16[256,256]{1,0:T(8,128)(2,1)S(1)} %get-tuple-element.66.refs_7_), channel_id=1, source_target_pairs={{0,6},{2,4},{4,2},{6,0},{8,14},{10,12},{12,10},{14,8},{16,22},{18,... | collective-permute-start | bytes 393224 | tf_op jit(solution)/shard_map/ppermute | solution.py:318
  76.4 2.9 %collective-permute-start.9 = (bf16[128,512]{1,0:T(8,128)(2,1)S(1)}, bf16[128,512]{1,0:T(8,128)(2,1)S(1)}, u32[]{:S(2)}, u32[]{:S(2)}) collective-permute-start(bf16[128,512]{1,0:T(8,128)(2,1)S(1)} %add_convert_fusion.3), channel_id=1, source_target_pairs={{0,16},{2,18},{4,20},{6,22},{8,24},{10,26},{12,28},{14,30},{16,0},... | collective-permute-start | bytes 393224 | tf_op jit(solution)/shard_map/ppermute | solution.py:318
  79.9 2.3 %collective-permute-start.18 = (bf16[128,512]{1,0:T(8,128)(2,1)S(1)}, bf16[128,512]{1,0:T(8,128)(2,1)S(1)}, u32[]{:S(2)}, u32[]{:S(2)}) collective-permute-start(bf16[128,512]{1,0:T(8,128)(2,1)S(1)} %get-tuple-element.71), channel_id=1, source_target_pairs={{0,8},{2,10},{4,12},{6,14},{8,0},{10,2},{12,4},{14,6},{16,24},{18,... | collective-permute-start | bytes 393224 | tf_op jit(solution)/shard_map/ppermute | solution.py:318
  82.2 3.0 %collective-permute-done.9 = bf16[128,512]{1,0:T(8,128)(2,1)S(1)} collective-permute-done((bf16[128,512]{1,0:T(8,128)(2,1)S(1)}, bf16[128,512]{1,0:T(8,128)(2,1)S(1)}, u32[]{:S(2)}, u32[]{:S(2)}) %collective-permute-start.9) | collective-permute-done | bytes 131104 | tf_op jit(solution)/shard_map/ppermute | solution.py:318
  85.2 2.0 %collective-permute-start.12 = (bf16[128,512]{1,0:T(8,128)(2,1)S(1)}, bf16[128,512]{1,0:T(8,128)(2,1)S(1)}, u32[]{:S(2)}, u32[]{:S(2)}) collective-permute-start(bf16[128,512]{1,0:T(8,128)(2,1)S(1)} %add_convert_fusion.2), channel_id=1, source_target_pairs={{0,8},{2,10},{4,12},{6,14},{8,0},{10,2},{12,4},{14,6},{16,24},{18,... | collective-permute-start | bytes 393224 | tf_op jit(solution)/shard_map/ppermute | solution.py:318
  87.3 3.4 %collective-permute-start.19 = (bf16[128,512]{1,0:T(8,128)(2,1)S(1)}, bf16[128,512]{1,0:T(8,128)(2,1)S(1)}, u32[]{:S(2)}, u32[]{:S(2)}) collective-permute-start(bf16[128,512]{1,0:T(8,128)(2,1)S(1)} %add_convert_fusion.1), channel_id=1, source_target_pairs={{0,16},{2,18},{4,20},{6,22},{8,24},{10,26},{12,28},{14,30},{16,0},... | collective-permute-start | bytes 393224 | tf_op jit(solution)/shard_map/ppermute | solution.py:318
  91.4 3.2 %collective-permute-start.13 = (bf16[128,512]{1,0:T(8,128)(2,1)S(1)}, bf16[128,512]{1,0:T(8,128)(2,1)S(1)}, u32[]{:S(2)}, u32[]{:S(2)}) collective-permute-start(bf16[128,512]{1,0:T(8,128)(2,1)S(1)} %collective-permute-done.12), channel_id=1, source_target_pairs={{0,4},{2,6},{4,0},{6,2},{8,12},{10,14},{12,8},{14,10},{16,20},{18,... | collective-permute-start | bytes 393224 | tf_op jit(solution)/shard_map/ppermute | solution.py:318
  97.7 1.7 %collective-permute-start.20 = (bf16[128,512]{1,0:T(8,128)(2,1)S(1)}, bf16[128,512]{1,0:T(8,128)(2,1)S(1)}, u32[]{:S(2)}, u32[]{:S(2)}) collective-permute-start(bf16[128,512]{1,0:T(8,128)(2,1)S(1)} %add_convert_fusion), channel_id=1, source_target_pairs={{0,2},{2,0},{4,6},{6,4},{8,10},{10,8},{12,14},{14,12},{16,18},{18,... | collective-permute-start | bytes 393224 | tf_op jit(solution)/shard_map/ppermute | solution.py:318
  100.8 2.1 %collective-permute-done.22 = bf16[128,512]{1,0:T(8,128)(2,1)S(1)} collective-permute-done((bf16[128,512]{1,0:T(8,128)(2,1)S(1)}, bf16[128,512]{1,0:T(8,128)(2,1)S(1)}, u32[]{:S(2)}, u32[]{:S(2)}) %collective-permute-start.22) | collective-permute-done | bytes 131104 | tf_op jit(solution)/shard_map/ppermute | solution.py:318
  104.9 1.6 %collective-permute-start.24 = (bf16[128,512]{1,0:T(8,128)(2,1)S(1)}, bf16[128,512]{1,0:T(8,128)(2,1)S(1)}, u32[]{:S(2)}, u32[]{:S(2)}) collective-permute-start(bf16[128,512]{1,0:T(8,128)(2,1)S(1)} %collective-permute-done.23), channel_id=1, source_target_pairs={{0,2},{2,0},{4,6},{6,4},{8,10},{10,8},{12,14},{14,12},{16,18},{18,... | collective-permute-start | bytes 393224 | tf_op jit(solution)/shard_map/ppermute | solution.py:318
  107.9 1.9 %collective-permute-done.26 = bf16[128,512]{1,0:T(8,128)(2,1)S(1)} collective-permute-done((bf16[128,512]{1,0:T(8,128)(2,1)S(1)}, bf16[128,512]{1,0:T(8,128)(2,1)S(1)}, u32[]{:S(2)}, u32[]{:S(2)}) %collective-permute-start.26) | collective-permute-done | bytes 131104 | tf_op jit(solution)/shard_map/ppermute | solution.py:318
  110.3 2.4 %shard_map.159 = f32[2048,512]{1,0:T(8,128)} custom-call(s32[1]{0:T(128)} %bitcast.me, bf16[2,128,512]{2,1,0:T(8,128)(2,1)S(1)} %pad_maximum_fusion.refs_0_, bf16[2,128,512]{2,1,0:T(8,128)(2,1)S(1)} %collective-permute-done.11.refs_1_, bf16[2,128,512]{2,1,0:T(8,128)(2,1)S(1)} %pad_maximum_fusion.1.refs_2_, ...), custom_call_target="tpu_custom_call" | custom-call | flops 4194304 | bytes 6291456 | tf_op jit(solution)/shard_map/pallas_call | solution.py:500
  (67 shorter events, 19.3 us)
Async XLA Ops:
  4.2 33.7 %all-to-all-start = ((bf16[16,264,128]{2,1,0:T(8,128)(2,1)}), bf16[16,264,128]{2,1,0:T(8,128)(2,1)}, u32[]{:S(2)}, u32[]{:S(2)}) async-start(bf16[16,264,128]{2,1,0:T(8,128)(2,1)} %shard_map.149), calls=%async_computation | async-start | bytes 2162688 | tf_op jit(solution)/shard_map/all_to_all | solution.py:398
  12.6 35.8 %collective-permute-start.1 = (bf16[256,512]{1,0:T(8,128)(2,1)}, bf16[256,512]{1,0:T(8,128)(2,1)}, u32[]{:S(2)}, u32[]{:S(2)}) collective-permute-start(bf16[256,512]{1,0:T(8,128)(2,1)} %refs_0_.1), channel_id=1, source_target_pairs={{0,4},{2,6},{4,0},{6,2},{8,12},{10,14},{12,8},{14,10},{16,20},{18,... | collective-permute-start | bytes 786440 | tf_op jit(solution)/shard_map/ppermute | solution.py:318
  14.4 34.0 %collective-permute-start = (bf16[256,512]{1,0:T(8,128)(2,1)}, bf16[256,512]{1,0:T(8,128)(2,1)}, u32[]{:S(2)}, u32[]{:S(2)}) collective-permute-start(bf16[256,512]{1,0:T(8,128)(2,1)} %refs_0_.1), channel_id=1, source_target_pairs={{0,2},{2,0},{4,6},{6,4},{8,10},{10,8},{12,14},{14,12},{16,18},{18,... | collective-permute-start | bytes 786440 | tf_op jit(solution)/shard_map/ppermute | solution.py:318
  15.9 32.5 %collective-permute-start.2 = (bf16[256,512]{1,0:T(8,128)(2,1)}, bf16[256,512]{1,0:T(8,128)(2,1)}, u32[]{:S(2)}, u32[]{:S(2)}) collective-permute-start(bf16[256,512]{1,0:T(8,128)(2,1)} %refs_0_.1), channel_id=1, source_target_pairs={{0,6},{2,4},{4,2},{6,0},{8,14},{10,12},{12,10},{14,8},{16,22},{18,... | collective-permute-start | bytes 786440 | tf_op jit(solution)/shard_map/ppermute | solution.py:318
  48.4 8.9 %collective-permute-start.3 = (bf16[128,512]{1,0:T(8,128)(2,1)}, bf16[128,512]{1,0:T(8,128)(2,1)S(1)}, u32[]{:S(2)}, u32[]{:S(2)}) collective-permute-start(bf16[128,512]{1,0:T(8,128)(2,1)} %get-tuple-element.40), channel_id=1, source_target_pairs={{0,2},{2,4},{4,6},{6,8},{8,10},{10,12},{12,14},{14,16},{16,18},{18... | collective-permute-start | bytes 393224 | tf_op jit(solution)/shard_map/ppermute | solution.py:436
  49.2 8.2 %collective-permute-start.4 = (bf16[128,512]{1,0:T(8,128)(2,1)}, bf16[128,512]{1,0:T(8,128)(2,1)S(1)}, u32[]{:S(2)}, u32[]{:S(2)}) collective-permute-start(bf16[128,512]{1,0:T(8,128)(2,1)} %get-tuple-element.41), channel_id=1, source_target_pairs={{2,0},{4,2},{6,4},{8,6},{10,8},{12,10},{14,12},{16,14},{18,16},{20... | collective-permute-start | bytes 393224 | tf_op jit(solution)/shard_map/ppermute | solution.py:437
  60.9 7.4 %collective-permute-start.6 = (bf16[256,256]{1,0:T(8,128)(2,1)S(1)}, bf16[256,256]{1,0:T(8,128)(2,1)S(1)}, u32[]{:S(2)}, u32[]{:S(2)}) collective-permute-start(bf16[256,256]{1,0:T(8,128)(2,1)S(1)} %get-tuple-element.56.refs_2_), channel_id=1, source_target_pairs={{0,4},{2,6},{4,0},{6,2},{8,12},{10,14},{12,8},{14,10},{16,20},{18,... | collective-permute-start | bytes 393224 | tf_op jit(solution)/shard_map/ppermute | solution.py:318
  64.4 5.9 %collective-permute-start.7 = (bf16[256,256]{1,0:T(8,128)(2,1)S(1)}, bf16[256,256]{1,0:T(8,128)(2,1)S(1)}, u32[]{:S(2)}, u32[]{:S(2)}) collective-permute-start(bf16[256,256]{1,0:T(8,128)(2,1)S(1)} %get-tuple-element.57.refs_3_), channel_id=1, source_target_pairs={{0,6},{2,4},{4,2},{6,0},{8,14},{10,12},{12,10},{14,8},{16,22},{18,... | collective-permute-start | bytes 393224 | tf_op jit(solution)/shard_map/ppermute | solution.py:318
  72.1 7.3 %collective-permute-start.15 = (bf16[256,256]{1,0:T(8,128)(2,1)S(1)}, bf16[256,256]{1,0:T(8,128)(2,1)S(1)}, u32[]{:S(2)}, u32[]{:S(2)}) collective-permute-start(bf16[256,256]{1,0:T(8,128)(2,1)S(1)} %get-tuple-element.64.refs_5_), channel_id=1, source_target_pairs={{0,2},{2,0},{4,6},{6,4},{8,10},{10,8},{12,14},{14,12},{16,18},{18,... | collective-permute-start | bytes 393224 | tf_op jit(solution)/shard_map/ppermute | solution.py:318
  72.1 7.2 %collective-permute-start.16 = (bf16[256,256]{1,0:T(8,128)(2,1)S(1)}, bf16[256,256]{1,0:T(8,128)(2,1)S(1)}, u32[]{:S(2)}, u32[]{:S(2)}) collective-permute-start(bf16[256,256]{1,0:T(8,128)(2,1)S(1)} %get-tuple-element.65.refs_6_), channel_id=1, source_target_pairs={{0,4},{2,6},{4,0},{6,2},{8,12},{10,14},{12,8},{14,10},{16,20},{18,... | collective-permute-start | bytes 393224 | tf_op jit(solution)/shard_map/ppermute | solution.py:318
  72.9 6.5 %collective-permute-start.17 = (bf16[256,256]{1,0:T(8,128)(2,1)S(1)}, bf16[256,256]{1,0:T(8,128)(2,1)S(1)}, u32[]{:S(2)}, u32[]{:S(2)}) collective-permute-start(bf16[256,256]{1,0:T(8,128)(2,1)S(1)} %get-tuple-element.66.refs_7_), channel_id=1, source_target_pairs={{0,6},{2,4},{4,2},{6,0},{8,14},{10,12},{12,10},{14,8},{16,22},{18,... | collective-permute-start | bytes 393224 | tf_op jit(solution)/shard_map/ppermute | solution.py:318
  76.4 8.8 %collective-permute-start.9 = (bf16[128,512]{1,0:T(8,128)(2,1)S(1)}, bf16[128,512]{1,0:T(8,128)(2,1)S(1)}, u32[]{:S(2)}, u32[]{:S(2)}) collective-permute-start(bf16[128,512]{1,0:T(8,128)(2,1)S(1)} %add_convert_fusion.3), channel_id=1, source_target_pairs={{0,16},{2,18},{4,20},{6,22},{8,24},{10,26},{12,28},{14,30},{16,0},... | collective-permute-start | bytes 393224 | tf_op jit(solution)/shard_map/ppermute | solution.py:318
  79.9 7.4 %collective-permute-start.18 = (bf16[128,512]{1,0:T(8,128)(2,1)S(1)}, bf16[128,512]{1,0:T(8,128)(2,1)S(1)}, u32[]{:S(2)}, u32[]{:S(2)}) collective-permute-start(bf16[128,512]{1,0:T(8,128)(2,1)S(1)} %get-tuple-element.71), channel_id=1, source_target_pairs={{0,8},{2,10},{4,12},{6,14},{8,0},{10,2},{12,4},{14,6},{16,24},{18,... | collective-permute-start | bytes 393224 | tf_op jit(solution)/shard_map/ppermute | solution.py:318
  85.2 6.2 %collective-permute-start.12 = (bf16[128,512]{1,0:T(8,128)(2,1)S(1)}, bf16[128,512]{1,0:T(8,128)(2,1)S(1)}, u32[]{:S(2)}, u32[]{:S(2)}) collective-permute-start(bf16[128,512]{1,0:T(8,128)(2,1)S(1)} %add_convert_fusion.2), channel_id=1, source_target_pairs={{0,8},{2,10},{4,12},{6,14},{8,0},{10,2},{12,4},{14,6},{16,24},{18,... | collective-permute-start | bytes 393224 | tf_op jit(solution)/shard_map/ppermute | solution.py:318
  87.3 7.4 %collective-permute-start.19 = (bf16[128,512]{1,0:T(8,128)(2,1)S(1)}, bf16[128,512]{1,0:T(8,128)(2,1)S(1)}, u32[]{:S(2)}, u32[]{:S(2)}) collective-permute-start(bf16[128,512]{1,0:T(8,128)(2,1)S(1)} %add_convert_fusion.1), channel_id=1, source_target_pairs={{0,16},{2,18},{4,20},{6,22},{8,24},{10,26},{12,28},{14,30},{16,0},... | collective-permute-start | bytes 393224 | tf_op jit(solution)/shard_map/ppermute | solution.py:318
  90.7 7.0 %collective-permute-start.10 = (bf16[128,512]{1,0:T(8,128)(2,1)S(1)}, bf16[128,512]{1,0:T(8,128)(2,1)S(1)}, u32[]{:S(2)}, u32[]{:S(2)}) collective-permute-start(bf16[128,512]{1,0:T(8,128)(2,1)S(1)} %add_convert_fusion.2), channel_id=1, source_target_pairs={{0,2},{2,0},{4,6},{6,4},{8,10},{10,8},{12,14},{14,12},{16,18},{18,... | collective-permute-start | bytes 393224 | tf_op jit(solution)/shard_map/ppermute | solution.py:318
  91.4 8.9 %collective-permute-start.13 = (bf16[128,512]{1,0:T(8,128)(2,1)S(1)}, bf16[128,512]{1,0:T(8,128)(2,1)S(1)}, u32[]{:S(2)}, u32[]{:S(2)}) collective-permute-start(bf16[128,512]{1,0:T(8,128)(2,1)S(1)} %collective-permute-done.12), channel_id=1, source_target_pairs={{0,4},{2,6},{4,0},{6,2},{8,12},{10,14},{12,8},{14,10},{16,20},{18,... | collective-permute-start | bytes 393224 | tf_op jit(solution)/shard_map/ppermute | solution.py:318
  95.9 7.1 %collective-permute-start.22 = (bf16[128,512]{1,0:T(8,128)(2,1)S(1)}, bf16[128,512]{1,0:T(8,128)(2,1)S(1)}, u32[]{:S(2)}, u32[]{:S(2)}) collective-permute-start(bf16[128,512]{1,0:T(8,128)(2,1)S(1)} %add_convert_fusion), channel_id=1, source_target_pairs={{0,6},{2,4},{4,2},{6,0},{8,14},{10,12},{12,10},{14,8},{16,22},{18,... | collective-permute-start | bytes 393224 | tf_op jit(solution)/shard_map/ppermute | solution.py:318
  96.5 7.4 %collective-permute-start.21 = (bf16[128,512]{1,0:T(8,128)(2,1)S(1)}, bf16[128,512]{1,0:T(8,128)(2,1)S(1)}, u32[]{:S(2)}, u32[]{:S(2)}) collective-permute-start(bf16[128,512]{1,0:T(8,128)(2,1)S(1)} %add_convert_fusion), channel_id=1, source_target_pairs={{0,4},{2,6},{4,0},{6,2},{8,12},{10,14},{12,8},{14,10},{16,20},{18,... | collective-permute-start | bytes 393224 | tf_op jit(solution)/shard_map/ppermute | solution.py:318
  97.7 7.2 %collective-permute-start.20 = (bf16[128,512]{1,0:T(8,128)(2,1)S(1)}, bf16[128,512]{1,0:T(8,128)(2,1)S(1)}, u32[]{:S(2)}, u32[]{:S(2)}) collective-permute-start(bf16[128,512]{1,0:T(8,128)(2,1)S(1)} %add_convert_fusion), channel_id=1, source_target_pairs={{0,2},{2,0},{4,6},{6,4},{8,10},{10,8},{12,14},{14,12},{16,18},{18,... | collective-permute-start | bytes 393224 | tf_op jit(solution)/shard_map/ppermute | solution.py:318
  100.3 10.0 %collective-permute-start.11 = (bf16[2,128,512]{2,1,0:T(8,128)(2,1)S(1)}, bf16[2,128,512]{2,1,0:T(8,128)(2,1)S(1)}, u32[]{:S(2)}, u32[]{:S(2)}) collective-permute-start(bf16[2,128,512]{2,1,0:T(8,128)(2,1)S(1)} %pad_maximum_fusion.refs_0_), channel_id=1, source_target_pairs={{0,4},{2,6},{4,0},{6,2},{8,12},{10,14},{12,8},{14,10},{16,20},{18,... | collective-permute-start | bytes 786440 | tf_op jit(solution)/shard_map/ppermute | solution.py:318
  100.4 9.9 %collective-permute-start.14 = (bf16[2,128,512]{2,1,0:T(8,128)(2,1)S(1)}, bf16[2,128,512]{2,1,0:T(8,128)(2,1)S(1)}, u32[]{:S(2)}, u32[]{:S(2)}) collective-permute-start(bf16[2,128,512]{2,1,0:T(8,128)(2,1)S(1)} %pad_maximum_fusion.1.refs_2_), channel_id=1, source_target_pairs={{0,2},{2,0},{4,6},{6,4},{8,10},{10,8},{12,14},{14,12},{16,18},{18,... | collective-permute-start | bytes 786440 | tf_op jit(solution)/shard_map/ppermute | solution.py:318
  102.9 6.9 %collective-permute-start.26 = (bf16[128,512]{1,0:T(8,128)(2,1)S(1)}, bf16[128,512]{1,0:T(8,128)(2,1)S(1)}, u32[]{:S(2)}, u32[]{:S(2)}) collective-permute-start(bf16[128,512]{1,0:T(8,128)(2,1)S(1)} %collective-permute-done.23), channel_id=1, source_target_pairs={{0,6},{2,4},{4,2},{6,0},{8,14},{10,12},{12,10},{14,8},{16,22},{18,... | collective-permute-start | bytes 393224 | tf_op jit(solution)/shard_map/ppermute | solution.py:318
  104.0 6.4 %collective-permute-start.25 = (bf16[128,512]{1,0:T(8,128)(2,1)S(1)}, bf16[128,512]{1,0:T(8,128)(2,1)S(1)}, u32[]{:S(2)}, u32[]{:S(2)}) collective-permute-start(bf16[128,512]{1,0:T(8,128)(2,1)S(1)} %collective-permute-done.23), channel_id=1, source_target_pairs={{0,4},{2,6},{4,0},{6,2},{8,12},{10,14},{12,8},{14,10},{16,20},{18,... | collective-permute-start | bytes 393224 | tf_op jit(solution)/shard_map/ppermute | solution.py:318
  (13 other events, 141.9 us)

commit v6 on v5

--- a/solution.py
+++ b/solution.py
@@ -480,7 +480,6 @@
         received = [[h[0]] + [flipped(h[j], j) for j in range(1, PLANE)] for h in hidden]
     part = hidden_width // tiles
     if fast:
-        received[0][0], received[1][0] = lax.optimization_barrier((received[0][0], received[1][0]))
         half = shape((step // 2, width), F32)
         pieces, order = [], []
         for c in range(CHUNKS):

time: 113 us -> 112 us (level)
  waiting for transfers between devices: 36.4 us -> 33.7 us
  starting transfers between devices: 49.4 us -> 51.3 us
    ppermute x25, waiting for transfers between devices: 14.9 us -> 12.3 us  [flipped(): lax.ppermute(value, 'tile', [(i, i ^ k) for i in range(PLANE * PLANE)])]
    ppermute x25, starting transfers between devices: 35.3 us -> 37.2 us  [flipped(): lax.ppermute(value, 'tile', [(i, i ^ k) for i in range(PLANE * PLANE)])]
where the time goes in v6:
time: 112 us
  starting transfers between devices  51.3 us (46%)
  waiting for transfers between devices  33.7 us (30%)
  Pallas kernels  24.3 us (22%)
  local copies, waits for them, and re-layouts  1.69 us (2%)
    ppermute x25, starting transfers between devices, flipped(): lax.ppermute(value, 'tile', [(i, i ^ k) for i in range(PLANE * PLANE)])  37.2 us
    all_to_all x1, waiting for transfers between devices, on_device(): lax.all_to_all(packed, 'tile', split_axis=0, concat_axis=0, tiled=True)  20.7 us
    ppermute x25, waiting for transfers between devices, flipped(): lax.ppermute(value, 'tile', [(i, i ^ k) for i in range(PLANE * PLANE)])  12.3 us
    pallas_call x1, Pallas kernels, on_device(): call(functools.partial(cross_kernel, cap=cap, inputs=len(operands)), (str...  10.5 us
    all_to_all x1, starting transfers between devices, on_device(): lax.all_to_all(packed, 'tile', split_axis=0, concat_axis=0, tiled=True)  8.37 us
    ppermute x1, starting transfers between devices, on_device(): after = lax.ppermute(top, 'tile', backward)  4.93 us
    pallas_call x1, Pallas kernels, on_device(): call(functools.partial(pack_kernel, tiles=tiles, cap=cap), shape((tiles,...  3.52 us
    pallas_call x1, Pallas kernels, on_device(): call(functools.partial(clip_kernel, order=order, unit=step // 2), shape((...  2.43 us
  transfers between devices with their start and end apart: 28, of which 12 were waited for; matrix products, arithmetic and copies ran while one was open for 0% of the time, Pallas kernels for 13%

profile of v6, /device:TPU:0, one launch (start us, length us, event | category | flops | bytes accessed | tf_op | source)
XLA Modules:
  0.0 112.2 jit_solution(3106017750216261092)
XLA Ops:
  0.7 3.5 %shard_map.149 = bf16[16,264,128]{2,1,0:T(8,128)(2,1)} custom-call(s32[1,1024]{1,0:T(1,128)} %bitcast.28, s32[1,1024]{1,0:T(1,128)} %bitcast.29, s32[1,1024]{1,0:T(1,128)} %bitcast.30, bf16[32,256]{1,0:T(8,128)(2,1)} %refs_3_.2, bf16[1024,256]{1,0:T(8,128)(2,1)} %refs_4_.2), custom_call_target="tpu_custom_call" | custom-call | flops 1073741824 | bytes 1572864 | tf_op jit(solution)/shard_map/pallas_call | solution.py:371
  4.2 8.4 %all-to-all-start = ((bf16[16,264,128]{2,1,0:T(8,128)(2,1)}), bf16[16,264,128]{2,1,0:T(8,128)(2,1)}, u32[]{:S(2)}, u32[]{:S(2)}) async-start(bf16[16,264,128]{2,1,0:T(8,128)(2,1)} %shard_map.149), calls=%async_computation | async-start | bytes 2162688 | tf_op jit(solution)/shard_map/all_to_all | solution.py:398
  12.6 1.9 %collective-permute-start.1 = (bf16[256,512]{1,0:T(8,128)(2,1)}, bf16[256,512]{1,0:T(8,128)(2,1)}, u32[]{:S(2)}, u32[]{:S(2)}) collective-permute-start(bf16[256,512]{1,0:T(8,128)(2,1)} %refs_0_.1), channel_id=1, source_target_pairs={{0,4},{2,6},{4,0},{6,2},{8,12},{10,14},{12,8},{14,10},{16,20},{18,... | collective-permute-start | bytes 786440 | tf_op jit(solution)/shard_map/ppermute | solution.py:318
  14.4 1.5 %collective-permute-start = (bf16[256,512]{1,0:T(8,128)(2,1)}, bf16[256,512]{1,0:T(8,128)(2,1)}, u32[]{:S(2)}, u32[]{:S(2)}) collective-permute-start(bf16[256,512]{1,0:T(8,128)(2,1)} %refs_0_.1), channel_id=1, source_target_pairs={{0,2},{2,0},{4,6},{6,4},{8,10},{10,8},{12,14},{14,12},{16,18},{18,... | collective-permute-start | bytes 786440 | tf_op jit(solution)/shard_map/ppermute | solution.py:318
  17.2 20.7 %all-to-all-done.refs_0_ = bf16[16,264,128]{2,1,0:T(8,128)(2,1)} async-done(((bf16[16,264,128]{2,1,0:T(8,128)(2,1)}), bf16[16,264,128]{2,1,0:T(8,128)(2,1)}, u32[]{:S(2)}, u32[]{:S(2)}) %all-to-all-start) | async-done | bytes 1081376 | tf_op jit(solution)/shard_map/all_to_all | solution.py:398
  37.9 10.5 %shard_map.151 = (f32[256,512]{1,0:T(8,128)}, bf16[256,512]{1,0:T(8,128)(2,1)}, bf16[128,512]{1,0:T(8,128)(2,1)}, bf16[128,512]{1,0:T(8,128)(2,1)}) custom-call(bf16[16,264,128]{2,1,0:T(8,128)(2,1)} %all-to-all-done.refs_0_, bf16[256,1024]{1,0:T(8,128)(2,1)} %refs_1_.1, bf16[256,512]{1,0:T(8,128)(2,1)} %copy-done.7, bf16[256,512]{1,0:T(8,128)(2,1)} %refs_3_.3, ...), custom_call_target="tpu_custom_call" | custom-call | flops 2147483648 | bytes 2621440 | tf_op jit(solution)/shard_map/pallas_call | solution.py:411
  49.2 4.9 %collective-permute-start.4 = (bf16[128,512]{1,0:T(8,128)(2,1)}, bf16[128,512]{1,0:T(8,128)(2,1)S(1)}, u32[]{:S(2)}, u32[]{:S(2)}) collective-permute-start(bf16[128,512]{1,0:T(8,128)(2,1)} %get-tuple-element.39), channel_id=1, source_target_pairs={{2,0},{4,2},{6,4},{8,6},{10,8},{12,10},{14,12},{16,14},{18,16},{20... | collective-permute-start | bytes 393224 | tf_op jit(solution)/shard_map/ppermute | solution.py:437
  55.1 1.5 %shard_map.152 = (bf16[256,512]{1,0:T(8,128)(2,1)S(1)}, f32[256,512]{1,0:T(8,128)S(1)}, f32[256,512]{1,0:T(8,128)S(1)}, f32[256,512]{1,0:T(8,128)S(1)}, bf16[256...) custom-call(bf16[512,1536]{1,0:T(8,128)(2,1)S(1)} %copy-done.1, ...), custom_call_target="tpu_custom_call" | custom-call | flops 536870912 | bytes 3670016 | tf_op jit(solution)/shard_map/pallas_call | solution.py:439
  57.4 2.3 %shard_map.153 = (f32[256,512]{1,0:T(8,128)S(1)}, bf16[256,512]{1,0:T(8,128)(2,1)S(1)}) custom-call(f32[256,512]{1,0:T(8,128)S(1)} %copy-done.4, bf16[128,512]{1,0:T(8,128)(2,1)S(1)} %collective-permute-done.3.before, bf16[128,512]{1,0:T(8,128)(2,1)S(1)} %collective-permute-done.4.after, bf16[512,1536]{1,0:T(8,128)(2,1)S(1)} %copy-done.1, ...), custom_call_target="tpu_custom_call" | custom-call | flops 469762048 | bytes 5242880 | tf_op jit(solution)/shard_map/pallas_call | solution.py:455
  60.9 3.5 %collective-permute-start.6 = (bf16[256,256]{1,0:T(8,128)(2,1)S(1)}, bf16[256,256]{1,0:T(8,128)(2,1)S(1)}, u32[]{:S(2)}, u32[]{:S(2)}) collective-permute-start(bf16[256,256]{1,0:T(8,128)(2,1)S(1)} %get-tuple-element.52.refs_2_), channel_id=1, source_target_pairs={{0,4},{2,6},{4,0},{6,2},{8,12},{10,14},{12,8},{14,10},{16,20},{18,... | collective-permute-start | bytes 393224 | tf_op jit(solution)/shard_map/ppermute | solution.py:318
  65.6 2.7 %collective-permute-done.6.refs_2_ = bf16[256,256]{1,0:T(8,128)(2,1)S(1)} collective-permute-done((bf16[256,256]{1,0:T(8,128)(2,1)S(1)}, bf16[256,256]{1,0:T(8,128)(2,1)S(1)}, u32[]{:S(2)}, u32[]{:S(2)}) %collective-permute-start.6) | collective-permute-done | bytes 131104 | tf_op jit(solution)/shard_map/ppermute | solution.py:318
  68.3 1.9 %collective-permute-done.7.refs_3_ = bf16[256,256]{1,0:T(8,128)(2,1)S(1)} collective-permute-done((bf16[256,256]{1,0:T(8,128)(2,1)S(1)}, bf16[256,256]{1,0:T(8,128)(2,1)S(1)}, u32[]{:S(2)}, u32[]{:S(2)}) %collective-permute-start.7) | collective-permute-done | bytes 131104 | tf_op jit(solution)/shard_map/ppermute | solution.py:318
  73.6 2.6 %collective-permute-start.17 = (bf16[256,256]{1,0:T(8,128)(2,1)S(1)}, bf16[256,256]{1,0:T(8,128)(2,1)S(1)}, u32[]{:S(2)}, u32[]{:S(2)}) collective-permute-start(bf16[256,256]{1,0:T(8,128)(2,1)S(1)} %get-tuple-element.63.refs_7_), channel_id=1, source_target_pairs={{0,6},{2,4},{4,2},{6,0},{8,14},{10,12},{12,10},{14,8},{16,22},{18,... | collective-permute-start | bytes 393224 | tf_op jit(solution)/shard_map/ppermute | solution.py:318
  76.4 2.9 %collective-permute-start.9 = (bf16[128,512]{1,0:T(8,128)(2,1)S(1)}, bf16[128,512]{1,0:T(8,128)(2,1)S(1)}, u32[]{:S(2)}, u32[]{:S(2)}) collective-permute-start(bf16[128,512]{1,0:T(8,128)(2,1)S(1)} %add_convert_fusion.3), channel_id=1, source_target_pairs={{0,16},{2,18},{4,20},{6,22},{8,24},{10,26},{12,28},{14,30},{16,0},... | collective-permute-start | bytes 393224 | tf_op jit(solution)/shard_map/ppermute | solution.py:318
  80.0 2.4 %collective-permute-start.18 = (bf16[128,512]{1,0:T(8,128)(2,1)S(1)}, bf16[128,512]{1,0:T(8,128)(2,1)S(1)}, u32[]{:S(2)}, u32[]{:S(2)}) collective-permute-start(bf16[128,512]{1,0:T(8,128)(2,1)S(1)} %get-tuple-element.67), channel_id=1, source_target_pairs={{0,8},{2,10},{4,12},{6,14},{8,0},{10,2},{12,4},{14,6},{16,24},{18,... | collective-permute-start | bytes 393224 | tf_op jit(solution)/shard_map/ppermute | solution.py:318
  82.9 4.3 %collective-permute-start.12 = (bf16[128,512]{1,0:T(8,128)(2,1)S(1)}, bf16[128,512]{1,0:T(8,128)(2,1)S(1)}, u32[]{:S(2)}, u32[]{:S(2)}) collective-permute-start(bf16[128,512]{1,0:T(8,128)(2,1)S(1)} %add_convert_fusion.2), channel_id=1, source_target_pairs={{0,8},{2,10},{4,12},{6,14},{8,0},{10,2},{12,4},{14,6},{16,24},{18,... | collective-permute-start | bytes 393224 | tf_op jit(solution)/shard_map/ppermute | solution.py:318
  87.2 3.4 %collective-permute-start.19 = (bf16[128,512]{1,0:T(8,128)(2,1)S(1)}, bf16[128,512]{1,0:T(8,128)(2,1)S(1)}, u32[]{:S(2)}, u32[]{:S(2)}) collective-permute-start(bf16[128,512]{1,0:T(8,128)(2,1)S(1)} %add_convert_fusion.1), channel_id=1, source_target_pairs={{0,16},{2,18},{4,20},{6,22},{8,24},{10,26},{12,28},{14,30},{16,0},... | collective-permute-start | bytes 393224 | tf_op jit(solution)/shard_map/ppermute | solution.py:318
  92.1 1.6 %collective-permute-done.19 = bf16[128,512]{1,0:T(8,128)(2,1)S(1)} collective-permute-done((bf16[128,512]{1,0:T(8,128)(2,1)S(1)}, bf16[128,512]{1,0:T(8,128)(2,1)S(1)}, u32[]{:S(2)}, u32[]{:S(2)}) %collective-permute-start.19) | collective-permute-done | bytes 131104 | tf_op jit(solution)/shard_map/ppermute | solution.py:318
  93.6 2.1 %collective-permute-start.23 = (bf16[128,512]{1,0:T(8,128)(2,1)S(1)}, bf16[128,512]{1,0:T(8,128)(2,1)S(1)}, u32[]{:S(2)}, u32[]{:S(2)}) collective-permute-start(bf16[128,512]{1,0:T(8,128)(2,1)S(1)} %add_convert_fusion), channel_id=1, source_target_pairs={{0,8},{2,10},{4,12},{6,14},{8,0},{10,2},{12,4},{14,6},{16,24},{18,... | collective-permute-start | bytes 393224 | tf_op jit(solution)/shard_map/ppermute | solution.py:318
  95.8 1.9 %collective-permute-start.21 = (bf16[128,512]{1,0:T(8,128)(2,1)S(1)}, bf16[128,512]{1,0:T(8,128)(2,1)S(1)}, u32[]{:S(2)}, u32[]{:S(2)}) collective-permute-start(bf16[128,512]{1,0:T(8,128)(2,1)S(1)} %add_convert_fusion), channel_id=1, source_target_pairs={{0,4},{2,6},{4,0},{6,2},{8,12},{10,14},{12,8},{14,10},{16,20},{18,... | collective-permute-start | bytes 393224 | tf_op jit(solution)/shard_map/ppermute | solution.py:318
  97.6 1.6 %collective-permute-start.20 = (bf16[128,512]{1,0:T(8,128)(2,1)S(1)}, bf16[128,512]{1,0:T(8,128)(2,1)S(1)}, u32[]{:S(2)}, u32[]{:S(2)}) collective-permute-start(bf16[128,512]{1,0:T(8,128)(2,1)S(1)} %add_convert_fusion), channel_id=1, source_target_pairs={{0,2},{2,0},{4,6},{6,4},{8,10},{10,8},{12,14},{14,12},{16,18},{18,... | collective-permute-start | bytes 393224 | tf_op jit(solution)/shard_map/ppermute | solution.py:318
  100.6 2.1 %collective-permute-done.22 = bf16[128,512]{1,0:T(8,128)(2,1)S(1)} collective-permute-done((bf16[128,512]{1,0:T(8,128)(2,1)S(1)}, bf16[128,512]{1,0:T(8,128)(2,1)S(1)}, u32[]{:S(2)}, u32[]{:S(2)}) %collective-permute-start.22) | collective-permute-done | bytes 131104 | tf_op jit(solution)/shard_map/ppermute | solution.py:318
  104.2 2.0 %collective-permute-start.24 = (bf16[128,512]{1,0:T(8,128)(2,1)S(1)}, bf16[128,512]{1,0:T(8,128)(2,1)S(1)}, u32[]{:S(2)}, u32[]{:S(2)}) collective-permute-start(bf16[128,512]{1,0:T(8,128)(2,1)S(1)} %collective-permute-done.23), channel_id=1, source_target_pairs={{0,2},{2,0},{4,6},{6,4},{8,10},{10,8},{12,14},{14,12},{16,18},{18,... | collective-permute-start | bytes 393224 | tf_op jit(solution)/shard_map/ppermute | solution.py:318
  109.6 2.4 %shard_map.159 = f32[2048,512]{1,0:T(8,128)} custom-call(s32[1]{0:T(128)} %bitcast.me, bf16[2,128,512]{2,1,0:T(8,128)(2,1)S(1)} %pad_maximum_fusion.refs_0_, bf16[2,128,512]{2,1,0:T(8,128)(2,1)S(1)} %collective-permute-done.11.refs_1_, bf16[2,128,512]{2,1,0:T(8,128)(2,1)S(1)} %pad_maximum_fusion.1.refs_2_, ...), custom_call_target="tpu_custom_call" | custom-call | flops 4194304 | bytes 6291456 | tf_op jit(solution)/shard_map/pallas_call | solution.py:499
  (67 shorter events, 18.6 us)
Async XLA Ops:
  4.2 33.7 %all-to-all-start = ((bf16[16,264,128]{2,1,0:T(8,128)(2,1)}), bf16[16,264,128]{2,1,0:T(8,128)(2,1)}, u32[]{:S(2)}, u32[]{:S(2)}) async-start(bf16[16,264,128]{2,1,0:T(8,128)(2,1)} %shard_map.149), calls=%async_computation | async-start | bytes 2162688 | tf_op jit(solution)/shard_map/all_to_all | solution.py:398
  12.6 35.8 %collective-permute-start.1 = (bf16[256,512]{1,0:T(8,128)(2,1)}, bf16[256,512]{1,0:T(8,128)(2,1)}, u32[]{:S(2)}, u32[]{:S(2)}) collective-permute-start(bf16[256,512]{1,0:T(8,128)(2,1)} %refs_0_.1), channel_id=1, source_target_pairs={{0,4},{2,6},{4,0},{6,2},{8,12},{10,14},{12,8},{14,10},{16,20},{18,... | collective-permute-start | bytes 786440 | tf_op jit(solution)/shard_map/ppermute | solution.py:318
  14.4 34.0 %collective-permute-start = (bf16[256,512]{1,0:T(8,128)(2,1)}, bf16[256,512]{1,0:T(8,128)(2,1)}, u32[]{:S(2)}, u32[]{:S(2)}) collective-permute-start(bf16[256,512]{1,0:T(8,128)(2,1)} %refs_0_.1), channel_id=1, source_target_pairs={{0,2},{2,0},{4,6},{6,4},{8,10},{10,8},{12,14},{14,12},{16,18},{18,... | collective-permute-start | bytes 786440 | tf_op jit(solution)/shard_map/ppermute | solution.py:318
  15.9 32.5 %collective-permute-start.2 = (bf16[256,512]{1,0:T(8,128)(2,1)}, bf16[256,512]{1,0:T(8,128)(2,1)}, u32[]{:S(2)}, u32[]{:S(2)}) collective-permute-start(bf16[256,512]{1,0:T(8,128)(2,1)} %refs_0_.1), channel_id=1, source_target_pairs={{0,6},{2,4},{4,2},{6,0},{8,14},{10,12},{12,10},{14,8},{16,22},{18,... | collective-permute-start | bytes 786440 | tf_op jit(solution)/shard_map/ppermute | solution.py:318
  48.4 8.9 %collective-permute-start.3 = (bf16[128,512]{1,0:T(8,128)(2,1)}, bf16[128,512]{1,0:T(8,128)(2,1)S(1)}, u32[]{:S(2)}, u32[]{:S(2)}) collective-permute-start(bf16[128,512]{1,0:T(8,128)(2,1)} %get-tuple-element.38), channel_id=1, source_target_pairs={{0,2},{2,4},{4,6},{6,8},{8,10},{10,12},{12,14},{14,16},{16,18},{18... | collective-permute-start | bytes 393224 | tf_op jit(solution)/shard_map/ppermute | solution.py:436
  49.2 8.2 %collective-permute-start.4 = (bf16[128,512]{1,0:T(8,128)(2,1)}, bf16[128,512]{1,0:T(8,128)(2,1)S(1)}, u32[]{:S(2)}, u32[]{:S(2)}) collective-permute-start(bf16[128,512]{1,0:T(8,128)(2,1)} %get-tuple-element.39), channel_id=1, source_target_pairs={{2,0},{4,2},{6,4},{8,6},{10,8},{12,10},{14,12},{16,14},{18,16},{20... | collective-permute-start | bytes 393224 | tf_op jit(solution)/shard_map/ppermute | solution.py:437
  60.9 7.4 %collective-permute-start.6 = (bf16[256,256]{1,0:T(8,128)(2,1)S(1)}, bf16[256,256]{1,0:T(8,128)(2,1)S(1)}, u32[]{:S(2)}, u32[]{:S(2)}) collective-permute-start(bf16[256,256]{1,0:T(8,128)(2,1)S(1)} %get-tuple-element.52.refs_2_), channel_id=1, source_target_pairs={{0,4},{2,6},{4,0},{6,2},{8,12},{10,14},{12,8},{14,10},{16,20},{18,... | collective-permute-start | bytes 393224 | tf_op jit(solution)/shard_map/ppermute | solution.py:318
  64.4 5.9 %collective-permute-start.7 = (bf16[256,256]{1,0:T(8,128)(2,1)S(1)}, bf16[256,256]{1,0:T(8,128)(2,1)S(1)}, u32[]{:S(2)}, u32[]{:S(2)}) collective-permute-start(bf16[256,256]{1,0:T(8,128)(2,1)S(1)} %get-tuple-element.53.refs_3_), channel_id=1, source_target_pairs={{0,6},{2,4},{4,2},{6,0},{8,14},{10,12},{12,10},{14,8},{16,22},{18,... | collective-permute-start | bytes 393224 | tf_op jit(solution)/shard_map/ppermute | solution.py:318
  72.7 6.6 %collective-permute-start.15 = (bf16[256,256]{1,0:T(8,128)(2,1)S(1)}, bf16[256,256]{1,0:T(8,128)(2,1)S(1)}, u32[]{:S(2)}, u32[]{:S(2)}) collective-permute-start(bf16[256,256]{1,0:T(8,128)(2,1)S(1)} %get-tuple-element.61.refs_5_), channel_id=1, source_target_pairs={{0,2},{2,0},{4,6},{6,4},{8,10},{10,8},{12,14},{14,12},{16,18},{18,... | collective-permute-start | bytes 393224 | tf_op jit(solution)/shard_map/ppermute | solution.py:318
  72.8 6.4 %collective-permute-start.16 = (bf16[256,256]{1,0:T(8,128)(2,1)S(1)}, bf16[256,256]{1,0:T(8,128)(2,1)S(1)}, u32[]{:S(2)}, u32[]{:S(2)}) collective-permute-start(bf16[256,256]{1,0:T(8,128)(2,1)S(1)} %get-tuple-element.62.refs_6_), channel_id=1, source_target_pairs={{0,4},{2,6},{4,0},{6,2},{8,12},{10,14},{12,8},{14,10},{16,20},{18,... | collective-permute-start | bytes 393224 | tf_op jit(solution)/shard_map/ppermute | solution.py:318
  76.4 6.5 %collective-permute-start.9 = (bf16[128,512]{1,0:T(8,128)(2,1)S(1)}, bf16[128,512]{1,0:T(8,128)(2,1)S(1)}, u32[]{:S(2)}, u32[]{:S(2)}) collective-permute-start(bf16[128,512]{1,0:T(8,128)(2,1)S(1)} %add_convert_fusion.3), channel_id=1, source_target_pairs={{0,16},{2,18},{4,20},{6,22},{8,24},{10,26},{12,28},{14,30},{16,0},... | collective-permute-start | bytes 393224 | tf_op jit(solution)/shard_map/ppermute | solution.py:318
  80.0 7.2 %collective-permute-start.18 = (bf16[128,512]{1,0:T(8,128)(2,1)S(1)}, bf16[128,512]{1,0:T(8,128)(2,1)S(1)}, u32[]{:S(2)}, u32[]{:S(2)}) collective-permute-start(bf16[128,512]{1,0:T(8,128)(2,1)S(1)} %get-tuple-element.67), channel_id=1, source_target_pairs={{0,8},{2,10},{4,12},{6,14},{8,0},{10,2},{12,4},{14,6},{16,24},{18,... | collective-permute-start | bytes 393224 | tf_op jit(solution)/shard_map/ppermute | solution.py:318
  82.9 8.1 %collective-permute-start.12 = (bf16[128,512]{1,0:T(8,128)(2,1)S(1)}, bf16[128,512]{1,0:T(8,128)(2,1)S(1)}, u32[]{:S(2)}, u32[]{:S(2)}) collective-permute-start(bf16[128,512]{1,0:T(8,128)(2,1)S(1)} %add_convert_fusion.2), channel_id=1, source_target_pairs={{0,8},{2,10},{4,12},{6,14},{8,0},{10,2},{12,4},{14,6},{16,24},{18,... | collective-permute-start | bytes 393224 | tf_op jit(solution)/shard_map/ppermute | solution.py:318
  87.2 6.4 %collective-permute-start.19 = (bf16[128,512]{1,0:T(8,128)(2,1)S(1)}, bf16[128,512]{1,0:T(8,128)(2,1)S(1)}, u32[]{:S(2)}, u32[]{:S(2)}) collective-permute-start(bf16[128,512]{1,0:T(8,128)(2,1)S(1)} %add_convert_fusion.1), channel_id=1, source_target_pairs={{0,16},{2,18},{4,20},{6,22},{8,24},{10,26},{12,28},{14,30},{16,0},... | collective-permute-start | bytes 393224 | tf_op jit(solution)/shard_map/ppermute | solution.py:318
  90.7 7.0 %collective-permute-start.10 = (bf16[128,512]{1,0:T(8,128)(2,1)S(1)}, bf16[128,512]{1,0:T(8,128)(2,1)S(1)}, u32[]{:S(2)}, u32[]{:S(2)}) collective-permute-start(bf16[128,512]{1,0:T(8,128)(2,1)S(1)} %add_convert_fusion.2), channel_id=1, source_target_pairs={{0,2},{2,0},{4,6},{6,4},{8,10},{10,8},{12,14},{14,12},{16,18},{18,... | collective-permute-start | bytes 393224 | tf_op jit(solution)/shard_map/ppermute | solution.py:318
  91.0 8.3 %collective-permute-start.13 = (bf16[128,512]{1,0:T(8,128)(2,1)S(1)}, bf16[128,512]{1,0:T(8,128)(2,1)S(1)}, u32[]{:S(2)}, u32[]{:S(2)}) collective-permute-start(bf16[128,512]{1,0:T(8,128)(2,1)S(1)} %collective-permute-done.12), channel_id=1, source_target_pairs={{0,4},{2,6},{4,0},{6,2},{8,12},{10,14},{12,8},{14,10},{16,20},{18,... | collective-permute-start | bytes 393224 | tf_op jit(solution)/shard_map/ppermute | solution.py:318
  93.6 6.1 %collective-permute-start.23 = (bf16[128,512]{1,0:T(8,128)(2,1)S(1)}, bf16[128,512]{1,0:T(8,128)(2,1)S(1)}, u32[]{:S(2)}, u32[]{:S(2)}) collective-permute-start(bf16[128,512]{1,0:T(8,128)(2,1)S(1)} %add_convert_fusion), channel_id=1, source_target_pairs={{0,8},{2,10},{4,12},{6,14},{8,0},{10,2},{12,4},{14,6},{16,24},{18,... | collective-permute-start | bytes 393224 | tf_op jit(solution)/shard_map/ppermute | solution.py:318
  95.8 6.9 %collective-permute-start.22 = (bf16[128,512]{1,0:T(8,128)(2,1)S(1)}, bf16[128,512]{1,0:T(8,128)(2,1)S(1)}, u32[]{:S(2)}, u32[]{:S(2)}) collective-permute-start(bf16[128,512]{1,0:T(8,128)(2,1)S(1)} %add_convert_fusion), channel_id=1, source_target_pairs={{0,6},{2,4},{4,2},{6,0},{8,14},{10,12},{12,10},{14,8},{16,22},{18,... | collective-permute-start | bytes 393224 | tf_op jit(solution)/shard_map/ppermute | solution.py:318
  95.8 7.4 %collective-permute-start.21 = (bf16[128,512]{1,0:T(8,128)(2,1)S(1)}, bf16[128,512]{1,0:T(8,128)(2,1)S(1)}, u32[]{:S(2)}, u32[]{:S(2)}) collective-permute-start(bf16[128,512]{1,0:T(8,128)(2,1)S(1)} %add_convert_fusion), channel_id=1, source_target_pairs={{0,4},{2,6},{4,0},{6,2},{8,12},{10,14},{12,8},{14,10},{16,20},{18,... | collective-permute-start | bytes 393224 | tf_op jit(solution)/shard_map/ppermute | solution.py:318
  97.6 6.5 %collective-permute-start.20 = (bf16[128,512]{1,0:T(8,128)(2,1)S(1)}, bf16[128,512]{1,0:T(8,128)(2,1)S(1)}, u32[]{:S(2)}, u32[]{:S(2)}) collective-permute-start(bf16[128,512]{1,0:T(8,128)(2,1)S(1)} %add_convert_fusion), channel_id=1, source_target_pairs={{0,2},{2,0},{4,6},{6,4},{8,10},{10,8},{12,14},{14,12},{16,18},{18,... | collective-permute-start | bytes 393224 | tf_op jit(solution)/shard_map/ppermute | solution.py:318
  99.3 10.2 %collective-permute-start.11 = (bf16[2,128,512]{2,1,0:T(8,128)(2,1)S(1)}, bf16[2,128,512]{2,1,0:T(8,128)(2,1)S(1)}, u32[]{:S(2)}, u32[]{:S(2)}) collective-permute-start(bf16[2,128,512]{2,1,0:T(8,128)(2,1)S(1)} %pad_maximum_fusion.refs_0_), channel_id=1, source_target_pairs={{0,4},{2,6},{4,0},{6,2},{8,12},{10,14},{12,8},{14,10},{16,20},{18,... | collective-permute-start | bytes 786440 | tf_op jit(solution)/shard_map/ppermute | solution.py:318
  99.8 9.8 %collective-permute-start.14 = (bf16[2,128,512]{2,1,0:T(8,128)(2,1)S(1)}, bf16[2,128,512]{2,1,0:T(8,128)(2,1)S(1)}, u32[]{:S(2)}, u32[]{:S(2)}) collective-permute-start(bf16[2,128,512]{2,1,0:T(8,128)(2,1)S(1)} %pad_maximum_fusion.1.refs_2_), channel_id=1, source_target_pairs={{0,2},{2,0},{4,6},{6,4},{8,10},{10,8},{12,14},{14,12},{16,18},{18,... | collective-permute-start | bytes 786440 | tf_op jit(solution)/shard_map/ppermute | solution.py:318
  102.7 6.1 %collective-permute-start.26 = (bf16[128,512]{1,0:T(8,128)(2,1)S(1)}, bf16[128,512]{1,0:T(8,128)(2,1)S(1)}, u32[]{:S(2)}, u32[]{:S(2)}) collective-permute-start(bf16[128,512]{1,0:T(8,128)(2,1)S(1)} %collective-permute-done.23), channel_id=1, source_target_pairs={{0,6},{2,4},{4,2},{6,0},{8,14},{10,12},{12,10},{14,8},{16,22},{18,... | collective-permute-start | bytes 393224 | tf_op jit(solution)/shard_map/ppermute | solution.py:318
  103.2 6.4 %collective-permute-start.25 = (bf16[128,512]{1,0:T(8,128)(2,1)S(1)}, bf16[128,512]{1,0:T(8,128)(2,1)S(1)}, u32[]{:S(2)}, u32[]{:S(2)}) collective-permute-start(bf16[128,512]{1,0:T(8,128)(2,1)S(1)} %collective-permute-done.23), channel_id=1, source_target_pairs={{0,4},{2,6},{4,0},{6,2},{8,12},{10,14},{12,8},{14,10},{16,20},{18,... | collective-permute-start | bytes 393224 | tf_op jit(solution)/shard_map/ppermute | solution.py:318
  (13 other events, 141.8 us)

commit v7 on v6

--- a/solution.py
+++ b/solution.py
@@ -433,8 +433,8 @@
         cotangents = [cotangent, *cotangents]
     forward = [(i, (i + 1) % tiles) for i in range(tiles)]
     backward = [(b, a) for a, b in forward]
+    after = lax.ppermute(top, "tile", backward)
     before = lax.ppermute(bottom, "tile", forward)
-    after = lax.ppermute(top, "tile", backward)
     fetched = len(cotangents)
     partial = call(
         functools.partial(inner_kernel, fetched=fetched),

time: 112 us -> 112 us (level)
  no operation moved by 1% of the time
where the time goes in v7:
time: 112 us
  starting transfers between devices  51.3 us (46%)
  waiting for transfers between devices  33.7 us (30%)
  Pallas kernels  24.3 us (22%)
  local copies, waits for them, and re-layouts  1.69 us (2%)
    ppermute x25, starting transfers between devices, flipped(): lax.ppermute(value, 'tile', [(i, i ^ k) for i in range(PLANE * PLANE)])  37.2 us
    all_to_all x1, waiting for transfers between devices, on_device(): lax.all_to_all(packed, 'tile', split_axis=0, concat_axis=0, tiled=True)  20.7 us
    ppermute x25, waiting for transfers between devices, flipped(): lax.ppermute(value, 'tile', [(i, i ^ k) for i in range(PLANE * PLANE)])  12.3 us
    pallas_call x1, Pallas kernels, on_device(): call(functools.partial(cross_kernel, cap=cap, inputs=len(operands)), (str...  10.5 us
    all_to_all x1, starting transfers between devices, on_device(): lax.all_to_all(packed, 'tile', split_axis=0, concat_axis=0, tiled=True)  8.37 us
    ppermute x1, starting transfers between devices, on_device(): after = lax.ppermute(top, 'tile', backward)  4.93 us
    pallas_call x1, Pallas kernels, on_device(): call(functools.partial(pack_kernel, tiles=tiles, cap=cap), shape((tiles,...  3.52 us
    pallas_call x1, Pallas kernels, on_device(): call(functools.partial(clip_kernel, order=order, unit=step // 2), shape((...  2.43 us
  transfers between devices with their start and end apart: 28, of which 12 were waited for; matrix products, arithmetic and copies ran while one was open for 0% of the time, Pallas kernels for 13%

profile of v7, /device:TPU:0, one launch (start us, length us, event | category | flops | bytes accessed | tf_op | source)
XLA Modules:
  0.0 112.2 jit_solution(3106017750216261092)
XLA Ops:
  0.7 3.5 %shard_map.149 = bf16[16,264,128]{2,1,0:T(8,128)(2,1)} custom-call(s32[1,1024]{1,0:T(1,128)} %bitcast.28, s32[1,1024]{1,0:T(1,128)} %bitcast.29, s32[1,1024]{1,0:T(1,128)} %bitcast.30, bf16[32,256]{1,0:T(8,128)(2,1)} %refs_3_.2, bf16[1024,256]{1,0:T(8,128)(2,1)} %refs_4_.2), custom_call_target="tpu_custom_call" | custom-call | flops 1073741824 | bytes 1572864 | tf_op jit(solution)/shard_map/pallas_call | solution.py:371
  4.2 8.4 %all-to-all-start = ((bf16[16,264,128]{2,1,0:T(8,128)(2,1)}), bf16[16,264,128]{2,1,0:T(8,128)(2,1)}, u32[]{:S(2)}, u32[]{:S(2)}) async-start(bf16[16,264,128]{2,1,0:T(8,128)(2,1)} %shard_map.149), calls=%async_computation | async-start | bytes 2162688 | tf_op jit(solution)/shard_map/all_to_all | solution.py:398
  12.6 1.9 %collective-permute-start.1 = (bf16[256,512]{1,0:T(8,128)(2,1)}, bf16[256,512]{1,0:T(8,128)(2,1)}, u32[]{:S(2)}, u32[]{:S(2)}) collective-permute-start(bf16[256,512]{1,0:T(8,128)(2,1)} %refs_0_.1), channel_id=1, source_target_pairs={{0,4},{2,6},{4,0},{6,2},{8,12},{10,14},{12,8},{14,10},{16,20},{18,... | collective-permute-start | bytes 786440 | tf_op jit(solution)/shard_map/ppermute | solution.py:318
  14.4 1.5 %collective-permute-start = (bf16[256,512]{1,0:T(8,128)(2,1)}, bf16[256,512]{1,0:T(8,128)(2,1)}, u32[]{:S(2)}, u32[]{:S(2)}) collective-permute-start(bf16[256,512]{1,0:T(8,128)(2,1)} %refs_0_.1), channel_id=1, source_target_pairs={{0,2},{2,0},{4,6},{6,4},{8,10},{10,8},{12,14},{14,12},{16,18},{18,... | collective-permute-start | bytes 786440 | tf_op jit(solution)/shard_map/ppermute | solution.py:318
  17.2 20.7 %all-to-all-done.refs_0_ = bf16[16,264,128]{2,1,0:T(8,128)(2,1)} async-done(((bf16[16,264,128]{2,1,0:T(8,128)(2,1)}), bf16[16,264,128]{2,1,0:T(8,128)(2,1)}, u32[]{:S(2)}, u32[]{:S(2)}) %all-to-all-start) | async-done | bytes 1081376 | tf_op jit(solution)/shard_map/all_to_all | solution.py:398
  37.9 10.5 %shard_map.151 = (f32[256,512]{1,0:T(8,128)}, bf16[256,512]{1,0:T(8,128)(2,1)}, bf16[128,512]{1,0:T(8,128)(2,1)}, bf16[128,512]{1,0:T(8,128)(2,1)}) custom-call(bf16[16,264,128]{2,1,0:T(8,128)(2,1)} %all-to-all-done.refs_0_, bf16[256,1024]{1,0:T(8,128)(2,1)} %refs_1_.1, bf16[256,512]{1,0:T(8,128)(2,1)} %copy-done.7, bf16[256,512]{1,0:T(8,128)(2,1)} %refs_3_.3, ...), custom_call_target="tpu_custom_call" | custom-call | flops 2147483648 | bytes 2621440 | tf_op jit(solution)/shard_map/pallas_call | solution.py:411
  49.2 4.9 %collective-permute-start.4 = (bf16[128,512]{1,0:T(8,128)(2,1)}, bf16[128,512]{1,0:T(8,128)(2,1)S(1)}, u32[]{:S(2)}, u32[]{:S(2)}) collective-permute-start(bf16[128,512]{1,0:T(8,128)(2,1)} %get-tuple-element.39), channel_id=1, source_target_pairs={{2,0},{4,2},{6,4},{8,6},{10,8},{12,10},{14,12},{16,14},{18,16},{20... | collective-permute-start | bytes 393224 | tf_op jit(solution)/shard_map/ppermute | solution.py:436
  55.1 1.5 %shard_map.152 = (bf16[256,512]{1,0:T(8,128)(2,1)S(1)}, f32[256,512]{1,0:T(8,128)S(1)}, f32[256,512]{1,0:T(8,128)S(1)}, f32[256,512]{1,0:T(8,128)S(1)}, bf16[256...) custom-call(bf16[512,1536]{1,0:T(8,128)(2,1)S(1)} %copy-done.1, ...), custom_call_target="tpu_custom_call" | custom-call | flops 536870912 | bytes 3670016 | tf_op jit(solution)/shard_map/pallas_call | solution.py:439
  57.4 2.3 %shard_map.153 = (f32[256,512]{1,0:T(8,128)S(1)}, bf16[256,512]{1,0:T(8,128)(2,1)S(1)}) custom-call(f32[256,512]{1,0:T(8,128)S(1)} %copy-done.4, bf16[128,512]{1,0:T(8,128)(2,1)S(1)} %collective-permute-done.3.before, bf16[128,512]{1,0:T(8,128)(2,1)S(1)} %collective-permute-done.4.after, bf16[512,1536]{1,0:T(8,128)(2,1)S(1)} %copy-done.1, ...), custom_call_target="tpu_custom_call" | custom-call | flops 469762048 | bytes 5242880 | tf_op jit(solution)/shard_map/pallas_call | solution.py:455
  60.9 3.5 %collective-permute-start.6 = (bf16[256,256]{1,0:T(8,128)(2,1)S(1)}, bf16[256,256]{1,0:T(8,128)(2,1)S(1)}, u32[]{:S(2)}, u32[]{:S(2)}) collective-permute-start(bf16[256,256]{1,0:T(8,128)(2,1)S(1)} %get-tuple-element.52.refs_2_), channel_id=1, source_target_pairs={{0,4},{2,6},{4,0},{6,2},{8,12},{10,14},{12,8},{14,10},{16,20},{18,... | collective-permute-start | bytes 393224 | tf_op jit(solution)/shard_map/ppermute | solution.py:318
  65.6 2.7 %collective-permute-done.6.refs_2_ = bf16[256,256]{1,0:T(8,128)(2,1)S(1)} collective-permute-done((bf16[256,256]{1,0:T(8,128)(2,1)S(1)}, bf16[256,256]{1,0:T(8,128)(2,1)S(1)}, u32[]{:S(2)}, u32[]{:S(2)}) %collective-permute-start.6) | collective-permute-done | bytes 131104 | tf_op jit(solution)/shard_map/ppermute | solution.py:318
  68.3 1.9 %collective-permute-done.7.refs_3_ = bf16[256,256]{1,0:T(8,128)(2,1)S(1)} collective-permute-done((bf16[256,256]{1,0:T(8,128)(2,1)S(1)}, bf16[256,256]{1,0:T(8,128)(2,1)S(1)}, u32[]{:S(2)}, u32[]{:S(2)}) %collective-permute-start.7) | collective-permute-done | bytes 131104 | tf_op jit(solution)/shard_map/ppermute | solution.py:318
  73.6 2.6 %collective-permute-start.17 = (bf16[256,256]{1,0:T(8,128)(2,1)S(1)}, bf16[256,256]{1,0:T(8,128)(2,1)S(1)}, u32[]{:S(2)}, u32[]{:S(2)}) collective-permute-start(bf16[256,256]{1,0:T(8,128)(2,1)S(1)} %get-tuple-element.63.refs_7_), channel_id=1, source_target_pairs={{0,6},{2,4},{4,2},{6,0},{8,14},{10,12},{12,10},{14,8},{16,22},{18,... | collective-permute-start | bytes 393224 | tf_op jit(solution)/shard_map/ppermute | solution.py:318
  76.4 2.9 %collective-permute-start.9 = (bf16[128,512]{1,0:T(8,128)(2,1)S(1)}, bf16[128,512]{1,0:T(8,128)(2,1)S(1)}, u32[]{:S(2)}, u32[]{:S(2)}) collective-permute-start(bf16[128,512]{1,0:T(8,128)(2,1)S(1)} %add_convert_fusion.3), channel_id=1, source_target_pairs={{0,16},{2,18},{4,20},{6,22},{8,24},{10,26},{12,28},{14,30},{16,0},... | collective-permute-start | bytes 393224 | tf_op jit(solution)/shard_map/ppermute | solution.py:318
  80.0 2.4 %collective-permute-start.18 = (bf16[128,512]{1,0:T(8,128)(2,1)S(1)}, bf16[128,512]{1,0:T(8,128)(2,1)S(1)}, u32[]{:S(2)}, u32[]{:S(2)}) collective-permute-start(bf16[128,512]{1,0:T(8,128)(2,1)S(1)} %get-tuple-element.67), channel_id=1, source_target_pairs={{0,8},{2,10},{4,12},{6,14},{8,0},{10,2},{12,4},{14,6},{16,24},{18,... | collective-permute-start | bytes 393224 | tf_op jit(solution)/shard_map/ppermute | solution.py:318
  82.9 4.3 %collective-permute-start.12 = (bf16[128,512]{1,0:T(8,128)(2,1)S(1)}, bf16[128,512]{1,0:T(8,128)(2,1)S(1)}, u32[]{:S(2)}, u32[]{:S(2)}) collective-permute-start(bf16[128,512]{1,0:T(8,128)(2,1)S(1)} %add_convert_fusion.2), channel_id=1, source_target_pairs={{0,8},{2,10},{4,12},{6,14},{8,0},{10,2},{12,4},{14,6},{16,24},{18,... | collective-permute-start | bytes 393224 | tf_op jit(solution)/shard_map/ppermute | solution.py:318
  87.2 3.4 %collective-permute-start.19 = (bf16[128,512]{1,0:T(8,128)(2,1)S(1)}, bf16[128,512]{1,0:T(8,128)(2,1)S(1)}, u32[]{:S(2)}, u32[]{:S(2)}) collective-permute-start(bf16[128,512]{1,0:T(8,128)(2,1)S(1)} %add_convert_fusion.1), channel_id=1, source_target_pairs={{0,16},{2,18},{4,20},{6,22},{8,24},{10,26},{12,28},{14,30},{16,0},... | collective-permute-start | bytes 393224 | tf_op jit(solution)/shard_map/ppermute | solution.py:318
  92.1 1.6 %collective-permute-done.19 = bf16[128,512]{1,0:T(8,128)(2,1)S(1)} collective-permute-done((bf16[128,512]{1,0:T(8,128)(2,1)S(1)}, bf16[128,512]{1,0:T(8,128)(2,1)S(1)}, u32[]{:S(2)}, u32[]{:S(2)}) %collective-permute-start.19) | collective-permute-done | bytes 131104 | tf_op jit(solution)/shard_map/ppermute | solution.py:318
  93.6 2.1 %collective-permute-start.23 = (bf16[128,512]{1,0:T(8,128)(2,1)S(1)}, bf16[128,512]{1,0:T(8,128)(2,1)S(1)}, u32[]{:S(2)}, u32[]{:S(2)}) collective-permute-start(bf16[128,512]{1,0:T(8,128)(2,1)S(1)} %add_convert_fusion), channel_id=1, source_target_pairs={{0,8},{2,10},{4,12},{6,14},{8,0},{10,2},{12,4},{14,6},{16,24},{18,... | collective-permute-start | bytes 393224 | tf_op jit(solution)/shard_map/ppermute | solution.py:318
  95.8 1.9 %collective-permute-start.21 = (bf16[128,512]{1,0:T(8,128)(2,1)S(1)}, bf16[128,512]{1,0:T(8,128)(2,1)S(1)}, u32[]{:S(2)}, u32[]{:S(2)}) collective-permute-start(bf16[128,512]{1,0:T(8,128)(2,1)S(1)} %add_convert_fusion), channel_id=1, source_target_pairs={{0,4},{2,6},{4,0},{6,2},{8,12},{10,14},{12,8},{14,10},{16,20},{18,... | collective-permute-start | bytes 393224 | tf_op jit(solution)/shard_map/ppermute | solution.py:318
  97.6 1.6 %collective-permute-start.20 = (bf16[128,512]{1,0:T(8,128)(2,1)S(1)}, bf16[128,512]{1,0:T(8,128)(2,1)S(1)}, u32[]{:S(2)}, u32[]{:S(2)}) collective-permute-start(bf16[128,512]{1,0:T(8,128)(2,1)S(1)} %add_convert_fusion), channel_id=1, source_target_pairs={{0,2},{2,0},{4,6},{6,4},{8,10},{10,8},{12,14},{14,12},{16,18},{18,... | collective-permute-start | bytes 393224 | tf_op jit(solution)/shard_map/ppermute | solution.py:318
  100.6 2.1 %collective-permute-done.22 = bf16[128,512]{1,0:T(8,128)(2,1)S(1)} collective-permute-done((bf16[128,512]{1,0:T(8,128)(2,1)S(1)}, bf16[128,512]{1,0:T(8,128)(2,1)S(1)}, u32[]{:S(2)}, u32[]{:S(2)}) %collective-permute-start.22) | collective-permute-done | bytes 131104 | tf_op jit(solution)/shard_map/ppermute | solution.py:318
  104.2 2.0 %collective-permute-start.24 = (bf16[128,512]{1,0:T(8,128)(2,1)S(1)}, bf16[128,512]{1,0:T(8,128)(2,1)S(1)}, u32[]{:S(2)}, u32[]{:S(2)}) collective-permute-start(bf16[128,512]{1,0:T(8,128)(2,1)S(1)} %collective-permute-done.23), channel_id=1, source_target_pairs={{0,2},{2,0},{4,6},{6,4},{8,10},{10,8},{12,14},{14,12},{16,18},{18,... | collective-permute-start | bytes 393224 | tf_op jit(solution)/shard_map/ppermute | solution.py:318
  109.6 2.4 %shard_map.159 = f32[2048,512]{1,0:T(8,128)} custom-call(s32[1]{0:T(128)} %bitcast.me, bf16[2,128,512]{2,1,0:T(8,128)(2,1)S(1)} %pad_maximum_fusion.refs_0_, bf16[2,128,512]{2,1,0:T(8,128)(2,1)S(1)} %collective-permute-done.11.refs_1_, bf16[2,128,512]{2,1,0:T(8,128)(2,1)S(1)} %pad_maximum_fusion.1.refs_2_, ...), custom_call_target="tpu_custom_call" | custom-call | flops 4194304 | bytes 6291456 | tf_op jit(solution)/shard_map/pallas_call | solution.py:499
  (67 shorter events, 18.6 us)
Async XLA Ops:
  4.2 33.7 %all-to-all-start = ((bf16[16,264,128]{2,1,0:T(8,128)(2,1)}), bf16[16,264,128]{2,1,0:T(8,128)(2,1)}, u32[]{:S(2)}, u32[]{:S(2)}) async-start(bf16[16,264,128]{2,1,0:T(8,128)(2,1)} %shard_map.149), calls=%async_computation | async-start | bytes 2162688 | tf_op jit(solution)/shard_map/all_to_all | solution.py:398
  12.6 35.8 %collective-permute-start.1 = (bf16[256,512]{1,0:T(8,128)(2,1)}, bf16[256,512]{1,0:T(8,128)(2,1)}, u32[]{:S(2)}, u32[]{:S(2)}) collective-permute-start(bf16[256,512]{1,0:T(8,128)(2,1)} %refs_0_.1), channel_id=1, source_target_pairs={{0,4},{2,6},{4,0},{6,2},{8,12},{10,14},{12,8},{14,10},{16,20},{18,... | collective-permute-start | bytes 786440 | tf_op jit(solution)/shard_map/ppermute | solution.py:318
  14.4 34.0 %collective-permute-start = (bf16[256,512]{1,0:T(8,128)(2,1)}, bf16[256,512]{1,0:T(8,128)(2,1)}, u32[]{:S(2)}, u32[]{:S(2)}) collective-permute-start(bf16[256,512]{1,0:T(8,128)(2,1)} %refs_0_.1), channel_id=1, source_target_pairs={{0,2},{2,0},{4,6},{6,4},{8,10},{10,8},{12,14},{14,12},{16,18},{18,... | collective-permute-start | bytes 786440 | tf_op jit(solution)/shard_map/ppermute | solution.py:318
  15.9 32.5 %collective-permute-start.2 = (bf16[256,512]{1,0:T(8,128)(2,1)}, bf16[256,512]{1,0:T(8,128)(2,1)}, u32[]{:S(2)}, u32[]{:S(2)}) collective-permute-start(bf16[256,512]{1,0:T(8,128)(2,1)} %refs_0_.1), channel_id=1, source_target_pairs={{0,6},{2,4},{4,2},{6,0},{8,14},{10,12},{12,10},{14,8},{16,22},{18,... | collective-permute-start | bytes 786440 | tf_op jit(solution)/shard_map/ppermute | solution.py:318
  48.4 8.9 %collective-permute-start.3 = (bf16[128,512]{1,0:T(8,128)(2,1)}, bf16[128,512]{1,0:T(8,128)(2,1)S(1)}, u32[]{:S(2)}, u32[]{:S(2)}) collective-permute-start(bf16[128,512]{1,0:T(8,128)(2,1)} %get-tuple-element.38), channel_id=1, source_target_pairs={{0,2},{2,4},{4,6},{6,8},{8,10},{10,12},{12,14},{14,16},{16,18},{18... | collective-permute-start | bytes 393224 | tf_op jit(solution)/shard_map/ppermute | solution.py:437
  49.2 8.2 %collective-permute-start.4 = (bf16[128,512]{1,0:T(8,128)(2,1)}, bf16[128,512]{1,0:T(8,128)(2,1)S(1)}, u32[]{:S(2)}, u32[]{:S(2)}) collective-permute-start(bf16[128,512]{1,0:T(8,128)(2,1)} %get-tuple-element.39), channel_id=1, source_target_pairs={{2,0},{4,2},{6,4},{8,6},{10,8},{12,10},{14,12},{16,14},{18,16},{20... | collective-permute-start | bytes 393224 | tf_op jit(solution)/shard_map/ppermute | solution.py:436
  60.9 7.4 %collective-permute-start.6 = (bf16[256,256]{1,0:T(8,128)(2,1)S(1)}, bf16[256,256]{1,0:T(8,128)(2,1)S(1)}, u32[]{:S(2)}, u32[]{:S(2)}) collective-permute-start(bf16[256,256]{1,0:T(8,128)(2,1)S(1)} %get-tuple-element.52.refs_2_), channel_id=1, source_target_pairs={{0,4},{2,6},{4,0},{6,2},{8,12},{10,14},{12,8},{14,10},{16,20},{18,... | collective-permute-start | bytes 393224 | tf_op jit(solution)/shard_map/ppermute | solution.py:318
  64.4 5.9 %collective-permute-start.7 = (bf16[256,256]{1,0:T(8,128)(2,1)S(1)}, bf16[256,256]{1,0:T(8,128)(2,1)S(1)}, u32[]{:S(2)}, u32[]{:S(2)}) collective-permute-start(bf16[256,256]{1,0:T(8,128)(2,1)S(1)} %get-tuple-element.53.refs_3_), channel_id=1, source_target_pairs={{0,6},{2,4},{4,2},{6,0},{8,14},{10,12},{12,10},{14,8},{16,22},{18,... | collective-permute-start | bytes 393224 | tf_op jit(solution)/shard_map/ppermute | solution.py:318
  72.7 6.6 %collective-permute-start.15 = (bf16[256,256]{1,0:T(8,128)(2,1)S(1)}, bf16[256,256]{1,0:T(8,128)(2,1)S(1)}, u32[]{:S(2)}, u32[]{:S(2)}) collective-permute-start(bf16[256,256]{1,0:T(8,128)(2,1)S(1)} %get-tuple-element.61.refs_5_), channel_id=1, source_target_pairs={{0,2},{2,0},{4,6},{6,4},{8,10},{10,8},{12,14},{14,12},{16,18},{18,... | collective-permute-start | bytes 393224 | tf_op jit(solution)/shard_map/ppermute | solution.py:318
  72.8 6.4 %collective-permute-start.16 = (bf16[256,256]{1,0:T(8,128)(2,1)S(1)}, bf16[256,256]{1,0:T(8,128)(2,1)S(1)}, u32[]{:S(2)}, u32[]{:S(2)}) collective-permute-start(bf16[256,256]{1,0:T(8,128)(2,1)S(1)} %get-tuple-element.62.refs_6_), channel_id=1, source_target_pairs={{0,4},{2,6},{4,0},{6,2},{8,12},{10,14},{12,8},{14,10},{16,20},{18,... | collective-permute-start | bytes 393224 | tf_op jit(solution)/shard_map/ppermute | solution.py:318
  76.4 6.5 %collective-permute-start.9 = (bf16[128,512]{1,0:T(8,128)(2,1)S(1)}, bf16[128,512]{1,0:T(8,128)(2,1)S(1)}, u32[]{:S(2)}, u32[]{:S(2)}) collective-permute-start(bf16[128,512]{1,0:T(8,128)(2,1)S(1)} %add_convert_fusion.3), channel_id=1, source_target_pairs={{0,16},{2,18},{4,20},{6,22},{8,24},{10,26},{12,28},{14,30},{16,0},... | collective-permute-start | bytes 393224 | tf_op jit(solution)/shard_map/ppermute | solution.py:318
  80.0 7.2 %collective-permute-start.18 = (bf16[128,512]{1,0:T(8,128)(2,1)S(1)}, bf16[128,512]{1,0:T(8,128)(2,1)S(1)}, u32[]{:S(2)}, u32[]{:S(2)}) collective-permute-start(bf16[128,512]{1,0:T(8,128)(2,1)S(1)} %get-tuple-element.67), channel_id=1, source_target_pairs={{0,8},{2,10},{4,12},{6,14},{8,0},{10,2},{12,4},{14,6},{16,24},{18,... | collective-permute-start | bytes 393224 | tf_op jit(solution)/shard_map/ppermute | solution.py:318
  82.9 8.1 %collective-permute-start.12 = (bf16[128,512]{1,0:T(8,128)(2,1)S(1)}, bf16[128,512]{1,0:T(8,128)(2,1)S(1)}, u32[]{:S(2)}, u32[]{:S(2)}) collective-permute-start(bf16[128,512]{1,0:T(8,128)(2,1)S(1)} %add_convert_fusion.2), channel_id=1, source_target_pairs={{0,8},{2,10},{4,12},{6,14},{8,0},{10,2},{12,4},{14,6},{16,24},{18,... | collective-permute-start | bytes 393224 | tf_op jit(solution)/shard_map/ppermute | solution.py:318
  87.2 6.4 %collective-permute-start.19 = (bf16[128,512]{1,0:T(8,128)(2,1)S(1)}, bf16[128,512]{1,0:T(8,128)(2,1)S(1)}, u32[]{:S(2)}, u32[]{:S(2)}) collective-permute-start(bf16[128,512]{1,0:T(8,128)(2,1)S(1)} %add_convert_fusion.1), channel_id=1, source_target_pairs={{0,16},{2,18},{4,20},{6,22},{8,24},{10,26},{12,28},{14,30},{16,0},... | collective-permute-start | bytes 393224 | tf_op jit(solution)/shard_map/ppermute | solution.py:318
  90.7 7.0 %collective-permute-start.10 = (bf16[128,512]{1,0:T(8,128)(2,1)S(1)}, bf16[128,512]{1,0:T(8,128)(2,1)S(1)}, u32[]{:S(2)}, u32[]{:S(2)}) collective-permute-start(bf16[128,512]{1,0:T(8,128)(2,1)S(1)} %add_convert_fusion.2), channel_id=1, source_target_pairs={{0,2},{2,0},{4,6},{6,4},{8,10},{10,8},{12,14},{14,12},{16,18},{18,... | collective-permute-start | bytes 393224 | tf_op jit(solution)/shard_map/ppermute | solution.py:318
  91.0 8.3 %collective-permute-start.13 = (bf16[128,512]{1,0:T(8,128)(2,1)S(1)}, bf16[128,512]{1,0:T(8,128)(2,1)S(1)}, u32[]{:S(2)}, u32[]{:S(2)}) collective-permute-start(bf16[128,512]{1,0:T(8,128)(2,1)S(1)} %collective-permute-done.12), channel_id=1, source_target_pairs={{0,4},{2,6},{4,0},{6,2},{8,12},{10,14},{12,8},{14,10},{16,20},{18,... | collective-permute-start | bytes 393224 | tf_op jit(solution)/shard_map/ppermute | solution.py:318
  93.6 6.1 %collective-permute-start.23 = (bf16[128,512]{1,0:T(8,128)(2,1)S(1)}, bf16[128,512]{1,0:T(8,128)(2,1)S(1)}, u32[]{:S(2)}, u32[]{:S(2)}) collective-permute-start(bf16[128,512]{1,0:T(8,128)(2,1)S(1)} %add_convert_fusion), channel_id=1, source_target_pairs={{0,8},{2,10},{4,12},{6,14},{8,0},{10,2},{12,4},{14,6},{16,24},{18,... | collective-permute-start | bytes 393224 | tf_op jit(solution)/shard_map/ppermute | solution.py:318
  95.8 6.9 %collective-permute-start.22 = (bf16[128,512]{1,0:T(8,128)(2,1)S(1)}, bf16[128,512]{1,0:T(8,128)(2,1)S(1)}, u32[]{:S(2)}, u32[]{:S(2)}) collective-permute-start(bf16[128,512]{1,0:T(8,128)(2,1)S(1)} %add_convert_fusion), channel_id=1, source_target_pairs={{0,6},{2,4},{4,2},{6,0},{8,14},{10,12},{12,10},{14,8},{16,22},{18,... | collective-permute-start | bytes 393224 | tf_op jit(solution)/shard_map/ppermute | solution.py:318
  95.8 7.4 %collective-permute-start.21 = (bf16[128,512]{1,0:T(8,128)(2,1)S(1)}, bf16[128,512]{1,0:T(8,128)(2,1)S(1)}, u32[]{:S(2)}, u32[]{:S(2)}) collective-permute-start(bf16[128,512]{1,0:T(8,128)(2,1)S(1)} %add_convert_fusion), channel_id=1, source_target_pairs={{0,4},{2,6},{4,0},{6,2},{8,12},{10,14},{12,8},{14,10},{16,20},{18,... | collective-permute-start | bytes 393224 | tf_op jit(solution)/shard_map/ppermute | solution.py:318
  97.6 6.5 %collective-permute-start.20 = (bf16[128,512]{1,0:T(8,128)(2,1)S(1)}, bf16[128,512]{1,0:T(8,128)(2,1)S(1)}, u32[]{:S(2)}, u32[]{:S(2)}) collective-permute-start(bf16[128,512]{1,0:T(8,128)(2,1)S(1)} %add_convert_fusion), channel_id=1, source_target_pairs={{0,2},{2,0},{4,6},{6,4},{8,10},{10,8},{12,14},{14,12},{16,18},{18,... | collective-permute-start | bytes 393224 | tf_op jit(solution)/shard_map/ppermute | solution.py:318
  99.3 10.2 %collective-permute-start.11 = (bf16[2,128,512]{2,1,0:T(8,128)(2,1)S(1)}, bf16[2,128,512]{2,1,0:T(8,128)(2,1)S(1)}, u32[]{:S(2)}, u32[]{:S(2)}) collective-permute-start(bf16[2,128,512]{2,1,0:T(8,128)(2,1)S(1)} %pad_maximum_fusion.refs_0_), channel_id=1, source_target_pairs={{0,4},{2,6},{4,0},{6,2},{8,12},{10,14},{12,8},{14,10},{16,20},{18,... | collective-permute-start | bytes 786440 | tf_op jit(solution)/shard_map/ppermute | solution.py:318
  99.8 9.8 %collective-permute-start.14 = (bf16[2,128,512]{2,1,0:T(8,128)(2,1)S(1)}, bf16[2,128,512]{2,1,0:T(8,128)(2,1)S(1)}, u32[]{:S(2)}, u32[]{:S(2)}) collective-permute-start(bf16[2,128,512]{2,1,0:T(8,128)(2,1)S(1)} %pad_maximum_fusion.1.refs_2_), channel_id=1, source_target_pairs={{0,2},{2,0},{4,6},{6,4},{8,10},{10,8},{12,14},{14,12},{16,18},{18,... | collective-permute-start | bytes 786440 | tf_op jit(solution)/shard_map/ppermute | solution.py:318
  102.7 6.1 %collective-permute-start.26 = (bf16[128,512]{1,0:T(8,128)(2,1)S(1)}, bf16[128,512]{1,0:T(8,128)(2,1)S(1)}, u32[]{:S(2)}, u32[]{:S(2)}) collective-permute-start(bf16[128,512]{1,0:T(8,128)(2,1)S(1)} %collective-permute-done.23), channel_id=1, source_target_pairs={{0,6},{2,4},{4,2},{6,0},{8,14},{10,12},{12,10},{14,8},{16,22},{18,... | collective-permute-start | bytes 393224 | tf_op jit(solution)/shard_map/ppermute | solution.py:318
  103.2 6.4 %collective-permute-start.25 = (bf16[128,512]{1,0:T(8,128)(2,1)S(1)}, bf16[128,512]{1,0:T(8,128)(2,1)S(1)}, u32[]{:S(2)}, u32[]{:S(2)}) collective-permute-start(bf16[128,512]{1,0:T(8,128)(2,1)S(1)} %collective-permute-done.23), channel_id=1, source_target_pairs={{0,4},{2,6},{4,0},{6,2},{8,12},{10,14},{12,8},{14,10},{16,20},{18,... | collective-permute-start | bytes 393224 | tf_op jit(solution)/shard_map/ppermute | solution.py:318
  (13 other events, 141.8 us)
